TPU v7x, 32 devices: a whole 2x2x4 slice. The times are simulated.
32 devices in a mesh: pipe: 4 (over y, x), ctx: 8 (over z, core).
Axes of the slice: x: 2, y: 2, z: 4, core: 2. Of those that a mesh axis runs over, the one named last changes fastest.
Arguments:
- queries: bfloat16 [4, 1024, 3072], P('pipe', 'ctx'), may hold values from -40 to 40
- keys: bfloat16 [4, 1024, 3072], P('pipe', 'ctx'), may hold values from -6 to 6
- values: bfloat16 [4, 1024, 3072], P('pipe', 'ctx'), may hold values from -6 to 6
- residual: bfloat16 [4, 1024, 3072], P('pipe', 'ctx'), may hold values from -6 to 6
- gate: float32 [4, 3072], P('pipe'), may hold values from 0.5 to 2
- tile_lists: int32 [4, 8, 24, 5], P('pipe', 'ctx'), may hold values from 0 to 7, as said below
- counts: int32 [4, 8, 24], P('pipe', 'ctx'), may hold values from 1 to 5
Outputs:
- passed: bfloat16 [4, 1024, 3072], P('pipe', 'ctx')
Inputs may be any that keep to these rules, and one draw needn't show every extreme that they name: `tile_lists`: each list names 5 distinct tiles, none equal to its query tile; entries past the count are tiles too. Over the 24 lists of one query tile no tile is named more than 18 times, and some tile is named exactly 18 times.
All inputs are finite; a program needn't handle non-finite values.
Results may differ from a plain program's by a relative error of at most 0.0022.
Values may be sent and summed in bfloat16 or wider, within the bound.
No kernel may reach another device: no remote copies, remote signals or barrier semaphores. Data moves between devices by JAX's collectives and lax.ppermute only.
A program may use at most 128 MiB of HBM per device.

v0:
```python
import math

import jax
import jax.numpy as jnp
from jax import lax
from jax.sharding import PartitionSpec as P

HEADS = 24
HEAD_DIM = 128
K_LIST = 5


def padded(array, sides, width):
    for axis, dim in sides:
        size, length = (lax.axis_size(axis), array.shape[dim])
        up = [(i, (i + 1) % size) for i in range(size - 1)]
        down = [(j, i) for i, j in up]
        last = lax.slice_in_dim(array, length - width, length, axis=dim)
        leading = lax.slice_in_dim(array, 0, width, axis=dim)
        before = lax.ppermute(last, axis, up)
        after = lax.ppermute(leading, axis, down)
        array = jnp.concatenate([before, array, after], axis=dim)
    return array


def shifted(block, axis, distance):
    devices = range(lax.axis_size(axis))
    route = [((i - distance) % len(devices), i) for i in devices]
    return lax.ppermute(block, axis, route)


def entry_ranks(flat):
    width = flat.shape[-1]
    same = flat[..., :, None] == flat[..., None, :]
    earlier = jnp.arange(width)[None, :] < jnp.arange(width)[:, None]
    return jnp.sum(same & earlier, axis=-1)


def near_scores(query_heads, near_rows):
    scale = 1.0 / math.sqrt(HEAD_DIM)
    return (
        jnp.einsum(
            "hqd,hjd->hqj",
            query_heads,
            near_rows[..., :HEAD_DIM],
            preferred_element_type=jnp.float32,
        )
        * scale
    )


def attend_group(query_heads, near_rows, far_rows, valid, local, near_ok, rows):
    scale = 1.0 / math.sqrt(HEAD_DIM)
    group_size = query_heads.shape[0]
    far_keys = far_rows[..., :HEAD_DIM].reshape(group_size, K_LIST * rows, HEAD_DIM)
    far_vals = far_rows[..., HEAD_DIM:].reshape(group_size, K_LIST * rows, HEAD_DIM)
    remote = (
        jnp.einsum("hqd,hjd->hqj", query_heads, far_keys, preferred_element_type=jnp.float32)
        * scale
    )
    local_ok = near_ok[None, None, :]
    far_ok = ((jnp.arange(K_LIST * rows) // rows)[None, :] < valid[:, None])[:, None, :]
    top = jnp.maximum(
        jnp.max(jnp.where(local_ok, local, -1e30), axis=-1, keepdims=True),
        jnp.max(jnp.where(far_ok, remote, -1e30), axis=-1, keepdims=True),
    )
    p_local = jnp.where(local_ok, jnp.exp(local - top), 0.0)
    p_far = jnp.where(far_ok, jnp.exp(remote - top), 0.0)
    total = jnp.sum(p_local, axis=-1, keepdims=True) + jnp.sum(p_far, axis=-1, keepdims=True)
    mixed = jnp.einsum(
        "hqj,hjd->hqd",
        p_local.astype(jnp.bfloat16),
        near_rows[..., HEAD_DIM:],
        preferred_element_type=jnp.float32,
    )
    mixed = mixed + jnp.einsum(
        "hqj,hjd->hqd", p_far.astype(jnp.bfloat16), far_vals, preferred_element_type=jnp.float32
    )
    return mixed / total


def shards(queries, keys, values, residual, gate, tile_lists, counts):
    rows = queries.shape[1]
    tiles = lax.axis_size("ctx")
    me = lax.axis_index("ctx")
    cap = (HEADS * K_LIST + tiles - 2) // (tiles - 1)
    query_heads = queries[0].reshape(rows, HEADS, HEAD_DIM).transpose(1, 0, 2)
    kv_heads = jnp.concatenate(
        (keys[0].reshape(rows, HEADS, HEAD_DIM), values[0].reshape(rows, HEADS, HEAD_DIM)), axis=2
    ).transpose(1, 0, 2)
    lists = tile_lists[0, 0]
    valid = counts[0, 0]
    near_rows = padded(kv_heads, (("ctx", 1),), rows)
    near_ok = jnp.concatenate(
        (jnp.full((rows,), me > 0), jnp.full((rows,), True), jnp.full((rows,), me < tiles - 1))
    )
    head_of = jnp.arange(HEADS * K_LIST) // K_LIST
    all_lists = lax.all_gather(lists[None], "ctx", axis=0, tiled=True)
    flat = all_lists.reshape(tiles, HEADS * K_LIST)
    used = jnp.ones(flat.shape, bool)
    ranks = entry_ranks(flat)
    slot_hit = ((flat == me) & used)[:, :, None] & (
        ranks[:, :, None] == jnp.arange(cap)[None, None, :]
    )
    head_idx = jnp.sum(jnp.where(slot_hit, head_of[None, :, None], 0), axis=1)
    filled = jnp.any(slot_hit, axis=1)
    outgoing = jnp.where(
        filled[:, :, None, None], jnp.take(kv_heads, head_idx, axis=0), jnp.zeros((), jnp.bfloat16)
    )
    arrived = lax.all_to_all(outgoing, "ctx", split_axis=0, concat_axis=0, tiled=True)
    my_rank = lax.dynamic_index_in_dim(ranks, me, 0, keepdims=False)
    pick = (lists.reshape(HEADS * K_LIST) * cap + my_rank).reshape(HEADS, K_LIST)
    far_rows = jnp.take(arrived.reshape(tiles * cap, rows, 2 * HEAD_DIM), pick, axis=0)
    group_size = 1
    for candidate in (6, 4, 3, 2):
        if HEADS % candidate == 0 and group_size == 1:
            group_size = candidate
    groups = HEADS // group_size
    grouped_q = query_heads.reshape(groups, group_size, rows, HEAD_DIM)
    grouped_near = near_rows.reshape(groups, group_size, 3 * rows, 2 * HEAD_DIM)
    grouped_far = far_rows.reshape(groups, group_size, K_LIST, rows, 2 * HEAD_DIM)
    grouped_valid = valid.reshape(groups, group_size)

    def run_group(inputs):
        one_q, one_near, one_far, one_valid = inputs
        local = near_scores(one_q, one_near)
        return attend_group(one_q, one_near, one_far, one_valid, local, near_ok, rows)

    heads_out = lax.map(run_group, (grouped_q, grouped_near, grouped_far, grouped_valid))
    attention = (
        heads_out.reshape(HEADS, rows, HEAD_DIM).transpose(1, 0, 2).reshape(rows, HEADS * HEAD_DIM)
    )
    updated = (residual[0].astype(jnp.float32) + gate[0][None, :] * attention).astype(jnp.bfloat16)
    return shifted(updated[None], "pipe", 1)


def solution(mesh):
    placed = (
        P("pipe", "ctx", None),
        P("pipe", "ctx", None),
        P("pipe", "ctx", None),
        P("pipe", "ctx", None),
        P("pipe", None),
        P("pipe", "ctx", None, None),
        P("pipe", "ctx", None),
    )
    return jax.shard_map(
        shards, mesh=mesh, in_specs=placed, out_specs=P("pipe", "ctx", None), check_vma=False
    )
```

profile of v0, /device:TPU:9, one launch (start us, length us, event | category | flops | bytes accessed | tf_op | source)
XLA Modules:
  0.0 327.6 jit_solution(9456275514849436942)
XLA Ops:
  0.0 14.9 %all-gather = s32[8,1,24,5]{2,1,3,0:T(1,128)S(1)} all-gather(s32[1,1,24,5]{2,1,3,0:T(1,128)} %param.14), channel_id=2, replica_groups=mesh['pipe'=4,'ctx'=8] {'ctx'}, dimensions={0}, use_global_device_ids=true | all-gather | bytes 4320 | tf_op jit(solution)/shard_map/all_gather | solution.py:98
  16.5 1.3 copy.58
  18.7 7.3 %gather_fusion = bf16[144,128,256]{2,1,0:T(8,128)(2,1)} fusion(bf16[24,128,256]{2,1,0:T(8,128)(2,1)S(1)} %maximum_bitcast_fusion, s32[1024]{0:T(1024)S(1)} %pad_clamp_fusion.1), kind=kCustom, calls=%fused_computation | custom fusion | bytes 18874944 | tf_op jit(solution)/shard_map/jit(_take)/gather | solution.py:108
  26.0 8.5 %select_select_fusion = bf16[8,18,128,256]{3,2,1,0:T(8,128)(2,1)} fusion(bf16[8,18,128,256]{3,2,1,0:T(8,128)(2,1)} %bitcast.85, pred[8,18]{1,0:T(8,128)(4,1)S(1)} %copy.52, pred[8,18]{1,0:T(8,128)(4,1)S(1)} %copy.51), kind=kLoop, calls=%fused_computation.47 | loop fusion | flops 9437184 | bytes 18874656 | tf_op jit(solution)/shard_map/jit(_where)/select_n | solution.py:107
  34.5 5.3 %all-to-all-start = ((bf16[8,18,128,256]{3,2,1,0:T(8,128)(2,1)}), bf16[8,18,128,256]{3,2,1,0:T(8,128)(2,1)}, u32[]{:S(2)}, u32[]{:S(2)}) async-start(bf16[8,18,128,256]{3,2,1,0:T(8,128)(2,1)} %select_select_fusion), calls=%async_computation | async-start | bytes 18874368 | tf_op jit(solution)/shard_map/all_to_all | solution.py:110
  39.8 3.3 %collective-permute-start = (bf16[24,128,256]{2,1,0:T(8,128)(2,1)S(1)}, bf16[24,128,256]{2,1,0:T(8,128)(2,1)}, u32[]{:S(2)}, u32[]{:S(2)}) collective-permute-start(bf16[24,128,256]{2,1,0:T(8,128)(2,1)S(1)} %maximum_bitcast_fusion), channel_id=1, source_target_pairs={{0,1},{1,2},{2,3},{3,4},{4,5},{5,6},{6,7},{8,9},{9,10},{10,11},{11... | collective-permute-start | bytes 4718600 | tf_op jit(solution)/shard_map/ppermute | solution.py:20
  43.1 2.1 collective-permute-start.1
  46.1 0.5 broadcast.224
  46.6 0.6 reduce.11
  47.8 211.6 %collective-permute-done = bf16[24,128,256]{2,1,0:T(8,128)(2,1)} collective-permute-done((bf16[24,128,256]{2,1,0:T(8,128)(2,1)S(1)}, bf16[24,128,256]{2,1,0:T(8,128)(2,1)}, u32[]{:S(2)}, u32[]{:S(2)}) %collective-permute-start) | collective-permute-done | bytes 1572896 | tf_op jit(solution)/shard_map/ppermute | solution.py:20
  259.4 1.9 collective-permute-done.1
  261.3 3.7 %pad_maximum_fusion = bf16[24,384,256]{2,1,0:T(8,128)(2,1)} fusion(bf16[24,128,256]{2,1,0:T(8,128)(2,1)} %collective-permute-done.1, bf16[24,128,256]{2,1,0:T(8,128)(2,1)S(1)} %maximum_bitcast_fusion, bf16[24,128,256]{2,1,0:T(8,128)(2,1)} %collective-permute-done), kind=kLoop, calls=%fused_computation.49 | loop fusion | flops 14155776 | bytes 9437184 | tf_op jit(solution)/shard_map/concatenate | solution.py:22
  265.0 10.1 %gather_fusion.1 = bf16[120,128,256]{2,1,0:T(8,128)(2,1)} fusion(bf16[144,128,256]{2,1,0:T(8,128)(2,1)} %bitcast.14, s32[1024]{0:T(1024)S(1)} %pad_clamp_fusion), kind=kCustom, calls=%fused_computation.1 | custom fusion | bytes 15729120 | tf_op jit(solution)/shard_map/jit(_take)/gather | solution.py:113
  275.1 7.2 %broadcast_select_fusion = bf16[4,6,5,128,256]{4,3,2,1,0:T(8,128)(2,1)} fusion(bf16[4,6,5,128,256]{4,3,2,1,0:T(8,128)(2,1)} %bitcast.86, pred[4,6,5]{2,1,0:T(8,128)(4,1)S(1)} %copy.50), kind=kLoop, calls=%fused_computation.48 | loop fusion | flops 3932160 | bytes 15728760 | tf_op jit(solution)/shard_map/jit(_take)/select_n | solution.py:113
  282.3 27.1 %while.12 = (s32[]{:T(128)}, f32[4,6,128,128]{3,2,1,0:T(8,128)S(1)}, pred[384]{0:T(512)(128)(4,1)S(1)}, bf16[4,6,128,128]{3,2,1,0:T(8,128)(2,1)S(1)}, bf16[4,6,3...) while((s32[]{:T(128)}, ...), condition=%wide.region_8.9_spmd, body=%wide.region_3.0_spmd.sunk | while | flops 410918144 | bytes 24453172 | solution.py:129
  282.4 1.7 dynamic-slice_bitcast_fusion.5
  284.1 0.5 fusion.57
  284.6 0.6 select_reduce_fusion.6
  285.2 1.4 dynamic-slice_bitcast_fusion.4
  286.6 0.5 select_reduce_fusion.5
  287.0 0.6 fusion.60
  288.4 0.7 fusion.61
  289.2 1.7 dynamic-slice_bitcast_fusion.5
  290.9 0.5 fusion.57
  291.4 0.6 select_reduce_fusion.6
  292.0 1.4 dynamic-slice_bitcast_fusion.4
  293.8 0.6 fusion.60
  295.2 0.7 fusion.61
  296.0 1.7 dynamic-slice_bitcast_fusion.5
  297.6 0.5 fusion.57
  298.2 0.6 select_reduce_fusion.6
  298.8 1.4 dynamic-slice_bitcast_fusion.4
  300.1 0.5 select_reduce_fusion.5
  300.6 0.6 fusion.60
  302.0 0.7 fusion.61
  302.7 1.7 dynamic-slice_bitcast_fusion.5
  304.4 0.5 fusion.57
  305.0 0.6 select_reduce_fusion.6
  305.6 1.4 dynamic-slice_bitcast_fusion.4
  306.9 0.5 select_reduce_fusion.5
  307.4 0.6 fusion.60
  308.7 0.7 fusion.61
  309.4 1.1 copy-done.1
  310.6 2.3 copy.61
  313.6 1.3 add_convert_fusion
  314.9 1.3 collective-permute-start.2
  316.2 10.5 %collective-permute-done.2 = bf16[1,128,3072]{2,1,0:T(8,128)(2,1)S(1)} collective-permute-done((bf16[1,128,3072]{2,1,0:T(8,128)(2,1)S(1)}, bf16[1,128,3072]{2,1,0:T(8,128)(2,1)S(1)}, u32[]{:S(2)}, u32[]{:S(2)}) %collective-permute-start.2) | collective-permute-done | bytes 786464 | tf_op jit(solution)/shard_map/ppermute | solution.py:29
  326.7 0.9 copy.72
  (84 shorter events, 8.4 us)
Async XLA Ops:
  0.0 18.0 %copy-start.2 = (bf16[1,128,3072]{2,1,0:T(8,128)(2,1)S(1)}, bf16[1,128,3072]{2,1,0:T(8,128)(2,1)}, u32[]{:S(2)}) copy-start(bf16[1,128,3072]{2,1,0:T(8,128)(2,1)} %param.11) | copy-start | bytes 2359300
  34.5 10.9 %copy-start.4 = (s32[1,1,24,5]{2,1,3,0:T(1,128)S(1)}, s32[1,1,24,5]{2,1,3,0:T(1,128)}, u32[]{:S(2)}) copy-start(s32[1,1,24,5]{2,1,3,0:T(1,128)} %param.14) | copy-start | bytes 1444
  34.5 12.2 %copy-start.6 = (s32[1,1,24]{2,1,0:T(1,128)S(1)}, s32[1,1,24]{2,1,0:T(1,128)}, u32[]{:S(2)}) copy-start(s32[1,1,24]{2,1,0:T(1,128)} %param.15) | copy-start | bytes 292
  34.5 12.9 %copy-start.3 = (bf16[1,128,3072]{2,1,0:T(8,128)(2,1)S(1)}, bf16[1,128,3072]{2,1,0:T(8,128)(2,1)}, u32[]{:S(2)}) copy-start(bf16[1,128,3072]{2,1,0:T(8,128)(2,1)} %param.9) | copy-start | bytes 2359300
  34.5 230.5 %all-to-all-start = ((bf16[8,18,128,256]{3,2,1,0:T(8,128)(2,1)}), bf16[8,18,128,256]{3,2,1,0:T(8,128)(2,1)}, u32[]{:S(2)}, u32[]{:S(2)}) async-start(bf16[8,18,128,256]{3,2,1,0:T(8,128)(2,1)} %select_select_fusion), calls=%async_computation | async-start | bytes 18874368 | tf_op jit(solution)/shard_map/all_to_all | solution.py:110
  39.8 219.6 %collective-permute-start = (bf16[24,128,256]{2,1,0:T(8,128)(2,1)S(1)}, bf16[24,128,256]{2,1,0:T(8,128)(2,1)}, u32[]{:S(2)}, u32[]{:S(2)}) collective-permute-start(bf16[24,128,256]{2,1,0:T(8,128)(2,1)S(1)} %maximum_bitcast_fusion), channel_id=1, source_target_pairs={{0,1},{1,2},{2,3},{3,4},{4,5},{5,6},{6,7},{8,9},{9,10},{10,11},{11... | collective-permute-start | bytes 4718600 | tf_op jit(solution)/shard_map/ppermute | solution.py:20
  43.1 218.2 %collective-permute-start.1 = (bf16[24,128,256]{2,1,0:T(8,128)(2,1)S(1)}, bf16[24,128,256]{2,1,0:T(8,128)(2,1)}, u32[]{:S(2)}, u32[]{:S(2)}) collective-permute-start(bf16[24,128,256]{2,1,0:T(8,128)(2,1)S(1)} %maximum_bitcast_fusion), channel_id=1, source_target_pairs={{1,0},{2,1},{3,2},{4,3},{5,4},{6,5},{7,6},{9,8},{10,9},{11,10},{12... | collective-permute-start | bytes 4718600 | tf_op jit(solution)/shard_map/ppermute | solution.py:21
  275.1 7.2 %copy-start = (f32[4,6,128,128]{3,2,1,0:T(8,128)S(1)}, f32[4,6,128,128]{3,2,1,0:T(8,128)}, u32[]{:S(2)}) copy-start(f32[4,6,128,128]{3,2,1,0:T(8,128)} %custom-call.4) | copy-start | bytes 4718596
  309.4 1.2 copy-start.1
  312.9 0.7 copy-start.5
  314.9 11.8 %collective-permute-start.2 = (bf16[1,128,3072]{2,1,0:T(8,128)(2,1)S(1)}, bf16[1,128,3072]{2,1,0:T(8,128)(2,1)S(1)}, u32[]{:S(2)}, u32[]{:S(2)}) collective-permute-start(bf16[1,128,3072]{2,1,0:T(8,128)(2,1)S(1)} %add_convert_fusion), channel_id=1, source_target_pairs={{24,0},{0,8},{8,16},{16,24},{25,1},{1,9},{9,17},{17,25},{26,2},{2,... | collective-permute-start | bytes 2359304 | tf_op jit(solution)/shard_map/ppermute | solution.py:29
where the time goes:
time: 328 us
  waiting for transfers between devices  224 us (68%)
  local copies, waits for them, and re-layouts  40.8 us (12%)
  other arithmetic  27 us (8%)
  blocking collectives  14.9 us (5%)
  starting transfers between devices  12 us (4%)
  matrix products  8.34 us (3%)
    ppermute x1, waiting for transfers between devices, padded(): before = lax.ppermute(last, axis, up)  212 us
    all_gather x1, blocking collectives, shards(): all_lists = lax.all_gather(lists[None], 'ctx', axis=0, tiled=True)  14.9 us
    squeeze x8, local copies, waits for them, and re-layouts, shards(): lax.map(run_group, (grouped_q, grouped_near, grouped_far, grouped_valid))  12.1 us
    ppermute x1, waiting for transfers between devices, shifted(): return lax.ppermute(block, axis, route)  10.5 us
    gather x1, local copies, waits for them, and re-layouts, shards(): jnp.take(arrived.reshape(tiles * cap, rows, 2 * HEAD_DIM), pick, axis=0)  10.1 us
    select_n x1, other arithmetic, shards(): jnp.where(filled[:, :, None, None], jnp.take(kv_heads, head_idx, axis=0),...  8.52 us
    gather x1, local copies, waits for them, and re-layouts, shards(): jnp.take(kv_heads, head_idx, axis=0)  7.26 us
    select_n x2, other arithmetic, shards(): jnp.take(arrived.reshape(tiles * cap, rows, 2 * HEAD_DIM), pick, axis=0)  7.21 us
  transfers between devices with their start and end apart: 4, of which 3 were waited for; matrix products, arithmetic and copies ran while one was open for 2% of the time, Pallas kernels for 0%

commit v1 on v0

v1 whole, which is shorter than its diff:
```python
import functools
import math

import jax
import jax.numpy as jnp
from jax import lax
from jax.experimental import pallas as pl
from jax.experimental.pallas import tpu as pltpu
from jax.sharding import PartitionSpec as P

HEADS = 24
HEAD_DIM = 128
K_LIST = 5
SCALE = math.log2(math.e) / math.sqrt(HEAD_DIM)
MASKED = -1e30


def dot_nt(a, b):
    return lax.dot_general(a, b, (((1,), (1,)), ((), ())), preferred_element_type=jnp.float32)


def attend(query, key_tiles, value_tiles, mults):
    scores = []
    top = None
    for key, mult in zip(key_tiles, mults):
        bias = jnp.where(mult > 0, 0.0, MASKED)
        one = dot_nt(query, key) * SCALE + bias
        scores.append(one)
        peak = jnp.max(one, axis=-1, keepdims=True)
        top = peak if top is None else jnp.maximum(top, peak)
    total = None
    mixed = None
    for one, value, mult in zip(scores, value_tiles, mults):
        weights = jnp.exp2(one - top) * mult
        part = jnp.sum(weights, axis=-1, keepdims=True)
        moved = jnp.dot(weights.astype(jnp.bfloat16), value, preferred_element_type=jnp.float32)
        total = part if total is None else total + part
        mixed = moved if mixed is None else mixed + moved
    return mixed / total


def finish(residual, gate, attention):
    return (residual.astype(jnp.float32) + gate * attention).astype(jnp.bfloat16)


def dense_kernel(tiles, mult_ref, q_ref, k_ref, v_ref, r_ref, g_ref, o_ref):
    head = pl.program_id(0)
    rows = q_ref.shape[0]
    keys = [k_ref[j * rows : (j + 1) * rows, :] for j in range(tiles)]
    vals = [v_ref[j * rows : (j + 1) * rows, :] for j in range(tiles)]
    mults = [mult_ref[head * tiles + j] for j in range(tiles)]
    o_ref[...] = finish(r_ref[...], g_ref[...], attend(q_ref[...], keys, vals, mults))


def multiplicity(lists, valid, me, tiles):
    tile = jnp.arange(tiles)
    near = (jnp.abs(tile - me) <= 1).astype(jnp.int32)
    chosen = (lists[:, :, None] == tile[None, None, :]) & (
        jnp.arange(K_LIST)[None, :] < valid[:, None]
    )[:, :, None]
    return (near[None, :] + jnp.sum(chosen.astype(jnp.int32), axis=1)).astype(jnp.float32)


def shifted(block, axis, distance):
    devices = range(lax.axis_size(axis))
    return lax.ppermute(block, axis, [((i - distance) % len(devices), i) for i in devices])


def gathered_section(queries, keys, values, residual, gate, tile_lists, counts):
    rows = queries.shape[1]
    tiles = lax.axis_size("ctx")
    me = lax.axis_index("ctx")
    all_k = lax.all_gather(keys[0], "ctx", axis=0, tiled=True)
    all_v = lax.all_gather(values[0], "ctx", axis=0, tiled=True)
    mult = multiplicity(tile_lists[0, 0], counts[0, 0], me, tiles).reshape(HEADS * tiles)
    own = pl.BlockSpec((rows, HEAD_DIM), lambda h, m: (0, h))
    full = pl.BlockSpec((tiles * rows, HEAD_DIM), lambda h, m: (0, h))
    updated = pl.pallas_call(
        functools.partial(dense_kernel, tiles),
        out_shape=jax.ShapeDtypeStruct((rows, HEADS * HEAD_DIM), jnp.bfloat16),
        grid_spec=pltpu.PrefetchScalarGridSpec(
            num_scalar_prefetch=1,
            grid=(HEADS,),
            in_specs=[own, full, full, own, pl.BlockSpec((1, HEAD_DIM), lambda h, m: (0, h))],
            out_specs=own,
        ),
    )(mult, queries[0], all_k, all_v, residual[0], gate)
    return shifted(updated[None], "pipe", 1)


def pick_kernel(head_ref, k_ref, v_ref, o_ref):
    o_ref[0, :, :HEAD_DIM] = k_ref[...]
    o_ref[0, :, HEAD_DIM:] = v_ref[...]


def listed_kernel(pick_ref, valid_ref, edge_ref, q_ref, *refs):
    near_k, near_v, far = refs[:3], refs[3:6], refs[6 : 6 + K_LIST]
    r_ref, g_ref, o_ref = refs[6 + K_LIST :]
    head = pl.program_id(0)
    one = jnp.float32(1.0)
    mults = [edge_ref[0].astype(jnp.float32), one, edge_ref[1].astype(jnp.float32)]
    mults += [jnp.where(k < valid_ref[head], 1.0, 0.0) for k in range(K_LIST)]
    keys = [ref[...] for ref in near_k] + [ref[0, :, :HEAD_DIM] for ref in far]
    vals = [ref[...] for ref in near_v] + [ref[0, :, HEAD_DIM:] for ref in far]
    o_ref[...] = finish(r_ref[...], g_ref[...], attend(q_ref[...], keys, vals, mults))


def listed_section(queries, keys, values, residual, gate, tile_lists, counts):
    rows = queries.shape[1]
    tiles = lax.axis_size("ctx")
    me = lax.axis_index("ctx")
    cap = (HEADS * K_LIST + tiles - 2) // (tiles - 1)
    lists = tile_lists[0, 0]
    up = [(i, i + 1) for i in range(tiles - 1)]
    down = [(j, i) for i, j in up]
    near_k = [lax.ppermute(keys[0], "ctx", up), keys[0], lax.ppermute(keys[0], "ctx", down)]
    near_v = [lax.ppermute(values[0], "ctx", up), values[0], lax.ppermute(values[0], "ctx", down)]
    flat = lax.all_gather(lists.reshape(1, HEADS * K_LIST), "ctx", axis=0, tiled=True)

    def entry_ranks(entries):
        same = entries[:, None] == entries[None, :]
        earlier = entry[None, :] < entry[:, None]
        return jnp.sum((same & earlier).astype(jnp.int32), axis=-1)

    mine = flat == me
    entry = jnp.arange(HEADS * K_LIST)
    before = (entry[:, None] < entry[None, :]).astype(jnp.float32)
    rank = jnp.dot(mine.astype(jnp.float32), before).astype(jnp.int32)
    head_of = jnp.arange(HEADS * K_LIST) // K_LIST
    slot = jnp.arange(cap)
    hit = mine[:, :, None] & (rank[:, :, None] == slot[None, None, :])
    heads = jnp.sum(jnp.where(hit, head_of[None, :, None], 0), axis=1).reshape(tiles * cap)
    pair = pl.BlockSpec((rows, HEAD_DIM), lambda i, h: (0, h[i]))
    outgoing = pl.pallas_call(
        pick_kernel,
        out_shape=jax.ShapeDtypeStruct((tiles * cap, rows, 2 * HEAD_DIM), jnp.bfloat16),
        grid_spec=pltpu.PrefetchScalarGridSpec(
            num_scalar_prefetch=1,
            grid=(tiles * cap,),
            in_specs=[pair, pair],
            out_specs=pl.BlockSpec((1, rows, 2 * HEAD_DIM), lambda i, h: (i, 0, 0)),
        ),
    )(heads, keys[0], values[0])
    arrived = lax.all_to_all(outgoing, "ctx", split_axis=0, concat_axis=0, tiled=True)
    own_entries = lists.reshape(HEADS * K_LIST)
    pick = own_entries * cap + entry_ranks(own_entries)
    edge = jnp.stack([me > 0, me < tiles - 1]).astype(jnp.int32)
    own = pl.BlockSpec((rows, HEAD_DIM), lambda h, p, c, e: (0, h))
    far = [
        pl.BlockSpec((1, rows, 2 * HEAD_DIM), lambda h, p, c, e, k=k: (p[h * K_LIST + k], 0, 0))
        for k in range(K_LIST)
    ]
    updated = pl.pallas_call(
        listed_kernel,
        out_shape=jax.ShapeDtypeStruct((rows, HEADS * HEAD_DIM), jnp.bfloat16),
        grid_spec=pltpu.PrefetchScalarGridSpec(
            num_scalar_prefetch=3,
            grid=(HEADS,),
            in_specs=[own] * 7 + far + [own, pl.BlockSpec((1, HEAD_DIM), lambda h, p, c, e: (0, h))],
            out_specs=own,
        ),
    )(pick, counts[0, 0], edge, queries[0], *near_k, *near_v, *([arrived] * K_LIST), residual[0], gate)
    return shifted(updated[None], "pipe", 1)


def solution(mesh):
    rows = P("pipe", "ctx", None)
    placed = (rows, rows, rows, rows, P("pipe", None), P("pipe", "ctx", None, None), rows)
    section = gathered_section if mesh.shape["ctx"] <= 8 else listed_section
    return jax.shard_map(section, mesh=mesh, in_specs=placed, out_specs=rows, check_vma=False)
```

time: 328 us -> 195 us (0.59)
  the two profiles are of different devices: /device:TPU:9 before, /device:TPU:0 now
where the time goes in v1:
time: 195 us; the launch traced here: 194 us
  waiting for transfers between devices  152 us (78%)
  Pallas kernels  23.8 us (12%)
  between operations  13.4 us (7%)
  local copies, waits for them, and re-layouts  2.27 us (1%)
    all_gather x1, waiting for transfers between devices, gathered_section(): all_k = lax.all_gather(keys[0], 'ctx', axis=0, tiled=True)  66.3 us
    all_gather x1, waiting for transfers between devices, gathered_section(): all_v = lax.all_gather(values[0], 'ctx', axis=0, tiled=True)  65.1 us
    pallas_call x1, Pallas kernels, gathered_section(): pl.pallas_call(functools.partial(dense_kernel, tiles), out_shape=jax.Shap...  23.8 us
    ppermute x1, waiting for transfers between devices, shifted(): lax.ppermute(block, axis, [((i - distance) % len(devices), i) for i in de...  19.3 us
  transfers between devices with their start and end apart: 3, of which 3 were waited for; matrix products, arithmetic and copies ran while one was open for 1% of the time, Pallas kernels for 0%

profile of v1, /device:TPU:0, one launch (start us, length us, event | category | flops | bytes accessed | tf_op | source)
XLA Modules:
  0.0 193.9 jit_solution(17577012334089317958)
XLA Ops:
  6.5 0.0 all-gather.5.cloned.1.call-start
  6.5 0.7 all-gather.5.cloned.1.call-update
  7.3 0.0 all-gather.7.cloned.1.call-start
  7.3 0.7 all-gather.7.cloned.1.call-update
  8.0 0.7 copy.13
  8.7 0.7 iota_compare_fusion.1
  9.4 0.1 add_convert_fusion
  9.5 0.1 copy.10
  9.5 0.6 convert_element_type.20.mult_ref
  10.2 66.3 %all-gather.5.cloned.1.call-done = bf16[1,1024,3072]{2,1,0:T(8,128)(2,1)} async-done(((bf16[1,128,3072]{2,1,0:T(8,128)(2,1)}), bf16[1,1024,3072]{2,1,0:T(8,128)(2,1)}) %all-gather.5.cloned.1.call-update) | async-done | bytes 6291472 | tf_op jit(solution)/shard_map/all_gather | solution.py:73
  76.5 65.1 %all-gather.7.cloned.1.call-done = bf16[1,1024,3072]{2,1,0:T(8,128)(2,1)} async-done(((bf16[1,128,3072]{2,1,0:T(8,128)(2,1)}), bf16[1,1024,3072]{2,1,0:T(8,128)(2,1)}) %all-gather.7.cloned.1.call-update) | async-done | bytes 6291472 | tf_op jit(solution)/shard_map/all_gather | solution.py:74
  141.6 23.8 %shard_map.73 = bf16[128,3072]{1,0:T(8,128)(2,1)} custom-call(f32[192]{0:T(256)} %convert_element_type.20.mult_ref, bf16[128,3072]{1,0:T(8,128)(2,1)} %bitcast.11, bf16[1024,3072]{1,0:T(8,128)(2,1)} %bitcast.9, bf16[1024,3072]{1,0:T(8,128)(2,1)} %bitcast.10, bf16[128,3072]{1,0:T(8,128)(2,1)} %bitcast.12, f32[1,3072]{1,0:T(1,128)} %g_ref.1), custom_call_target="tpu_custom_call" | custom-call | tf_op jit(solution)/shard_map/pallas_call | solution.py:78
  165.4 1.5 collective-permute-start
  166.9 19.3 %collective-permute-done = bf16[1,128,3072]{2,1,0:T(8,128)(2,1)S(1)} collective-permute-done((bf16[1,128,3072]{2,1,0:T(8,128)(2,1)}, bf16[1,128,3072]{2,1,0:T(8,128)(2,1)S(1)}, u32[]{:S(2)}, u32[]{:S(2)}) %collective-permute-start) | collective-permute-done | bytes 786464 | tf_op jit(solution)/shard_map/ppermute | solution.py:66
  186.2 0.9 copy.15
  (2 shorter events, 0.0 us)
Async XLA Ops:
  6.5 70.0 %all-gather.5.cloned.1.call-start = ((), (), s32[]{:S(2)}) async-start(), calls=%async_computation | async-start | bytes 7077888 | tf_op jit(solution)/shard_map/all_gather | solution.py:73
  7.3 134.3 %all-gather.7.cloned.1.call-start = ((), (), s32[]{:S(2)}) async-start(), calls=%async_computation.1 | async-start | bytes 7077888 | tf_op jit(solution)/shard_map/all_gather | solution.py:74
  165.4 20.8 %collective-permute-start = (bf16[1,128,3072]{2,1,0:T(8,128)(2,1)}, bf16[1,128,3072]{2,1,0:T(8,128)(2,1)S(1)}, u32[]{:S(2)}, u32[]{:S(2)}) collective-permute-start(bf16[1,128,3072]{2,1,0:T(8,128)(2,1)} %bitcast.13), channel_id=1, source_target_pairs={{24,0},{0,8},{8,16},{16,24},{25,1},{1,9},{9,17},{17,25},{26,2},{2,... | collective-permute-start | bytes 2359304 | tf_op jit(solution)/shard_map/ppermute | solution.py:66
Sparse Core Ops, SparseCore 0:
  9.0 67.4 all-gather.4
  78.1 63.3 all-gather.6

commit v2 on v1

--- a/solution.py
+++ b/solution.py
@@ -11,6 +11,7 @@
 HEADS = 24
 HEAD_DIM = 128
 K_LIST = 5
+GROUPS = (5, 5, 2)
 SCALE = math.log2(math.e) / math.sqrt(HEAD_DIM)
 MASKED = -1e30
 
@@ -20,36 +21,34 @@
 
 
 def attend(query, key_tiles, value_tiles, mults):
-    scores = []
-    top = None
-    for key, mult in zip(key_tiles, mults):
-        bias = jnp.where(mult > 0, 0.0, MASKED)
-        one = dot_nt(query, key) * SCALE + bias
-        scores.append(one)
-        peak = jnp.max(one, axis=-1, keepdims=True)
-        top = peak if top is None else jnp.maximum(top, peak)
-    total = None
-    mixed = None
-    for one, value, mult in zip(scores, value_tiles, mults):
-        weights = jnp.exp2(one - top) * mult
-        part = jnp.sum(weights, axis=-1, keepdims=True)
-        moved = jnp.dot(weights.astype(jnp.bfloat16), value, preferred_element_type=jnp.float32)
-        total = part if total is None else total + part
-        mixed = moved if mixed is None else mixed + moved
-    return mixed / total
+    scores = [
+        dot_nt(query, key) * SCALE + jnp.where(mult > 0, 0.0, MASKED)
+        for key, mult in zip(key_tiles, mults)
+    ]
+    top = jnp.max(functools.reduce(jnp.maximum, scores), axis=-1, keepdims=True)
+    weights = [jnp.exp2(one - top) * mult for one, mult in zip(scores, mults)]
+    total = jnp.sum(functools.reduce(jnp.add, weights), axis=-1, keepdims=True)
+    rounded = jnp.concatenate([one.astype(jnp.bfloat16) for one in weights], axis=1)
+    value = jnp.concatenate(value_tiles, axis=0)
+    return jnp.dot(rounded, value, preferred_element_type=jnp.float32) / total
 
 
 def finish(residual, gate, attention):
     return (residual.astype(jnp.float32) + gate * attention).astype(jnp.bfloat16)
 
 
-def dense_kernel(tiles, mult_ref, q_ref, k_ref, v_ref, r_ref, g_ref, o_ref):
-    head = pl.program_id(0)
-    rows = q_ref.shape[0]
-    keys = [k_ref[j * rows : (j + 1) * rows, :] for j in range(tiles)]
-    vals = [v_ref[j * rows : (j + 1) * rows, :] for j in range(tiles)]
-    mults = [mult_ref[head * tiles + j] for j in range(tiles)]
-    o_ref[...] = finish(r_ref[...], g_ref[...], attend(q_ref[...], keys, vals, mults))
+def relay_kernel(first, heads, mult_ref, *refs):
+    pairs, rests, (g_ref,), outs = refs[:4], refs[4:6], refs[6:7], refs[7:]
+    head = first + pl.program_id(0)
+    rows = pairs[0].shape[0] // 4
+    tile = [slice(j * rows, (j + 1) * rows) for j in range(4)]
+    keys = [ref[tile[j], :] for ref in pairs for j in (0, 2)]
+    vals = [ref[tile[j], :] for ref in pairs for j in (1, 3)]
+    for t, o_ref in enumerate(outs):
+        rest, place = rests[t // 2], 2 * (t % 2)
+        mults = [mult_ref[(t * heads + head) * 8 + j] for j in range(8)]
+        mixed = attend(rest[tile[place], :], keys, vals, mults)
+        o_ref[...] = finish(rest[tile[place + 1], :], g_ref[...], mixed)
 
 
 def multiplicity(lists, valid, me, tiles):
@@ -66,26 +65,97 @@
     return lax.ppermute(block, axis, [((i - distance) % len(devices), i) for i in devices])
 
 
-def gathered_section(queries, keys, values, residual, gate, tile_lists, counts):
+def relay_section(queries, keys, values, residual, gate, tile_lists, counts):
     rows = queries.shape[1]
     tiles = lax.axis_size("ctx")
+    sections = lax.axis_size("pipe")
     me = lax.axis_index("ctx")
-    all_k = lax.all_gather(keys[0], "ctx", axis=0, tiled=True)
-    all_v = lax.all_gather(values[0], "ctx", axis=0, tiled=True)
-    mult = multiplicity(tile_lists[0, 0], counts[0, 0], me, tiles).reshape(HEADS * tiles)
-    own = pl.BlockSpec((rows, HEAD_DIM), lambda h, m: (0, h))
-    full = pl.BlockSpec((tiles * rows, HEAD_DIM), lambda h, m: (0, h))
-    updated = pl.pallas_call(
-        functools.partial(dense_kernel, tiles),
-        out_shape=jax.ShapeDtypeStruct((rows, HEADS * HEAD_DIM), jnp.bfloat16),
-        grid_spec=pltpu.PrefetchScalarGridSpec(
-            num_scalar_prefetch=1,
-            grid=(HEADS,),
-            in_specs=[own, full, full, own, pl.BlockSpec((1, HEAD_DIM), lambda h, m: (0, h))],
-            out_specs=own,
-        ),
-    )(mult, queries[0], all_k, all_v, residual[0], gate)
-    return shifted(updated[None], "pipe", 1)
+    chip, core = me // 2, me % 2
+    half = HEADS // 2
+    width = half * HEAD_DIM
+
+    swap = [(i, i ^ 1) for i in range(8)]
+    inward = [(2 * z + c, 2 * (z ^ 1) + c) for z in range(4) for c in (0, 1)]
+    across = [(2, 4), (3, 5), (4, 2), (5, 3), (0, 1), (1, 0), (6, 7), (7, 6)]
+
+    def onward(change):
+        return [
+            (p * tiles + i, (p + 1) % sections * tiles + (i ^ change))
+            for p in range(sections)
+            for i in range(tiles)
+        ]
+
+    def ctx(block, route):
+        return lax.ppermute(block, "ctx", route)
+
+    def halves(block):
+        left, right = block[..., :width], block[..., width:]
+        return jnp.where(core == 0, left, right), jnp.where(core == 0, right, left)
+
+    edges = [0]
+    for size in GROUPS:
+        edges.append(edges[-1] + size)
+    cut = [slice(a * HEAD_DIM, b * HEAD_DIM) for a, b in zip(edges, edges[1:])]
+    groups = range(len(GROUPS))
+
+    kv_mine, kv_theirs = halves(jnp.concatenate([keys[0], values[0]], axis=0))
+    qr_mine, qr_theirs = halves(jnp.concatenate([queries[0], residual[0]], axis=0))
+    first = ctx(kv_theirs[:, cut[0]], swap)
+    later = ctx(jnp.concatenate([kv_theirs[:, cut[0].stop :], qr_theirs], axis=1), swap)
+    kv_got = jnp.concatenate([first, later[:, : width - cut[0].stop]], axis=1)
+    qr_got = later[:, width - cut[0].stop :]
+    own = [jnp.concatenate([kv_mine[:, c], kv_got[:, c]], axis=0) for c in cut]
+    own_qr = [jnp.concatenate([qr_mine[:, c], qr_got[:, c]], axis=0) for c in cut]
+
+    end, end_qr, near, far = [], [], [], []
+    for g in groups:
+        near.append(ctx(own[g], across))
+        end.append(ctx(own[g], inward))
+        end_qr.append(ctx(own_qr[g], inward))
+        far.append(ctx(end[g], across))
+
+    table = multiplicity(tile_lists[0, 0], counts[0, 0], me, tiles).reshape(2, half, tiles)
+    table_mine = jnp.where(core == 0, table[0], table[1])
+    table_theirs = jnp.where(core == 0, table[1], table[0])
+    table = jnp.stack([table_mine, ctx(table_theirs, swap)])
+    table = jnp.concatenate([table, ctx(table, inward)], axis=0)
+    chips = jnp.stack([chip, chip ^ 1, 3 - chip, 3 - (chip ^ 1)])
+    order = (2 * chips[:, None] + jnp.stack([core, 1 - core])[None, :]).reshape(1, 1, 8, 1)
+    table = jnp.sum(jnp.where(order == jnp.arange(tiles), table[:, :, None, :], 0.0), axis=-1)
+    table = table.reshape(4 * half * tiles)
+    gate_mine, _ = halves(gate)
+
+    block = pl.BlockSpec((4 * rows, HEAD_DIM), lambda h, m: (0, h))
+    line = pl.BlockSpec((1, HEAD_DIM), lambda h, m: (0, h))
+    one = pl.BlockSpec((rows, HEAD_DIM), lambda h, m: (0, h))
+    same, other = [], []
+    for g in groups:
+        size = GROUPS[g]
+        results = pl.pallas_call(
+            functools.partial(relay_kernel, edges[g], half),
+            out_shape=[jax.ShapeDtypeStruct((rows, size * HEAD_DIM), jnp.bfloat16)] * 4,
+            grid_spec=pltpu.PrefetchScalarGridSpec(
+                num_scalar_prefetch=1,
+                grid=(size,),
+                in_specs=[block] * 6 + [line],
+                out_specs=[one] * 4,
+            ),
+            cost_estimate=pl.CostEstimate(
+                flops=size * 16 * rows * 8 * rows * HEAD_DIM,
+                bytes_accessed=size * 28 * rows * HEAD_DIM * 2,
+                transcendentals=size * 4 * rows * 8 * rows,
+            ),
+        )(table, own[g], end[g], near[g], far[g], own_qr[g], end_qr[g], gate_mine[:, cut[g]])
+        sent = [
+            lax.ppermute(piece, ("pipe", "ctx"), onward(change))
+            for piece, change in zip(results, (0, 1, 2, 3))
+        ]
+        inner = (chip == 1) | (chip == 2)
+        same.append(jnp.where(inner, sent[0], sent[2]))
+        other.append(jnp.where(inner, sent[1], sent[3]))
+    same, other = jnp.concatenate(same, axis=1), jnp.concatenate(other, axis=1)
+    left, right = jnp.where(core == 0, same, other), jnp.where(core == 0, other, same)
+    return jnp.concatenate([left, right], axis=1)[None]
 
 
 def pick_kernel(head_ref, k_ref, v_ref, o_ref):
@@ -166,5 +236,5 @@
 def solution(mesh):
     rows = P("pipe", "ctx", None)
     placed = (rows, rows, rows, rows, P("pipe", None), P("pipe", "ctx", None, None), rows)
-    section = gathered_section if mesh.shape["ctx"] <= 8 else listed_section
+    section = relay_section if mesh.shape["ctx"] == 8 else listed_section
     return jax.shard_map(section, mesh=mesh, in_specs=placed, out_specs=rows, check_vma=False)

time: 195 us -> 134 us (0.69)
  waiting for transfers between devices: 152 us -> 40.7 us
  starting transfers between devices: 1.51 us -> 46.1 us
  between operations: 13.4 us -> 0.34 us
  Pallas kernels: 23.8 us -> 31.3 us
  other arithmetic: 0.75 us -> 7.54 us
  local copies, waits for them, and re-layouts: 2.27 us -> 7.28 us
    all_gather x2 -> x0, waiting for transfers between devices: 131 us -> none  [the longest x1 66.3 us: gathered_section(): all_k = lax.all_gather(keys[0], 'ctx', axis=0, tiled=True)]
    ppermute x1 -> x28, starting transfers between devices: 1.47 us -> 46.1 us  [the longest x12 30.8 us: relay_section(): lax.ppermute(piece, ('pipe', 'ctx'), onward(change))]
    ppermute x1 -> x28, waiting for transfers between devices: 19.3 us -> 40.7 us  [the longest x12 24 us: relay_section(): lax.ppermute(piece, ('pipe', 'ctx'), onward(change))]
    pallas_call x1 -> x3, Pallas kernels: 23.8 us -> 31.3 us  [relay_section(): pl.pallas_call(functools.partial(relay_kernel, edges[g], half), out_shape...]
    slice x0 -> x10, local copies, waits for them, and re-layouts: none -> 4.35 us  [the longest x2 2.25 us: relay_section(): qr_got[:, c]]
    select_n x0 -> x9, other arithmetic: none -> 3.02 us  [the longest x2 2.78 us: halves(): jnp.where(core == 0, left, right)]
    concatenate x0 -> x8, other arithmetic: none -> 2.31 us  [the longest x1 1.17 us: relay_section(): jnp.concatenate([kv_theirs[:, cut[0].stop:], qr_theirs], axis=1)]
  transfers between devices with their start and end apart: 3 -> 28, of which waited for: 3 -> 7; matrix products, arithmetic and copies ran while one was open for 1% -> 8% of each run, Pallas kernels for 0% -> 24%
where the time goes in v2:
time: 134 us; the launch traced here: 133 us
  starting transfers between devices  46.1 us (34%)
  waiting for transfers between devices  40.7 us (30%)
  Pallas kernels  31.3 us (23%)
  other arithmetic  7.54 us (6%)
  local copies, waits for them, and re-layouts  7.28 us (5%)
    pallas_call x3, Pallas kernels, relay_section(): pl.pallas_call(functools.partial(relay_kernel, edges[g], half), out_shape...  31.3 us
    ppermute x12, starting transfers between devices, relay_section(): lax.ppermute(piece, ('pipe', 'ctx'), onward(change))  30.8 us
    ppermute x12, waiting for transfers between devices, relay_section(): lax.ppermute(piece, ('pipe', 'ctx'), onward(change))  24 us
    ppermute x16, waiting for transfers between devices, ctx(): return lax.ppermute(block, 'ctx', route)  16.7 us
    ppermute x16, starting transfers between devices, ctx(): return lax.ppermute(block, 'ctx', route)  15.3 us
    select_n x2, other arithmetic, halves(): jnp.where(core == 0, left, right)  2.78 us
  transfers between devices with their start and end apart: 28, of which 7 were waited for; matrix products, arithmetic and copies ran while one was open for 8% of the time, Pallas kernels for 24%

profile of v2, /device:TPU:0, one launch (start us, length us, event | category | flops | bytes accessed | tf_op | source)
XLA Modules:
  0.0 133.2 jit_solution(2435455409513464063)
XLA Ops:
  0.0 0.7 copy.15
  0.7 0.7 iota_compare_fusion.1
  1.5 0.5 collective-permute-start
  2.0 2.8 %broadcast_select_fusion.1 = (bf16[256,1536]{1,0:T(8,128)(2,1)S(1)}, bf16[256,1536]{1,0:T(8,128)(2,1)S(1)}, bf16[256,1536]{1,0:T(8,128)(2,1)S(1)}, bf16[256,1536]{1,0:T(8,128)(2,1)S(1)}) fusion(pred[]{:T(512)S(6)} %eq.27, bf16[128,3072]{1,0:T(8,128)(2,1)} %bitcast.19, bf16[128,3072]{1,0:T(8,128)(2,1)} %bitcast.20, bf16[128,3072]{1,0:T(8,128)(2,1)} %bitcast.21, ...), kind=kLoop, calls=%fused_computation.11 | loop fusion | flops 11010048 | bytes 6291457 | tf_op jit(solution)/shard_map/jit(_where)/select_n | solution.py:93
  4.8 1.2 pad_maximum_fusion
  6.0 0.8 slice.110
  6.8 0.5 collective-permute-start.2
  7.4 0.6 fusion.7
  8.2 0.1 add.37
  8.3 2.6 %collective-permute-start.1 = (f32[2,12,8]{1,2,0:T(8,128)S(1)}, f32[2,12,8]{1,2,0:T(8,128)S(1)}, u32[]{:S(2)}, u32[]{:S(2)}) collective-permute-start(f32[2,12,8]{1,2,0:T(8,128)S(1)} %pad_maximum_fusion.12), channel_id=1, source_target_pairs={{0,2},{1,3},{2,0},{3,1},{4,6},{5,7},{6,4},{7,5},{8,10},{9,11},{10,... | collective-permute-start | bytes 2312 | tf_op jit(solution)/shard_map/ppermute | solution.py:89
  11.0 0.9 pad_maximum_fusion.3.refs_0_
  11.9 1.3 %collective-permute-start.3 = (bf16[512,640]{1,0:T(8,128)(2,1)}, bf16[512,640]{1,0:T(8,128)(2,1)}, u32[]{:S(2)}, u32[]{:S(2)}) collective-permute-start(bf16[512,640]{1,0:T(8,128)(2,1)} %pad_maximum_fusion.3.refs_0_), channel_id=1, source_target_pairs={{0,2},{1,3},{2,0},{3,1},{4,6},{5,7},{6,4},{7,5},{8,10},{9,11},{10,... | collective-permute-start | bytes 1966088 | tf_op jit(solution)/shard_map/ppermute | solution.py:89
  13.3 1.0 fusion.4
  14.3 0.7 collective-permute-start.16
  15.1 3.2 %collective-permute-start.19 = (bf16[512,256]{1,0:T(8,128)(2,1)S(1)}, bf16[512,256]{1,0:T(8,128)(2,1)S(1)}, u32[]{:S(2)}, u32[]{:S(2)}) collective-permute-start(bf16[512,256]{1,0:T(8,128)(2,1)S(1)} %pad_maximum_fusion.10.refs_4_), channel_id=1, source_target_pairs={{0,2},{1,3},{2,0},{3,1},{4,6},{5,7},{6,4},{7,5},{8,10},{9,11},{10,... | collective-permute-start | bytes 786440 | tf_op jit(solution)/shard_map/ppermute | solution.py:89
  18.3 1.3 fusion.3
  19.7 10.1 %collective-permute-done.3.refs_1_ = bf16[512,640]{1,0:T(8,128)(2,1)} collective-permute-done((bf16[512,640]{1,0:T(8,128)(2,1)}, bf16[512,640]{1,0:T(8,128)(2,1)}, u32[]{:S(2)}, u32[]{:S(2)}) %collective-permute-start.3) | collective-permute-done | bytes 655392 | tf_op jit(solution)/shard_map/ppermute | solution.py:89
  29.8 1.3 collective-permute-start.10
  31.2 4.2 %collective-permute-done.16.refs_1_ = bf16[512,256]{1,0:T(8,128)(2,1)} collective-permute-done((bf16[512,256]{1,0:T(8,128)(2,1)S(1)}, bf16[512,256]{1,0:T(8,128)(2,1)}, u32[]{:S(2)}, u32[]{:S(2)}) %collective-permute-start.16) | collective-permute-done | bytes 262176 | tf_op jit(solution)/shard_map/ppermute | solution.py:89
  35.4 3.1 %collective-permute-start.7 = (bf16[512,640]{1,0:T(8,128)(2,1)S(1)}, bf16[512,640]{1,0:T(8,128)(2,1)}, u32[]{:S(2)}, u32[]{:S(2)}) collective-permute-start(bf16[512,640]{1,0:T(8,128)(2,1)S(1)} %pad_maximum_fusion.4.refs_4_), channel_id=1, source_target_pairs={{0,2},{1,3},{2,0},{3,1},{4,6},{5,7},{6,4},{7,5},{8,10},{9,11},{10,... | collective-permute-start | bytes 1966088 | tf_op jit(solution)/shard_map/ppermute | solution.py:89
  38.6 2.4 %collective-permute-done.19.refs_5_ = bf16[512,256]{1,0:T(8,128)(2,1)S(1)} collective-permute-done((bf16[512,256]{1,0:T(8,128)(2,1)S(1)}, bf16[512,256]{1,0:T(8,128)(2,1)S(1)}, u32[]{:S(2)}, u32[]{:S(2)}) %collective-permute-start.19) | collective-permute-done | bytes 262176 | tf_op jit(solution)/shard_map/ppermute | solution.py:89
  41.0 0.6 copy-done.7
  41.6 0.6 slice.126.refs_6_
  42.2 0.1 select_reduce_fusion
  42.3 0.1 copy.12
  42.4 0.7 reshape.114.mult_ref
  43.1 0.7 copy-done.8
  43.8 6.5 %shard_map.75 = (bf16[128,256]{1,0:T(8,128)(2,1)}, bf16[128,256]{1,0:T(8,128)(2,1)}, bf16[128,256]{1,0:T(8,128)(2,1)}, bf16[128,256]{1,0:T(8,128)(2,1)}) custom-call(f32[384]{0:T(512)} %reshape.114.mult_ref, bf16[512,256]{1,0:T(8,128)(2,1)} %copy-done.3, bf16[512,256]{1,0:T(8,128)(2,1)} %collective-permute-done.16.refs_1_, bf16[512,256]{1,0:T(8,128)(2,1)} %copy-done.6, ...), custom_call_target="tpu_custom_call" | custom-call | flops 536870912 | bytes 1835008 | tf_op jit(solution)/shard_map/pallas_call | solution.py:134
  50.3 1.0 collective-permute-start.26
  51.3 16.2 %collective-permute-start.27 = (bf16[128,256]{1,0:T(8,128)(2,1)}, bf16[128,256]{1,0:T(8,128)(2,1)S(1)}, u32[]{:S(2)}, u32[]{:S(2)}) collective-permute-start(bf16[128,256]{1,0:T(8,128)(2,1)} %get-tuple-element.28), channel_id=1, source_target_pairs={{0,11},{1,10},{2,9},{3,8},{4,15},{5,14},{6,13},{7,12},{8,19},{9,18... | collective-permute-start | bytes 196616 | tf_op jit(solution)/shard_map/ppermute | solution.py:150
  67.8 3.1 %collective-permute-done.27 = bf16[128,256]{1,0:T(8,128)(2,1)S(1)} collective-permute-done((bf16[128,256]{1,0:T(8,128)(2,1)}, bf16[128,256]{1,0:T(8,128)(2,1)S(1)}, u32[]{:S(2)}, u32[]{:S(2)}) %collective-permute-start.27) | collective-permute-done | bytes 65568 | tf_op jit(solution)/shard_map/ppermute | solution.py:150
  70.9 1.5 %collective-permute-start.13 = (bf16[512,640]{1,0:T(8,128)(2,1)S(1)}, bf16[512,640]{1,0:T(8,128)(2,1)}, u32[]{:S(2)}, u32[]{:S(2)}) collective-permute-start(bf16[512,640]{1,0:T(8,128)(2,1)S(1)} %pad_maximum_fusion.6.refs_4_), channel_id=1, source_target_pairs={{0,2},{1,3},{2,0},{3,1},{4,6},{5,7},{6,4},{7,5},{8,10},{9,11},{10,... | collective-permute-start | bytes 1966088 | tf_op jit(solution)/shard_map/ppermute | solution.py:89
  72.4 0.2 collective-permute-start.12
  72.6 0.5 collective-permute-start.20
  73.2 4.0 %collective-permute-start.21 = (bf16[128,256]{1,0:T(8,128)(2,1)S(1)}, bf16[128,256]{1,0:T(8,128)(2,1)S(1)}, u32[]{:S(2)}, u32[]{:S(2)}) collective-permute-start(bf16[128,256]{1,0:T(8,128)(2,1)S(1)} %copy-done.9), channel_id=1, source_target_pairs={{0,10},{1,11},{2,8},{3,9},{4,14},{5,15},{6,12},{7,13},{8,18},{9,19... | collective-permute-start | bytes 196616 | tf_op jit(solution)/shard_map/ppermute | solution.py:150
  77.2 12.4 %shard_map.73 = (bf16[128,640]{1,0:T(8,128)(2,1)}, bf16[128,640]{1,0:T(8,128)(2,1)}, bf16[128,640]{1,0:T(8,128)(2,1)}, bf16[128,640]{1,0:T(8,128)(2,1)}) custom-call(f32[384]{0:T(512)} %reshape.114.mult_ref, bf16[512,640]{1,0:T(8,128)(2,1)} %pad_maximum_fusion.3.refs_0_, bf16[512,640]{1,0:T(8,128)(2,1)} %collective-permute-done.3.refs_1_, ...), custom_call_target="tpu_custom_call" | custom-call | flops 1342177280 | bytes 4587520 | tf_op jit(solution)/shard_map/pallas_call | solution.py:134
  89.7 1.4 %collective-permute-start.23 = (bf16[128,640]{1,0:T(8,128)(2,1)}, bf16[128,640]{1,0:T(8,128)(2,1)S(1)}, u32[]{:S(2)}, u32[]{:S(2)}) collective-permute-start(bf16[128,640]{1,0:T(8,128)(2,1)} %get-tuple-element.24), channel_id=1, source_target_pairs={{0,11},{1,10},{2,9},{3,8},{4,15},{5,14},{6,13},{7,12},{8,19},{9,18... | collective-permute-start | bytes 491528 | tf_op jit(solution)/shard_map/ppermute | solution.py:150
  91.1 9.1 %collective-permute-done.22 = bf16[128,640]{1,0:T(8,128)(2,1)S(1)} collective-permute-done((bf16[128,640]{1,0:T(8,128)(2,1)}, bf16[128,640]{1,0:T(8,128)(2,1)S(1)}, u32[]{:S(2)}, u32[]{:S(2)}) %collective-permute-start.22) | collective-permute-done | bytes 163872 | tf_op jit(solution)/shard_map/ppermute | solution.py:150
  100.2 0.2 collective-permute-start.8
  100.5 1.7 %collective-permute-start.9 = (bf16[128,640]{1,0:T(8,128)(2,1)}, bf16[128,640]{1,0:T(8,128)(2,1)S(1)}, u32[]{:S(2)}, u32[]{:S(2)}) collective-permute-start(bf16[128,640]{1,0:T(8,128)(2,1)} %get-tuple-element.18), channel_id=1, source_target_pairs={{0,10},{1,11},{2,8},{3,9},{4,14},{5,15},{6,12},{7,13},{8,18},{9,19... | collective-permute-start | bytes 491528 | tf_op jit(solution)/shard_map/ppermute | solution.py:150
  102.2 12.4 %shard_map.74 = (bf16[128,640]{1,0:T(8,128)(2,1)}, bf16[128,640]{1,0:T(8,128)(2,1)}, bf16[128,640]{1,0:T(8,128)(2,1)}, bf16[128,640]{1,0:T(8,128)(2,1)}) custom-call(f32[384]{0:T(512)} %reshape.114.mult_ref, bf16[512,640]{1,0:T(8,128)(2,1)} %copy-done, bf16[512,640]{1,0:T(8,128)(2,1)} %collective-permute-done.10.refs_1_, ...), custom_call_target="tpu_custom_call" | custom-call | flops 1342177280 | bytes 4587520 | tf_op jit(solution)/shard_map/pallas_call | solution.py:134
  114.6 3.7 %collective-permute-start.25 = (bf16[128,640]{1,0:T(8,128)(2,1)}, bf16[128,640]{1,0:T(8,128)(2,1)S(1)}, u32[]{:S(2)}, u32[]{:S(2)}) collective-permute-start(bf16[128,640]{1,0:T(8,128)(2,1)} %get-tuple-element.26), channel_id=1, source_target_pairs={{0,11},{1,10},{2,9},{3,8},{4,15},{5,14},{6,13},{7,12},{8,19},{9,18... | collective-permute-start | bytes 491528 | tf_op jit(solution)/shard_map/ppermute | solution.py:150
  118.3 0.3 collective-permute-start.14
  118.6 1.6 %collective-permute-start.15 = (bf16[128,640]{1,0:T(8,128)(2,1)}, bf16[128,640]{1,0:T(8,128)(2,1)S(1)}, u32[]{:S(2)}, u32[]{:S(2)}) collective-permute-start(bf16[128,640]{1,0:T(8,128)(2,1)} %get-tuple-element.20), channel_id=1, source_target_pairs={{0,10},{1,11},{2,8},{3,9},{4,14},{5,15},{6,12},{7,13},{8,18},{9,19... | collective-permute-start | bytes 491528 | tf_op jit(solution)/shard_map/ppermute | solution.py:150
  120.2 9.0 %collective-permute-done.24 = bf16[128,640]{1,0:T(8,128)(2,1)S(1)} collective-permute-done((bf16[128,640]{1,0:T(8,128)(2,1)}, bf16[128,640]{1,0:T(8,128)(2,1)S(1)}, u32[]{:S(2)}, u32[]{:S(2)}) %collective-permute-start.24) | collective-permute-done | bytes 163872 | tf_op jit(solution)/shard_map/ppermute | solution.py:150
  129.2 2.8 %collective-permute-done.14 = bf16[128,640]{1,0:T(8,128)(2,1)S(1)} collective-permute-done((bf16[128,640]{1,0:T(8,128)(2,1)}, bf16[128,640]{1,0:T(8,128)(2,1)S(1)}, u32[]{:S(2)}, u32[]{:S(2)}) %collective-permute-start.14) | collective-permute-done | bytes 163872 | tf_op jit(solution)/shard_map/ppermute | solution.py:150
  132.1 0.1 broadcast_select_fusion.5
  132.2 1.0 maximum_bitcast_fusion
  (76 shorter events, 1.4 us)
Async XLA Ops:
  1.5 6.8 %collective-permute-start = (f32[12,8]{0,1:T(8,128)S(1)}, f32[12,8]{0,1:T(8,128)S(1)}, u32[]{:S(2)}, u32[]{:S(2)}) collective-permute-start(f32[12,8]{0,1:T(8,128)S(1)} %get-tuple-element.47), channel_id=1, source_target_pairs={{0,1},{1,0},{2,3},{3,2},{4,5},{5,4},{6,7},{7,6},{8,9},{9,8},{10,11... | collective-permute-start | bytes 1160 | tf_op jit(solution)/shard_map/ppermute | solution.py:89
  4.8 2.4 %copy-start.5 = (f32[1,3072]{1,0:T(1,128)S(1)}, f32[1,3072]{1,0:T(1,128)}, u32[]{:S(2)}) copy-start(f32[1,3072]{1,0:T(1,128)} %param.11) | copy-start | bytes 36868
  6.0 7.3 %collective-permute-start.6 = (bf16[256,2432]{1,0:T(8,128)(2,1)}, bf16[256,2432]{1,0:T(8,128)(2,1)}, u32[]{:S(2)}, u32[]{:S(2)}) collective-permute-start(bf16[256,2432]{1,0:T(8,128)(2,1)} %pad_maximum_fusion), channel_id=1, source_target_pairs={{0,1},{1,0},{2,3},{3,2},{4,5},{5,4},{6,7},{7,6},{8,9},{9,8},{10,11... | collective-permute-start | bytes 3735560 | tf_op jit(solution)/shard_map/ppermute | solution.py:89
  6.8 4.2 %collective-permute-start.2 = (bf16[256,640]{1,0:T(8,128)(2,1)}, bf16[256,640]{1,0:T(8,128)(2,1)S(1)}, u32[]{:S(2)}, u32[]{:S(2)}) collective-permute-start(bf16[256,640]{1,0:T(8,128)(2,1)} %slice.110), channel_id=1, source_target_pairs={{0,1},{1,0},{2,3},{3,2},{4,5},{5,4},{6,7},{7,6},{8,9},{9,8},{10,11... | collective-permute-start | bytes 983048 | tf_op jit(solution)/shard_map/ppermute | solution.py:89
  8.3 11.2 %collective-permute-start.1 = (f32[2,12,8]{1,2,0:T(8,128)S(1)}, f32[2,12,8]{1,2,0:T(8,128)S(1)}, u32[]{:S(2)}, u32[]{:S(2)}) collective-permute-start(f32[2,12,8]{1,2,0:T(8,128)S(1)} %pad_maximum_fusion.12), channel_id=1, source_target_pairs={{0,2},{1,3},{2,0},{3,1},{4,6},{5,7},{6,4},{7,5},{8,10},{9,11},{10,... | collective-permute-start | bytes 2312 | tf_op jit(solution)/shard_map/ppermute | solution.py:89
  11.9 17.9 %collective-permute-start.3 = (bf16[512,640]{1,0:T(8,128)(2,1)}, bf16[512,640]{1,0:T(8,128)(2,1)}, u32[]{:S(2)}, u32[]{:S(2)}) collective-permute-start(bf16[512,640]{1,0:T(8,128)(2,1)} %pad_maximum_fusion.3.refs_0_), channel_id=1, source_target_pairs={{0,2},{1,3},{2,0},{3,1},{4,6},{5,7},{6,4},{7,5},{8,10},{9,11},{10,... | collective-permute-start | bytes 1966088 | tf_op jit(solution)/shard_map/ppermute | solution.py:89
  14.3 5.3 %copy-start.3 = (bf16[512,256]{1,0:T(8,128)(2,1)}, bf16[512,256]{1,0:T(8,128)(2,1)S(1)}, u32[]{:S(2)}) copy-start(bf16[512,256]{1,0:T(8,128)(2,1)S(1)} %pad_maximum_fusion.9.refs_0_) | copy-start | bytes 786436
  14.3 21.1 %collective-permute-start.16 = (bf16[512,256]{1,0:T(8,128)(2,1)S(1)}, bf16[512,256]{1,0:T(8,128)(2,1)}, u32[]{:S(2)}, u32[]{:S(2)}) collective-permute-start(bf16[512,256]{1,0:T(8,128)(2,1)S(1)} %pad_maximum_fusion.9.refs_0_), channel_id=1, source_target_pairs={{0,2},{1,3},{2,0},{3,1},{4,6},{5,7},{6,4},{7,5},{8,10},{9,11},{10,... | collective-permute-start | bytes 786440 | tf_op jit(solution)/shard_map/ppermute | solution.py:89
  15.0 20.4 %collective-permute-start.17 = (bf16[512,256]{1,0:T(8,128)(2,1)S(1)}, bf16[512,256]{1,0:T(8,128)(2,1)S(1)}, u32[]{:S(2)}, u32[]{:S(2)}) collective-permute-start(bf16[512,256]{1,0:T(8,128)(2,1)S(1)} %pad_maximum_fusion.9.refs_0_), channel_id=1, source_target_pairs={{2,4},{3,5},{4,2},{5,3},{0,1},{1,0},{6,7},{7,6},{10,12},{11,13},{1... | collective-permute-start | bytes 786440 | tf_op jit(solution)/shard_map/ppermute | solution.py:89
  15.1 4.7 %copy-start.4 = (bf16[512,256]{1,0:T(8,128)(2,1)}, bf16[512,256]{1,0:T(8,128)(2,1)S(1)}, u32[]{:S(2)}) copy-start(bf16[512,256]{1,0:T(8,128)(2,1)S(1)} %pad_maximum_fusion.10.refs_4_) | copy-start | bytes 786436
  15.1 25.9 %collective-permute-start.19 = (bf16[512,256]{1,0:T(8,128)(2,1)S(1)}, bf16[512,256]{1,0:T(8,128)(2,1)S(1)}, u32[]{:S(2)}, u32[]{:S(2)}) collective-permute-start(bf16[512,256]{1,0:T(8,128)(2,1)S(1)} %pad_maximum_fusion.10.refs_4_), channel_id=1, source_target_pairs={{0,2},{1,3},{2,0},{3,1},{4,6},{5,7},{6,4},{7,5},{8,10},{9,11},{10,... | collective-permute-start | bytes 786440 | tf_op jit(solution)/shard_map/ppermute | solution.py:89
  19.6 31.8 %collective-permute-start.4 = (bf16[512,640]{1,0:T(8,128)(2,1)}, bf16[512,640]{1,0:T(8,128)(2,1)}, u32[]{:S(2)}, u32[]{:S(2)}) collective-permute-start(bf16[512,640]{1,0:T(8,128)(2,1)} %pad_maximum_fusion.3.refs_0_), channel_id=1, source_target_pairs={{2,4},{3,5},{4,2},{5,3},{0,1},{1,0},{6,7},{7,6},{10,12},{11,13},{1... | collective-permute-start | bytes 1966088 | tf_op jit(solution)/shard_map/ppermute | solution.py:89
  19.7 48.0 %copy-start = (bf16[512,640]{1,0:T(8,128)(2,1)}, bf16[512,640]{1,0:T(8,128)(2,1)S(1)}, u32[]{:S(2)}) copy-start(bf16[512,640]{1,0:T(8,128)(2,1)S(1)} %pad_maximum_fusion.5.refs_0_) | copy-start | bytes 1966084
  29.8 42.6 %collective-permute-start.10 = (bf16[512,640]{1,0:T(8,128)(2,1)S(1)}, bf16[512,640]{1,0:T(8,128)(2,1)}, u32[]{:S(2)}, u32[]{:S(2)}) collective-permute-start(bf16[512,640]{1,0:T(8,128)(2,1)S(1)} %pad_maximum_fusion.5.refs_0_), channel_id=1, source_target_pairs={{0,2},{1,3},{2,0},{3,1},{4,6},{5,7},{6,4},{7,5},{8,10},{9,11},{10,... | collective-permute-start | bytes 1966088 | tf_op jit(solution)/shard_map/ppermute | solution.py:89
  31.2 36.5 %copy-start.1 = (bf16[512,640]{1,0:T(8,128)(2,1)}, bf16[512,640]{1,0:T(8,128)(2,1)S(1)}, u32[]{:S(2)}) copy-start(bf16[512,640]{1,0:T(8,128)(2,1)S(1)} %pad_maximum_fusion.4.refs_4_) | copy-start | bytes 1966084
  35.4 37.2 %collective-permute-start.5 = (bf16[512,640]{1,0:T(8,128)(2,1)}, bf16[512,640]{1,0:T(8,128)(2,1)}, u32[]{:S(2)}, u32[]{:S(2)}) collective-permute-start(bf16[512,640]{1,0:T(8,128)(2,1)} %collective-permute-done.3.refs_1_), channel_id=1, source_target_pairs={{2,4},{3,5},{4,2},{5,3},{0,1},{1,0},{6,7},{7,6},{10,12},{11,13},{1... | collective-permute-start | bytes 1966088 | tf_op jit(solution)/shard_map/ppermute | solution.py:89
  35.4 5.6 %copy-start.6 = (bf16[512,256]{1,0:T(8,128)(2,1)}, bf16[512,256]{1,0:T(8,128)(2,1)S(1)}, u32[]{:S(2)}) copy-start(bf16[512,256]{1,0:T(8,128)(2,1)S(1)} %collective-permute-done.17.refs_2_) | copy-start | bytes 786436
  35.4 37.7 %collective-permute-start.7 = (bf16[512,640]{1,0:T(8,128)(2,1)S(1)}, bf16[512,640]{1,0:T(8,128)(2,1)}, u32[]{:S(2)}, u32[]{:S(2)}) collective-permute-start(bf16[512,640]{1,0:T(8,128)(2,1)S(1)} %pad_maximum_fusion.4.refs_4_), channel_id=1, source_target_pairs={{0,2},{1,3},{2,0},{3,1},{4,6},{5,7},{6,4},{7,5},{8,10},{9,11},{10,... | collective-permute-start | bytes 1966088 | tf_op jit(solution)/shard_map/ppermute | solution.py:89
  40.9 0.7 copy-start.7
  40.9 2.2 %collective-permute-start.18 = (bf16[512,256]{1,0:T(8,128)(2,1)}, bf16[512,256]{1,0:T(8,128)(2,1)S(1)}, u32[]{:S(2)}, u32[]{:S(2)}) collective-permute-start(bf16[512,256]{1,0:T(8,128)(2,1)} %collective-permute-done.16.refs_1_), channel_id=1, source_target_pairs={{2,4},{3,5},{4,2},{5,3},{0,1},{1,0},{6,7},{7,6},{10,12},{11,13},{1... | collective-permute-start | bytes 786440 | tf_op jit(solution)/shard_map/ppermute | solution.py:89
  43.1 0.7 copy-start.8
  50.3 22.4 %copy-start.10 = (bf16[128,256]{1,0:T(8,128)(2,1)S(1)}, bf16[128,256]{1,0:T(8,128)(2,1)}, u32[]{:S(2)}) copy-start(bf16[128,256]{1,0:T(8,128)(2,1)} %get-tuple-element.21) | copy-start | bytes 196612
  50.3 22.9 %copy-start.9 = (bf16[128,256]{1,0:T(8,128)(2,1)S(1)}, bf16[128,256]{1,0:T(8,128)(2,1)}, u32[]{:S(2)}) copy-start(bf16[128,256]{1,0:T(8,128)(2,1)} %get-tuple-element.22) | copy-start | bytes 196612
  50.3 17.4 %collective-permute-start.26 = (bf16[128,256]{1,0:T(8,128)(2,1)}, bf16[128,256]{1,0:T(8,128)(2,1)S(1)}, u32[]{:S(2)}, u32[]{:S(2)}) collective-permute-start(bf16[128,256]{1,0:T(8,128)(2,1)} %get-tuple-element.27), channel_id=1, source_target_pairs={{0,9},{1,8},{2,11},{3,10},{4,13},{5,12},{6,15},{7,14},{8,17},{9,16... | collective-permute-start | bytes 196616 | tf_op jit(solution)/shard_map/ppermute | solution.py:150
  51.3 19.5 %collective-permute-start.27 = (bf16[128,256]{1,0:T(8,128)(2,1)}, bf16[128,256]{1,0:T(8,128)(2,1)S(1)}, u32[]{:S(2)}, u32[]{:S(2)}) collective-permute-start(bf16[128,256]{1,0:T(8,128)(2,1)} %get-tuple-element.28), channel_id=1, source_target_pairs={{0,11},{1,10},{2,9},{3,8},{4,15},{5,14},{6,13},{7,12},{8,19},{9,18... | collective-permute-start | bytes 196616 | tf_op jit(solution)/shard_map/ppermute | solution.py:150
  67.7 22.0 %copy-start.2 = (bf16[512,640]{1,0:T(8,128)(2,1)}, bf16[512,640]{1,0:T(8,128)(2,1)S(1)}, u32[]{:S(2)}) copy-start(bf16[512,640]{1,0:T(8,128)(2,1)S(1)} %pad_maximum_fusion.6.refs_4_) | copy-start | bytes 1966084
  67.7 34.4 %collective-permute-start.11 = (bf16[512,640]{1,0:T(8,128)(2,1)S(1)}, bf16[512,640]{1,0:T(8,128)(2,1)}, u32[]{:S(2)}, u32[]{:S(2)}) collective-permute-start(bf16[512,640]{1,0:T(8,128)(2,1)S(1)} %pad_maximum_fusion.5.refs_0_), channel_id=1, source_target_pairs={{2,4},{3,5},{4,2},{5,3},{0,1},{1,0},{6,7},{7,6},{10,12},{11,13},{1... | collective-permute-start | bytes 1966088 | tf_op jit(solution)/shard_map/ppermute | solution.py:89
  70.9 31.3 %collective-permute-start.13 = (bf16[512,640]{1,0:T(8,128)(2,1)S(1)}, bf16[512,640]{1,0:T(8,128)(2,1)}, u32[]{:S(2)}, u32[]{:S(2)}) collective-permute-start(bf16[512,640]{1,0:T(8,128)(2,1)S(1)} %pad_maximum_fusion.6.refs_4_), channel_id=1, source_target_pairs={{0,2},{1,3},{2,0},{3,1},{4,6},{5,7},{6,4},{7,5},{8,10},{9,11},{10,... | collective-permute-start | bytes 1966088 | tf_op jit(solution)/shard_map/ppermute | solution.py:89
  72.4 29.7 %collective-permute-start.12 = (bf16[512,640]{1,0:T(8,128)(2,1)}, bf16[512,640]{1,0:T(8,128)(2,1)}, u32[]{:S(2)}, u32[]{:S(2)}) collective-permute-start(bf16[512,640]{1,0:T(8,128)(2,1)} %collective-permute-done.10.refs_1_), channel_id=1, source_target_pairs={{2,4},{3,5},{4,2},{5,3},{0,1},{1,0},{6,7},{7,6},{10,12},{11,13},{1... | collective-permute-start | bytes 1966088 | tf_op jit(solution)/shard_map/ppermute | solution.py:89
  72.6 17.0 %collective-permute-start.20 = (bf16[128,256]{1,0:T(8,128)(2,1)S(1)}, bf16[128,256]{1,0:T(8,128)(2,1)S(1)}, u32[]{:S(2)}, u32[]{:S(2)}) collective-permute-start(bf16[128,256]{1,0:T(8,128)(2,1)S(1)} %copy-done.10), channel_id=1, source_target_pairs={{0,8},{1,9},{2,10},{3,11},{4,12},{5,13},{6,14},{7,15},{8,16},{9,17... | collective-permute-start | bytes 196616 | tf_op jit(solution)/shard_map/ppermute | solution.py:150
  73.2 16.5 %collective-permute-start.21 = (bf16[128,256]{1,0:T(8,128)(2,1)S(1)}, bf16[128,256]{1,0:T(8,128)(2,1)S(1)}, u32[]{:S(2)}, u32[]{:S(2)}) collective-permute-start(bf16[128,256]{1,0:T(8,128)(2,1)S(1)} %copy-done.9), channel_id=1, source_target_pairs={{0,10},{1,11},{2,8},{3,9},{4,14},{5,15},{6,12},{7,13},{8,18},{9,19... | collective-permute-start | bytes 196616 | tf_op jit(solution)/shard_map/ppermute | solution.py:150
  89.6 10.6 %collective-permute-start.22 = (bf16[128,640]{1,0:T(8,128)(2,1)}, bf16[128,640]{1,0:T(8,128)(2,1)S(1)}, u32[]{:S(2)}, u32[]{:S(2)}) collective-permute-start(bf16[128,640]{1,0:T(8,128)(2,1)} %get-tuple-element.23), channel_id=1, source_target_pairs={{0,9},{1,8},{2,11},{3,10},{4,13},{5,12},{6,15},{7,14},{8,17},{9,16... | collective-permute-start | bytes 491528 | tf_op jit(solution)/shard_map/ppermute | solution.py:150
  89.7 10.7 %collective-permute-start.23 = (bf16[128,640]{1,0:T(8,128)(2,1)}, bf16[128,640]{1,0:T(8,128)(2,1)S(1)}, u32[]{:S(2)}, u32[]{:S(2)}) collective-permute-start(bf16[128,640]{1,0:T(8,128)(2,1)} %get-tuple-element.24), channel_id=1, source_target_pairs={{0,11},{1,10},{2,9},{3,8},{4,15},{5,14},{6,13},{7,12},{8,19},{9,18... | collective-permute-start | bytes 491528 | tf_op jit(solution)/shard_map/ppermute | solution.py:150
  100.2 18.1 %collective-permute-start.8 = (bf16[128,640]{1,0:T(8,128)(2,1)}, bf16[128,640]{1,0:T(8,128)(2,1)S(1)}, u32[]{:S(2)}, u32[]{:S(2)}) collective-permute-start(bf16[128,640]{1,0:T(8,128)(2,1)} %get-tuple-element.17), channel_id=1, source_target_pairs={{0,8},{1,9},{2,10},{3,11},{4,12},{5,13},{6,14},{7,15},{8,16},{9,17... | collective-permute-start | bytes 491528 | tf_op jit(solution)/shard_map/ppermute | solution.py:150
  100.5 17.8 %collective-permute-start.9 = (bf16[128,640]{1,0:T(8,128)(2,1)}, bf16[128,640]{1,0:T(8,128)(2,1)S(1)}, u32[]{:S(2)}, u32[]{:S(2)}) collective-permute-start(bf16[128,640]{1,0:T(8,128)(2,1)} %get-tuple-element.18), channel_id=1, source_target_pairs={{0,10},{1,11},{2,8},{3,9},{4,14},{5,15},{6,12},{7,13},{8,18},{9,19... | collective-permute-start | bytes 491528 | tf_op jit(solution)/shard_map/ppermute | solution.py:150
  114.6 14.6 %collective-permute-start.24 = (bf16[128,640]{1,0:T(8,128)(2,1)}, bf16[128,640]{1,0:T(8,128)(2,1)S(1)}, u32[]{:S(2)}, u32[]{:S(2)}) collective-permute-start(bf16[128,640]{1,0:T(8,128)(2,1)} %get-tuple-element.25), channel_id=1, source_target_pairs={{0,9},{1,8},{2,11},{3,10},{4,13},{5,12},{6,15},{7,14},{8,17},{9,16... | collective-permute-start | bytes 491528 | tf_op jit(solution)/shard_map/ppermute | solution.py:150
  114.6 14.6 %collective-permute-start.25 = (bf16[128,640]{1,0:T(8,128)(2,1)}, bf16[128,640]{1,0:T(8,128)(2,1)S(1)}, u32[]{:S(2)}, u32[]{:S(2)}) collective-permute-start(bf16[128,640]{1,0:T(8,128)(2,1)} %get-tuple-element.26), channel_id=1, source_target_pairs={{0,11},{1,10},{2,9},{3,8},{4,15},{5,14},{6,13},{7,12},{8,19},{9,18... | collective-permute-start | bytes 491528 | tf_op jit(solution)/shard_map/ppermute | solution.py:150
  118.3 13.8 %collective-permute-start.14 = (bf16[128,640]{1,0:T(8,128)(2,1)}, bf16[128,640]{1,0:T(8,128)(2,1)S(1)}, u32[]{:S(2)}, u32[]{:S(2)}) collective-permute-start(bf16[128,640]{1,0:T(8,128)(2,1)} %get-tuple-element.19), channel_id=1, source_target_pairs={{0,8},{1,9},{2,10},{3,11},{4,12},{5,13},{6,14},{7,15},{8,16},{9,17... | collective-permute-start | bytes 491528 | tf_op jit(solution)/shard_map/ppermute | solution.py:150
  118.6 13.5 %collective-permute-start.15 = (bf16[128,640]{1,0:T(8,128)(2,1)}, bf16[128,640]{1,0:T(8,128)(2,1)S(1)}, u32[]{:S(2)}, u32[]{:S(2)}) collective-permute-start(bf16[128,640]{1,0:T(8,128)(2,1)} %get-tuple-element.20), channel_id=1, source_target_pairs={{0,10},{1,11},{2,8},{3,9},{4,14},{5,15},{6,12},{7,13},{8,18},{9,19... | collective-permute-start | bytes 491528 | tf_op jit(solution)/shard_map/ppermute | solution.py:150

commit v3 on v2

--- a/solution.py
+++ b/solution.py
@@ -11,7 +11,9 @@
 HEADS = 24
 HEAD_DIM = 128
 K_LIST = 5
-GROUPS = (5, 5, 2)
+GROUPS = (6, 4, 2)
+BLOCKS = (3, 4, 2)
+COST = 96
 SCALE = math.log2(math.e) / math.sqrt(HEAD_DIM)
 MASKED = -1e30
 
@@ -20,35 +22,45 @@
     return lax.dot_general(a, b, (((1,), (1,)), ((), ())), preferred_element_type=jnp.float32)
 
 
-def attend(query, key_tiles, value_tiles, mults):
-    scores = [
-        dot_nt(query, key) * SCALE + jnp.where(mult > 0, 0.0, MASKED)
-        for key, mult in zip(key_tiles, mults)
-    ]
-    top = jnp.max(functools.reduce(jnp.maximum, scores), axis=-1, keepdims=True)
-    weights = [jnp.exp2(one - top) * mult for one, mult in zip(scores, mults)]
-    total = jnp.sum(functools.reduce(jnp.add, weights), axis=-1, keepdims=True)
-    rounded = jnp.concatenate([one.astype(jnp.bfloat16) for one in weights], axis=1)
-    value = jnp.concatenate(value_tiles, axis=0)
-    return jnp.dot(rounded, value, preferred_element_type=jnp.float32) / total
+def attend(query, key, value, mults):
+    scores = dot_nt(query, key)
+    rows = query.shape[0] // len(mults)
+    span = key.shape[0] // len(mults[0])
+    rounded, totals = [], []
+    for t, counted in enumerate(mults):
+        parts = [
+            scores[t * rows : (t + 1) * rows, j * span : (j + 1) * span] * SCALE
+            + jnp.where(mult > 0, 0.0, MASKED)
+            for j, mult in enumerate(counted)
+        ]
+        top = jnp.max(functools.reduce(jnp.maximum, parts), axis=-1, keepdims=True)
+        weights = [jnp.exp2(part - top) * mult for part, mult in zip(parts, counted)]
+        totals.append(jnp.sum(functools.reduce(jnp.add, weights), axis=-1, keepdims=True))
+        rounded.append(jnp.concatenate([one.astype(jnp.bfloat16) for one in weights], axis=1))
+    mixed = jnp.dot(jnp.concatenate(rounded, axis=0), value, preferred_element_type=jnp.float32)
+    return mixed / jnp.concatenate(totals, axis=0)
 
 
 def finish(residual, gate, attention):
     return (residual.astype(jnp.float32) + gate * attention).astype(jnp.bfloat16)
 
 
-def relay_kernel(first, heads, mult_ref, *refs):
-    pairs, rests, (g_ref,), outs = refs[:4], refs[4:6], refs[6:7], refs[7:]
-    head = first + pl.program_id(0)
-    rows = pairs[0].shape[0] // 4
-    tile = [slice(j * rows, (j + 1) * rows) for j in range(4)]
-    keys = [ref[tile[j], :] for ref in pairs for j in (0, 2)]
-    vals = [ref[tile[j], :] for ref in pairs for j in (1, 3)]
-    for t, o_ref in enumerate(outs):
-        rest, place = rests[t // 2], 2 * (t % 2)
-        mults = [mult_ref[(t * heads + head) * 8 + j] for j in range(8)]
-        mixed = attend(rest[tile[place], :], keys, vals, mults)
-        o_ref[...] = finish(rest[tile[place + 1], :], g_ref[...], mixed)
+def relay_kernel(first, heads, block, mult_ref, *refs):
+    pairs, rests, g_ref, outs = refs[:8], refs[8:12], refs[12], refs[13:]
+    rows = pairs[0].shape[0] // 2
+    for h in range(block):
+        head = first + pl.program_id(0) * block + h
+        cols = slice(h * HEAD_DIM, (h + 1) * HEAD_DIM)
+        mults = [[mult_ref[(t * heads + head) * 8 + j] for j in range(8)] for t in range(4)]
+        mixed = attend(
+            jnp.concatenate([ref[:rows, cols] for ref in rests], axis=0),
+            jnp.concatenate([ref[:rows, cols] for ref in pairs], axis=0),
+            jnp.concatenate([ref[rows:, cols] for ref in pairs], axis=0),
+            mults,
+        )
+        for t, (rest, o_ref) in enumerate(zip(rests, outs)):
+            part = mixed[t * rows : (t + 1) * rows]
+            o_ref[:, cols] = finish(rest[rows:, cols], g_ref[:, cols], part)
 
 
 def multiplicity(lists, valid, me, tiles):
@@ -75,8 +87,9 @@
     width = half * HEAD_DIM
 
     swap = [(i, i ^ 1) for i in range(8)]
-    inward = [(2 * z + c, 2 * (z ^ 1) + c) for z in range(4) for c in (0, 1)]
-    across = [(2, 4), (3, 5), (4, 2), (5, 3), (0, 1), (1, 0), (6, 7), (7, 6)]
+    idle = [(0, 1), (1, 0), (6, 7), (7, 6)]
+    inward, inward_x = ([(i, i ^ change) for i in range(8)] for change in (2, 3))
+    across, across_x = ([(i, (i ^ 6) ^ change) for i in (2, 3, 4, 5)] + idle for change in (0, 1))
 
     def onward(change):
         return [
@@ -85,72 +98,108 @@
             for i in range(tiles)
         ]
 
-    def ctx(block, route):
-        return lax.ppermute(block, "ctx", route)
+    def ctx(block, route, name):
+        with jax.named_scope(name):
+            return lax.ppermute(block, "ctx", route)
+
+    def after(block, *others):
+        return lax.optimization_barrier((block, *others))[0]
 
     def halves(block):
-        left, right = block[..., :width], block[..., width:]
+        left, right = jnp.split(block, 2, axis=-1)
         return jnp.where(core == 0, left, right), jnp.where(core == 0, right, left)
 
     edges = [0]
     for size in GROUPS:
         edges.append(edges[-1] + size)
     cut = [slice(a * HEAD_DIM, b * HEAD_DIM) for a, b in zip(edges, edges[1:])]
-    groups = range(len(GROUPS))
-
-    kv_mine, kv_theirs = halves(jnp.concatenate([keys[0], values[0]], axis=0))
-    qr_mine, qr_theirs = halves(jnp.concatenate([queries[0], residual[0]], axis=0))
-    first = ctx(kv_theirs[:, cut[0]], swap)
-    later = ctx(jnp.concatenate([kv_theirs[:, cut[0].stop :], qr_theirs], axis=1), swap)
-    kv_got = jnp.concatenate([first, later[:, : width - cut[0].stop]], axis=1)
-    qr_got = later[:, width - cut[0].stop :]
-    own = [jnp.concatenate([kv_mine[:, c], kv_got[:, c]], axis=0) for c in cut]
-    own_qr = [jnp.concatenate([qr_mine[:, c], qr_got[:, c]], axis=0) for c in cut]
-
-    end, end_qr, near, far = [], [], [], []
-    for g in groups:
-        near.append(ctx(own[g], across))
-        end.append(ctx(own[g], inward))
-        end_qr.append(ctx(own_qr[g], inward))
-        far.append(ctx(end[g], across))
-
+
+    def picked(cols):
+        pairs = []
+        for array in (keys[0], values[0]):
+            left, right = array[:, cols], array[:, width + cols.start : width + cols.stop]
+            pairs.append((jnp.where(core == 0, left, right), jnp.where(core == 0, right, left)))
+        return [jnp.concatenate(pair, axis=0) for pair in zip(*pairs)]
+
+    mine, theirs = picked(cut[0])
+    near0, near1 = ctx(mine, across, "near_a0"), ctx(theirs, across_x, "near_a1")
+    end0 = ctx(mine, inward, "end_a0")
+    sibling = ctx(theirs, swap, "swap_a")
     table = multiplicity(tile_lists[0, 0], counts[0, 0], me, tiles).reshape(2, half, tiles)
     table_mine = jnp.where(core == 0, table[0], table[1])
     table_theirs = jnp.where(core == 0, table[1], table[0])
-    table = jnp.stack([table_mine, ctx(table_theirs, swap)])
-    table = jnp.concatenate([table, ctx(table, inward)], axis=0)
+    tables = [table_mine, ctx(table_theirs, swap, "table_swap")]
+    tables += [ctx(table_mine, inward, "table_end0"), ctx(table_theirs, inward_x, "table_end1")]
+    end1 = ctx(after(theirs, *tables), inward_x, "end_a1")
+
+    kv_mine, kv_theirs = picked(slice(cut[0].stop, width))
+    qr_mine, qr_theirs = halves(jnp.concatenate([queries[0], residual[0]], axis=0))
+    got = ctx(after(jnp.concatenate([kv_theirs, qr_theirs], axis=1), sibling), swap, "swap_rest")
+    start = cut[0].stop
+    own = [
+        jnp.concatenate([part[:, c.start - start : c.stop - start] for part in (kv_mine, got)], axis=0)
+        for c in cut[1:]
+    ]
+    qr_got = got[:, width - start :]
+    own_qr = [jnp.concatenate([qr_mine[:, c], qr_got[:, c]], axis=0) for c in cut]
+
+    near_b = ctx(own[0], across, "near_b")
+    end_b = ctx(after(own[0], end0), inward, "end_b")
+    far0, far1 = ctx(end0, across, "far_a0"), ctx(end1, across, "far_a1")
+    qr_a = ctx(after(own_qr[0], end1), inward, "qr_a")
+    qr_b = ctx(after(own_qr[1], end_b), inward, "qr_b")
+    far_b = ctx(end_b, across, "far_b")
+    near_c = ctx(after(own[1], end_b), across, "near_c")
+    end_c = ctx(after(own[1], qr_a), inward, "end_c")
+    far_c = ctx(end_c, across, "far_c")
+    qr_c = ctx(after(own_qr[2], qr_b), inward, "qr_c")
+
     chips = jnp.stack([chip, chip ^ 1, 3 - chip, 3 - (chip ^ 1)])
     order = (2 * chips[:, None] + jnp.stack([core, 1 - core])[None, :]).reshape(1, 1, 8, 1)
+    table = jnp.stack(tables)
     table = jnp.sum(jnp.where(order == jnp.arange(tiles), table[:, :, None, :], 0.0), axis=-1)
     table = table.reshape(4 * half * tiles)
     gate_mine, _ = halves(gate)
 
-    block = pl.BlockSpec((4 * rows, HEAD_DIM), lambda h, m: (0, h))
-    line = pl.BlockSpec((1, HEAD_DIM), lambda h, m: (0, h))
-    one = pl.BlockSpec((rows, HEAD_DIM), lambda h, m: (0, h))
+    def twice(block):
+        return [(block, 0), (block, 1)]
+
+    whole = lambda *blocks: [(block, 0) for block in blocks]
+    pairs = [
+        whole(mine, sibling, end0, end1, near0, near1, far0, far1),
+        twice(own[0]) + twice(end_b) + twice(near_b) + twice(far_b),
+        twice(own[1]) + twice(end_c) + twice(near_c) + twice(far_c),
+    ]
+    rests = [twice(own_qr[g]) + twice(block) for g, block in enumerate((qr_a, qr_b, qr_c))]
     same, other = [], []
-    for g in groups:
-        size = GROUPS[g]
+    inner = (chip == 1) | (chip == 2)
+    for g, (size, block) in enumerate(zip(GROUPS, BLOCKS)):
+        cols = block * HEAD_DIM
+        inputs = pairs[g] + rests[g] + [(gate_mine[:, cut[g]], 0)]
+        heights = [2 * rows] * 12 + [1]
         results = pl.pallas_call(
-            functools.partial(relay_kernel, edges[g], half),
+            functools.partial(relay_kernel, edges[g], half, block),
             out_shape=[jax.ShapeDtypeStruct((rows, size * HEAD_DIM), jnp.bfloat16)] * 4,
             grid_spec=pltpu.PrefetchScalarGridSpec(
                 num_scalar_prefetch=1,
-                grid=(size,),
-                in_specs=[block] * 6 + [line],
-                out_specs=[one] * 4,
+                grid=(size // block,),
+                in_specs=[
+                    pl.BlockSpec((height, cols), lambda h, m, place=place: (place, h))
+                    for height, (_, place) in zip(heights, inputs)
+                ],
+                out_specs=[pl.BlockSpec((rows, cols), lambda h, m: (0, h))] * 4,
             ),
             cost_estimate=pl.CostEstimate(
-                flops=size * 16 * rows * 8 * rows * HEAD_DIM,
+                flops=size * COST * rows * 8 * rows * HEAD_DIM,
                 bytes_accessed=size * 28 * rows * HEAD_DIM * 2,
                 transcendentals=size * 4 * rows * 8 * rows,
             ),
-        )(table, own[g], end[g], near[g], far[g], own_qr[g], end_qr[g], gate_mine[:, cut[g]])
+        )(table, *(array for array, _ in inputs))
+        table = after(table, results[0])
         sent = [
             lax.ppermute(piece, ("pipe", "ctx"), onward(change))
             for piece, change in zip(results, (0, 1, 2, 3))
         ]
-        inner = (chip == 1) | (chip == 2)
         same.append(jnp.where(inner, sent[0], sent[2]))
         other.append(jnp.where(inner, sent[1], sent[3]))
     same, other = jnp.concatenate(same, axis=1), jnp.concatenate(other, axis=1)
@@ -172,7 +221,8 @@
     mults += [jnp.where(k < valid_ref[head], 1.0, 0.0) for k in range(K_LIST)]
     keys = [ref[...] for ref in near_k] + [ref[0, :, :HEAD_DIM] for ref in far]
     vals = [ref[...] for ref in near_v] + [ref[0, :, HEAD_DIM:] for ref in far]
-    o_ref[...] = finish(r_ref[...], g_ref[...], attend(q_ref[...], keys, vals, mults))
+    mixed = attend(q_ref[...], jnp.concatenate(keys, axis=0), jnp.concatenate(vals, axis=0), [mults])
+    o_ref[...] = finish(r_ref[...], g_ref[...], mixed)
 
 
 def listed_section(queries, keys, values, residual, gate, tile_lists, counts):

time: 134 us -> 121 us (0.903)
  Pallas kernels: 31.3 us -> 20.6 us
  starting transfers between devices: 46.1 us -> 38.2 us
  waiting for transfers between devices: 40.7 us -> 48.1 us
  local copies, waits for them, and re-layouts: 7.28 us -> 5.07 us
    ppermute x16 -> x20, waiting for transfers between devices: 16.7 us -> 33.7 us  [ctx(): return lax.ppermute(block, 'ctx', route)]
    ppermute x12, starting transfers between devices: 30.8 us -> 18.1 us  [relay_section(): lax.ppermute(piece, ('pipe', 'ctx'), onward(change))]
    pallas_call x3, Pallas kernels: 31.3 us -> 20.6 us  [relay_section(): pl.pallas_call(functools.partial(relay_kernel, edges[g], half, block), ou...]
    ppermute x12, waiting for transfers between devices: 24 us -> 14.5 us  [relay_section(): lax.ppermute(piece, ('pipe', 'ctx'), onward(change))]
    ppermute x16 -> x20, starting transfers between devices: 15.3 us -> 20.2 us  [ctx(): return lax.ppermute(block, 'ctx', route)]
    select_n x2, other arithmetic: 2.78 us -> 0.28 us  [halves(): jnp.where(core == 0, left, right)]
    slice x2 -> x3, local copies, waits for them, and re-layouts: 2.25 us -> 0.08 us  [relay_section(): qr_got[:, c]]
    select_n x0 -> x2, other arithmetic: none -> 1.71 us  [the longest x1 1.63 us: picked(): jnp.where(core == 0, left, right)]
  transfers between devices with their start and end apart: 28 -> 32, of which waited for: 7 -> 14; matrix products, arithmetic and copies ran while one was open for 8% -> 6% of each run, Pallas kernels for 24% -> 17%
where the time goes in v3:
time: 121 us; the launch traced here: 120 us
  waiting for transfers between devices  48.1 us (40%)
  starting transfers between devices  38.2 us (32%)
  Pallas kernels  20.6 us (17%)
  other arithmetic  8.14 us (7%)
  local copies, waits for them, and re-layouts  5.07 us (4%)
    ppermute x20, waiting for transfers between devices, ctx(): return lax.ppermute(block, 'ctx', route)  33.7 us
    pallas_call x3, Pallas kernels, relay_section(): pl.pallas_call(functools.partial(relay_kernel, edges[g], half, block), ou...  20.6 us
    ppermute x20, starting transfers between devices, ctx(): return lax.ppermute(block, 'ctx', route)  20.2 us
    ppermute x12, starting transfers between devices, relay_section(): lax.ppermute(piece, ('pipe', 'ctx'), onward(change))  18.1 us
    ppermute x12, waiting for transfers between devices, relay_section(): lax.ppermute(piece, ('pipe', 'ctx'), onward(change))  14.5 us
  transfers between devices with their start and end apart: 32, of which 14 were waited for; matrix products, arithmetic and copies ran while one was open for 6% of the time, Pallas kernels for 17%

profile of v3, /device:TPU:0, one launch (start us, length us, event | category | flops | bytes accessed | tf_op | source)
XLA Modules:
  0.0 120.5 jit_solution(15557059299665670247)
XLA Ops:
  0.0 1.6 %broadcast_select_fusion.4 = (bf16[128,768]{1,0:T(8,128)(2,1)S(1)}, bf16[128,768]{1,0:T(8,128)(2,1)S(1)}, bf16[128,768]{1,0:T(8,128)(2,1)S(1)}, bf16[128,768]{1,...) fusion(pred[]{:T(512)S(6)} %eq.27, ...), kind=kLoop, calls=%fused_computation.23 | loop fusion | flops 786432 | bytes 3145729 | tf_op jit(solution)/shard_map/jit(_where)/select_n | solution.py:121
  1.7 0.8 pad_maximum_fusion.6
  3.3 1.1 pad_maximum_fusion
  5.2 2.7 %collective-permute-start.2 = (f32[12,8]{0,1:T(8,128)S(1)}, f32[12,8]{0,1:T(8,128)S(1)}, u32[]{:S(2)}, u32[]{:S(2)}) collective-permute-start(f32[12,8]{0,1:T(8,128)S(1)} %get-tuple-element.66), channel_id=1, source_target_pairs={{0,3},{1,2},{2,1},{3,0},{4,7},{5,6},{6,5},{7,4},{8,11},{9,10},{10,... | collective-permute-start | bytes 1160 | tf_op jit(solution)/shard_map/table_end1/ppermute | solution.py:103
  8.2 0.8 pad_maximum_fusion.5.refs_0_
  9.0 1.7 %collective-permute-start.4 = (bf16[256,768]{1,0:T(8,128)(2,1)}, bf16[256,768]{1,0:T(8,128)(2,1)}, u32[]{:S(2)}, u32[]{:S(2)}) collective-permute-start(bf16[256,768]{1,0:T(8,128)(2,1)} %pad_maximum_fusion.5.refs_0_), channel_id=1, source_target_pairs={{0,2},{1,3},{2,0},{3,1},{4,6},{5,7},{6,4},{7,5},{8,10},{9,11},{10,... | collective-permute-start | bytes 1179656 | tf_op jit(solution)/shard_map/end_a0/ppermute | solution.py:103
  10.9 0.6 collective-permute-done.1
  12.1 2.4 %collective-permute-start.5 = (bf16[256,768]{1,0:T(8,128)(2,1)}, bf16[256,768]{1,0:T(8,128)(2,1)}, u32[]{:S(2)}, u32[]{:S(2)}) collective-permute-start(bf16[256,768]{1,0:T(8,128)(2,1)} %pad_maximum_fusion.6), channel_id=1, source_target_pairs={{0,3},{1,2},{2,1},{3,0},{4,7},{5,6},{6,5},{7,4},{8,11},{9,10},{10,... | collective-permute-start | bytes 1179656 | tf_op jit(solution)/shard_map/end_a1/ppermute | solution.py:103
  14.6 0.8 pad_maximum_fusion.3.refs_0_.refs_1_
  15.4 5.9 %collective-permute-done.4.refs_2_ = bf16[256,768]{1,0:T(8,128)(2,1)} collective-permute-done((bf16[256,768]{1,0:T(8,128)(2,1)}, bf16[256,768]{1,0:T(8,128)(2,1)}, u32[]{:S(2)}, u32[]{:S(2)}) %collective-permute-start.4) | collective-permute-done | bytes 393248 | tf_op jit(solution)/shard_map/end_a0/ppermute | solution.py:103
  21.3 1.7 %collective-permute-start.14 = (bf16[512,512]{1,0:T(8,128)(2,1)}, bf16[512,512]{1,0:T(8,128)(2,1)}, u32[]{:S(2)}, u32[]{:S(2)}) collective-permute-start(bf16[512,512]{1,0:T(8,128)(2,1)} %pad_maximum_fusion.3.refs_0_.refs_1_), channel_id=1, source_target_pairs={{0,2},{1,3},{2,0},{3,1},{4,6},{5,7},{6,4},{7,5},{8,10},{9,11},{10,... | collective-permute-start | bytes 1572872 | tf_op jit(solution)/shard_map/end_b/ppermute | solution.py:103
  23.1 0.6 slice.110.refs_12_
  23.7 0.6 slice.116.refs_12_
  24.3 0.6 slice.120.refs_12_
  25.1 3.8 %collective-permute-done.5.refs_3_ = bf16[256,768]{1,0:T(8,128)(2,1)} collective-permute-done((bf16[256,768]{1,0:T(8,128)(2,1)}, bf16[256,768]{1,0:T(8,128)(2,1)}, u32[]{:S(2)}, u32[]{:S(2)}) %collective-permute-start.5) | collective-permute-done | bytes 393248 | tf_op jit(solution)/shard_map/end_a1/ppermute | solution.py:103
  29.0 0.7 collective-permute-start.11
  29.8 1.6 %collective-permute-start.8 = (bf16[256,768]{1,0:T(8,128)(2,1)}, bf16[256,768]{1,0:T(8,128)(2,1)}, u32[]{:S(2)}, u32[]{:S(2)}) collective-permute-start(bf16[256,768]{1,0:T(8,128)(2,1)} %collective-permute-done.4.refs_2_), channel_id=1, source_target_pairs={{2,4},{3,5},{4,2},{5,3},{0,1},{1,0},{6,7},{7,6},{10,12},{11,13},{1... | collective-permute-start | bytes 1179656 | tf_op jit(solution)/shard_map/far_a0/ppermute | solution.py:103
  31.4 9.5 %collective-permute-done.14.refs_2_.refs_3_ = bf16[512,512]{1,0:T(8,128)(2,1)} collective-permute-done((bf16[512,512]{1,0:T(8,128)(2,1)}, bf16[512,512]{1,0:T(8,128)(2,1)}, u32[]{:S(2)}, u32[]{:S(2)}) %collective-permute-start.14) | collective-permute-done | bytes 524320 | tf_op jit(solution)/shard_map/end_b/ppermute | solution.py:103
  41.2 0.7 reshape.114.mult_ref
  41.8 0.8 pad_maximum_fusion.4.refs_8_.refs_9_
  42.7 0.6 collective-permute-start.15
  43.3 3.3 %collective-permute-start.17 = (bf16[512,512]{1,0:T(8,128)(2,1)}, bf16[512,512]{1,0:T(8,128)(2,1)S(1)}, u32[]{:S(2)}, u32[]{:S(2)}) collective-permute-start(bf16[512,512]{1,0:T(8,128)(2,1)} %pad_maximum_fusion.4.refs_8_.refs_9_), channel_id=1, source_target_pairs={{0,2},{1,3},{2,0},{3,1},{4,6},{5,7},{6,4},{7,5},{8,10},{9,11},{10,... | collective-permute-start | bytes 1572872 | tf_op jit(solution)/shard_map/qr_b/ppermute | solution.py:103
  46.6 11.2 %collective-permute-done.11.refs_10_.refs_11_ = bf16[512,768]{1,0:T(8,128)(2,1)} collective-permute-done((bf16[512,768]{1,0:T(8,128)(2,1)S(1)}, bf16[512,768]{1,0:T(8,128)(2,1)}, u32[]{:S(2)}, u32[]{:S(2)}) %collective-permute-start.11) | collective-permute-done | bytes 786464 | tf_op jit(solution)/shard_map/qr_a/ppermute | solution.py:103
  57.8 8.9 %shard_map.73 = (bf16[128,768]{1,0:T(8,128)(2,1)}, bf16[128,768]{1,0:T(8,128)(2,1)}, bf16[128,768]{1,0:T(8,128)(2,1)}, bf16[128,768]{1,0:T(8,128)(2,1)}) custom-call(f32[384]{0:T(512)} %reshape.114.mult_ref, bf16[256,768]{1,0:T(8,128)(2,1)} %pad_maximum_fusion.5.refs_0_, bf16[256,768]{1,0:T(8,128)(2,1)} %collective-permute-done.3.refs_1_, ...), custom_call_target="tpu_custom_call" | custom-call | flops 9663676416 | bytes 5505024 | tf_op jit(solution)/shard_map/pallas_call | solution.py:180
  66.7 1.7 %collective-permute-start.12 = (bf16[128,768]{1,0:T(8,128)(2,1)}, bf16[128,768]{1,0:T(8,128)(2,1)S(1)}, u32[]{:S(2)}, u32[]{:S(2)}) collective-permute-start(bf16[128,768]{1,0:T(8,128)(2,1)} %get-tuple-element.30), channel_id=1, source_target_pairs={{0,8},{1,9},{2,10},{3,11},{4,12},{5,13},{6,14},{7,15},{8,16},{9,17... | collective-permute-start | bytes 589832 | tf_op jit(solution)/shard_map/ppermute | solution.py:200
  68.4 2.5 %collective-permute-start.13 = (bf16[128,768]{1,0:T(8,128)(2,1)}, bf16[128,768]{1,0:T(8,128)(2,1)S(1)}, u32[]{:S(2)}, u32[]{:S(2)}) collective-permute-start(bf16[128,768]{1,0:T(8,128)(2,1)} %get-tuple-element.31), channel_id=1, source_target_pairs={{0,10},{1,11},{2,8},{3,9},{4,14},{5,15},{6,12},{7,13},{8,18},{9,19... | collective-permute-start | bytes 589832 | tf_op jit(solution)/shard_map/ppermute | solution.py:200
  71.0 6.4 %collective-permute-done.12 = bf16[128,768]{1,0:T(8,128)(2,1)S(1)} collective-permute-done((bf16[128,768]{1,0:T(8,128)(2,1)}, bf16[128,768]{1,0:T(8,128)(2,1)S(1)}, u32[]{:S(2)}, u32[]{:S(2)}) %collective-permute-start.12) | collective-permute-done | bytes 196640 | tf_op jit(solution)/shard_map/ppermute | solution.py:200
  77.4 3.2 %collective-permute-start.20 = (bf16[512,256]{1,0:T(8,128)(2,1)S(1)}, bf16[512,256]{1,0:T(8,128)(2,1)}, u32[]{:S(2)}, u32[]{:S(2)}) collective-permute-start(bf16[512,256]{1,0:T(8,128)(2,1)S(1)} %fusion.2.refs_0_.refs_1_), channel_id=1, source_target_pairs={{0,2},{1,3},{2,0},{3,1},{4,6},{5,7},{6,4},{7,5},{8,10},{9,11},{10,... | collective-permute-start | bytes 786440 | tf_op jit(solution)/shard_map/end_c/ppermute | solution.py:103
  80.7 2.1 %collective-permute-start.27 = (bf16[128,768]{1,0:T(8,128)(2,1)}, bf16[128,768]{1,0:T(8,128)(2,1)S(1)}, u32[]{:S(2)}, u32[]{:S(2)}) collective-permute-start(bf16[128,768]{1,0:T(8,128)(2,1)} %get-tuple-element.44), channel_id=1, source_target_pairs={{0,11},{1,10},{2,9},{3,8},{4,15},{5,14},{6,13},{7,12},{8,19},{9,18... | collective-permute-start | bytes 589832 | tf_op jit(solution)/shard_map/ppermute | solution.py:200
  82.9 0.8 copy-done.9
  83.7 6.8 %shard_map.74 = (bf16[128,512]{1,0:T(8,128)(2,1)}, bf16[128,512]{1,0:T(8,128)(2,1)}, bf16[128,512]{1,0:T(8,128)(2,1)}, bf16[128,512]{1,0:T(8,128)(2,1)}) custom-call(f32[384]{0:T(512)} %reshape.114.mult_ref, bf16[512,512]{1,0:T(8,128)(2,1)} %pad_maximum_fusion.3.refs_0_.refs_1_, bf16[512,512]{1,0:T(8,128)(2,1)} %pad_maximum_fusion.3.refs_0_.refs_1_, ...), custom_call_target="tpu_custom_call" | custom-call | flops 6442450944 | bytes 3670016 | tf_op jit(solution)/shard_map/pallas_call | solution.py:180
  90.4 0.6 collective-permute-start.18
  91.1 1.3 %collective-permute-done.26 = bf16[128,768]{1,0:T(8,128)(2,1)S(1)} collective-permute-done((bf16[128,768]{1,0:T(8,128)(2,1)}, bf16[128,768]{1,0:T(8,128)(2,1)S(1)}, u32[]{:S(2)}, u32[]{:S(2)}) %collective-permute-start.26) | collective-permute-done | bytes 196640 | tf_op jit(solution)/shard_map/ppermute | solution.py:200
  92.4 1.5 %collective-permute-start.19 = (bf16[128,512]{1,0:T(8,128)(2,1)}, bf16[128,512]{1,0:T(8,128)(2,1)S(1)}, u32[]{:S(2)}, u32[]{:S(2)}) collective-permute-start(bf16[128,512]{1,0:T(8,128)(2,1)} %get-tuple-element.36), channel_id=1, source_target_pairs={{0,10},{1,11},{2,8},{3,9},{4,14},{5,15},{6,12},{7,13},{8,18},{9,19... | collective-permute-start | bytes 393224 | tf_op jit(solution)/shard_map/ppermute | solution.py:200
  94.4 2.9 %collective-permute-done.18 = bf16[128,512]{1,0:T(8,128)(2,1)S(1)} collective-permute-done((bf16[128,512]{1,0:T(8,128)(2,1)}, bf16[128,512]{1,0:T(8,128)(2,1)S(1)}, u32[]{:S(2)}, u32[]{:S(2)}) %collective-permute-start.18) | collective-permute-done | bytes 131104 | tf_op jit(solution)/shard_map/ppermute | solution.py:200
  97.3 2.8 %collective-permute-start.28 = (bf16[128,512]{1,0:T(8,128)(2,1)}, bf16[128,512]{1,0:T(8,128)(2,1)S(1)}, u32[]{:S(2)}, u32[]{:S(2)}) collective-permute-start(bf16[128,512]{1,0:T(8,128)(2,1)} %get-tuple-element.45), channel_id=1, source_target_pairs={{0,9},{1,8},{2,11},{3,10},{4,13},{5,12},{6,15},{7,14},{8,17},{9,16... | collective-permute-start | bytes 393224 | tf_op jit(solution)/shard_map/ppermute | solution.py:200
  100.1 0.7 collective-permute-done.19
  100.8 1.1 collective-permute-start.29
  102.0 2.3 %collective-permute-done.23.refs_10_.refs_11_ = bf16[512,256]{1,0:T(8,128)(2,1)S(1)} collective-permute-done((bf16[512,256]{1,0:T(8,128)(2,1)S(1)}, bf16[512,256]{1,0:T(8,128)(2,1)S(1)}, u32[]{:S(2)}, u32[]{:S(2)}) %collective-permute-start.23) | collective-permute-done | bytes 262176 | tf_op jit(solution)/shard_map/qr_c/ppermute | solution.py:103
  104.3 0.7 copy-done.11
  105.0 0.7 copy-done.12
  105.7 4.9 %shard_map.75 = (bf16[128,256]{1,0:T(8,128)(2,1)}, bf16[128,256]{1,0:T(8,128)(2,1)}, bf16[128,256]{1,0:T(8,128)(2,1)}, bf16[128,256]{1,0:T(8,128)(2,1)}) custom-call(f32[384]{0:T(512)} %reshape.114.mult_ref, bf16[512,256]{1,0:T(8,128)(2,1)} %copy-done.3, bf16[512,256]{1,0:T(8,128)(2,1)} %copy-done.3, ...), custom_call_target="tpu_custom_call" | custom-call | flops 3221225472 | bytes 1835008 | tf_op jit(solution)/shard_map/pallas_call | solution.py:180
  111.0 1.6 %collective-permute-start.25 = (bf16[128,256]{1,0:T(8,128)(2,1)}, bf16[128,256]{1,0:T(8,128)(2,1)S(1)}, u32[]{:S(2)}, u32[]{:S(2)}) collective-permute-start(bf16[128,256]{1,0:T(8,128)(2,1)} %get-tuple-element.42), channel_id=1, source_target_pairs={{0,10},{1,11},{2,8},{3,9},{4,14},{5,15},{6,12},{7,13},{8,18},{9,19... | collective-permute-start | bytes 196616 | tf_op jit(solution)/shard_map/ppermute | solution.py:200
  112.7 3.6 %collective-permute-start.31 = (bf16[128,256]{1,0:T(8,128)(2,1)}, bf16[128,256]{1,0:T(8,128)(2,1)S(1)}, u32[]{:S(2)}, u32[]{:S(2)}) collective-permute-start(bf16[128,256]{1,0:T(8,128)(2,1)} %get-tuple-element.48), channel_id=1, source_target_pairs={{0,11},{1,10},{2,9},{3,8},{4,15},{5,14},{6,13},{7,12},{8,19},{9,18... | collective-permute-start | bytes 196616 | tf_op jit(solution)/shard_map/ppermute | solution.py:200
  116.3 1.0 collective-permute-done.25
  117.4 0.9 collective-permute-done.30
  118.3 1.1 collective-permute-done.31
  119.5 1.0 maximum_bitcast_fusion
  (91 shorter events, 4.5 us)
Async XLA Ops:
  0.0 2.9 %copy-start.6 = (s32[1,1,24,5]{2,1,3,0:T(1,128)S(1)}, s32[1,1,24,5]{2,1,3,0:T(1,128)}, u32[]{:S(2)}) copy-start(s32[1,1,24,5]{2,1,3,0:T(1,128)} %param.12) | copy-start | bytes 1444
  0.0 2.9 %copy-start.13 = (s32[1,1,24]{2,1,0:T(1,128)S(1)}, s32[1,1,24]{2,1,0:T(1,128)}, u32[]{:S(2)}) copy-start(s32[1,1,24]{2,1,0:T(1,128)} %param.13) | copy-start | bytes 292
  0.0 2.9 %copy-start.2 = (bf16[1,128,3072]{2,1,0:T(8,128)(2,1)S(1)}, bf16[1,128,3072]{2,1,0:T(8,128)(2,1)}, u32[]{:S(2)}) copy-start(bf16[1,128,3072]{2,1,0:T(8,128)(2,1)} %param.7) | copy-start | bytes 2359300
  1.6 1.3 %copy-start.1 = (bf16[1,128,3072]{2,1,0:T(8,128)(2,1)S(1)}, bf16[1,128,3072]{2,1,0:T(8,128)(2,1)}, u32[]{:S(2)}) copy-start(bf16[1,128,3072]{2,1,0:T(8,128)(2,1)} %param.10) | copy-start | bytes 2359300
  2.4 2.2 %collective-permute-start.3 = (bf16[256,768]{1,0:T(8,128)(2,1)}, bf16[256,768]{1,0:T(8,128)(2,1)}, u32[]{:S(2)}, u32[]{:S(2)}) collective-permute-start(bf16[256,768]{1,0:T(8,128)(2,1)} %pad_maximum_fusion.6), channel_id=1, source_target_pairs={{0,1},{1,0},{2,3},{3,2},{4,5},{5,4},{6,7},{7,6},{8,9},{9,8},{10,11... | collective-permute-start | bytes 1179656 | tf_op jit(solution)/shard_map/swap_a/ppermute | solution.py:103
  4.4 6.4 %copy-start.5 = (f32[1,3072]{1,0:T(1,128)S(1)}, f32[1,3072]{1,0:T(1,128)}, u32[]{:S(2)}) copy-start(f32[1,3072]{1,0:T(1,128)} %param.11) | copy-start | bytes 36868
  4.6 9.9 %collective-permute-start.10 = (bf16[256,2304]{1,0:T(8,128)(2,1)}, bf16[256,2304]{1,0:T(8,128)(2,1)S(1)}, u32[]{:S(2)}, u32[]{:S(2)}) collective-permute-start(bf16[256,2304]{1,0:T(8,128)(2,1)} %pad_maximum_fusion), channel_id=1, source_target_pairs={{0,1},{1,0},{2,3},{3,2},{4,5},{5,4},{6,7},{7,6},{8,9},{9,8},{10,11... | collective-permute-start | bytes 3538952 | tf_op jit(solution)/shard_map/swap_rest/ppermute | solution.py:103
  5.1 6.5 %collective-permute-start = (f32[12,8]{0,1:T(8,128)S(1)}, f32[12,8]{0,1:T(8,128)S(1)}, u32[]{:S(2)}, u32[]{:S(2)}) collective-permute-start(f32[12,8]{0,1:T(8,128)S(1)} %get-tuple-element.66), channel_id=1, source_target_pairs={{0,1},{1,0},{2,3},{3,2},{4,5},{5,4},{6,7},{7,6},{8,9},{9,8},{10,11... | collective-permute-start | bytes 1160 | tf_op jit(solution)/shard_map/table_swap/ppermute | solution.py:103
  5.2 6.8 %collective-permute-start.2 = (f32[12,8]{0,1:T(8,128)S(1)}, f32[12,8]{0,1:T(8,128)S(1)}, u32[]{:S(2)}, u32[]{:S(2)}) collective-permute-start(f32[12,8]{0,1:T(8,128)S(1)} %get-tuple-element.66), channel_id=1, source_target_pairs={{0,3},{1,2},{2,1},{3,0},{4,7},{5,6},{6,5},{7,4},{8,11},{9,10},{10,... | collective-permute-start | bytes 1160 | tf_op jit(solution)/shard_map/table_end1/ppermute | solution.py:103
  7.9 3.6 %collective-permute-start.1 = (f32[12,8]{0,1:T(8,128)S(1)}, f32[12,8]{0,1:T(8,128)S(1)}, u32[]{:S(2)}, u32[]{:S(2)}) collective-permute-start(f32[12,8]{0,1:T(8,128)S(1)} %get-tuple-element.65), channel_id=1, source_target_pairs={{0,2},{1,3},{2,0},{3,1},{4,6},{5,7},{6,4},{7,5},{8,10},{9,11},{10,... | collective-permute-start | bytes 1160 | tf_op jit(solution)/shard_map/table_end0/ppermute | solution.py:103
  9.0 12.3 %collective-permute-start.4 = (bf16[256,768]{1,0:T(8,128)(2,1)}, bf16[256,768]{1,0:T(8,128)(2,1)}, u32[]{:S(2)}, u32[]{:S(2)}) collective-permute-start(bf16[256,768]{1,0:T(8,128)(2,1)} %pad_maximum_fusion.5.refs_0_), channel_id=1, source_target_pairs={{0,2},{1,3},{2,0},{3,1},{4,6},{5,7},{6,4},{7,5},{8,10},{9,11},{10,... | collective-permute-start | bytes 1179656 | tf_op jit(solution)/shard_map/end_a0/ppermute | solution.py:103
  11.6 31.1 %collective-permute-start.7 = (bf16[256,768]{1,0:T(8,128)(2,1)}, bf16[256,768]{1,0:T(8,128)(2,1)}, u32[]{:S(2)}, u32[]{:S(2)}) collective-permute-start(bf16[256,768]{1,0:T(8,128)(2,1)} %pad_maximum_fusion.6), channel_id=1, source_target_pairs={{2,5},{3,4},{4,3},{5,2},{0,1},{1,0},{6,7},{7,6},{10,13},{11,12},{1... | collective-permute-start | bytes 1179656 | tf_op jit(solution)/shard_map/near_a1/ppermute | solution.py:103
  11.6 31.7 %collective-permute-start.6 = (bf16[256,768]{1,0:T(8,128)(2,1)}, bf16[256,768]{1,0:T(8,128)(2,1)}, u32[]{:S(2)}, u32[]{:S(2)}) collective-permute-start(bf16[256,768]{1,0:T(8,128)(2,1)} %pad_maximum_fusion.5.refs_0_), channel_id=1, source_target_pairs={{2,4},{3,5},{4,2},{5,3},{0,1},{1,0},{6,7},{7,6},{10,12},{11,13},{1... | collective-permute-start | bytes 1179656 | tf_op jit(solution)/shard_map/near_a0/ppermute | solution.py:103
  12.1 16.9 %collective-permute-start.5 = (bf16[256,768]{1,0:T(8,128)(2,1)}, bf16[256,768]{1,0:T(8,128)(2,1)}, u32[]{:S(2)}, u32[]{:S(2)}) collective-permute-start(bf16[256,768]{1,0:T(8,128)(2,1)} %pad_maximum_fusion.6), channel_id=1, source_target_pairs={{0,3},{1,2},{2,1},{3,0},{4,7},{5,6},{6,5},{7,4},{8,11},{9,10},{10,... | collective-permute-start | bytes 1179656 | tf_op jit(solution)/shard_map/end_a1/ppermute | solution.py:103
  21.3 19.7 %collective-permute-start.14 = (bf16[512,512]{1,0:T(8,128)(2,1)}, bf16[512,512]{1,0:T(8,128)(2,1)}, u32[]{:S(2)}, u32[]{:S(2)}) collective-permute-start(bf16[512,512]{1,0:T(8,128)(2,1)} %pad_maximum_fusion.3.refs_0_.refs_1_), channel_id=1, source_target_pairs={{0,2},{1,3},{2,0},{3,1},{4,6},{5,7},{6,4},{7,5},{8,10},{9,11},{10,... | collective-permute-start | bytes 1572872 | tf_op jit(solution)/shard_map/end_b/ppermute | solution.py:103
  25.1 32.7 %copy-start = (bf16[512,768]{1,0:T(8,128)(2,1)}, bf16[512,768]{1,0:T(8,128)(2,1)S(1)}, u32[]{:S(2)}) copy-start(bf16[512,768]{1,0:T(8,128)(2,1)S(1)} %pad_maximum_fusion.2.refs_8_.refs_9_) | copy-start | bytes 2359300
  29.0 28.8 %collective-permute-start.11 = (bf16[512,768]{1,0:T(8,128)(2,1)S(1)}, bf16[512,768]{1,0:T(8,128)(2,1)}, u32[]{:S(2)}, u32[]{:S(2)}) collective-permute-start(bf16[512,768]{1,0:T(8,128)(2,1)S(1)} %pad_maximum_fusion.2.refs_8_.refs_9_), channel_id=1, source_target_pairs={{0,2},{1,3},{2,0},{3,1},{4,6},{5,7},{6,4},{7,5},{8,10},{9,11},{10,... | collective-permute-start | bytes 2359304 | tf_op jit(solution)/shard_map/qr_a/ppermute | solution.py:103
  29.8 16.8 %collective-permute-start.8 = (bf16[256,768]{1,0:T(8,128)(2,1)}, bf16[256,768]{1,0:T(8,128)(2,1)}, u32[]{:S(2)}, u32[]{:S(2)}) collective-permute-start(bf16[256,768]{1,0:T(8,128)(2,1)} %collective-permute-done.4.refs_2_), channel_id=1, source_target_pairs={{2,4},{3,5},{4,2},{5,3},{0,1},{1,0},{6,7},{7,6},{10,12},{11,13},{1... | collective-permute-start | bytes 1179656 | tf_op jit(solution)/shard_map/far_a0/ppermute | solution.py:103
  40.9 5.6 %collective-permute-start.9 = (bf16[256,768]{1,0:T(8,128)(2,1)}, bf16[256,768]{1,0:T(8,128)(2,1)}, u32[]{:S(2)}, u32[]{:S(2)}) collective-permute-start(bf16[256,768]{1,0:T(8,128)(2,1)} %collective-permute-done.5.refs_3_), channel_id=1, source_target_pairs={{2,4},{3,5},{4,2},{5,3},{0,1},{1,0},{6,7},{7,6},{10,12},{11,13},{1... | collective-permute-start | bytes 1179656 | tf_op jit(solution)/shard_map/far_a1/ppermute | solution.py:103
  42.7 37.9 %collective-permute-start.15 = (bf16[512,512]{1,0:T(8,128)(2,1)}, bf16[512,512]{1,0:T(8,128)(2,1)S(1)}, u32[]{:S(2)}, u32[]{:S(2)}) collective-permute-start(bf16[512,512]{1,0:T(8,128)(2,1)} %pad_maximum_fusion.3.refs_0_.refs_1_), channel_id=1, source_target_pairs={{2,4},{3,5},{4,2},{5,3},{0,1},{1,0},{6,7},{7,6},{10,12},{11,13},{1... | collective-permute-start | bytes 1572872 | tf_op jit(solution)/shard_map/near_b/ppermute | solution.py:103
  43.3 37.4 %collective-permute-start.17 = (bf16[512,512]{1,0:T(8,128)(2,1)}, bf16[512,512]{1,0:T(8,128)(2,1)S(1)}, u32[]{:S(2)}, u32[]{:S(2)}) collective-permute-start(bf16[512,512]{1,0:T(8,128)(2,1)} %pad_maximum_fusion.4.refs_8_.refs_9_), channel_id=1, source_target_pairs={{0,2},{1,3},{2,0},{3,1},{4,6},{5,7},{6,4},{7,5},{8,10},{9,11},{10,... | collective-permute-start | bytes 1572872 | tf_op jit(solution)/shard_map/qr_b/ppermute | solution.py:103
  46.6 36.3 %collective-permute-start.16 = (bf16[512,512]{1,0:T(8,128)(2,1)}, bf16[512,512]{1,0:T(8,128)(2,1)S(1)}, u32[]{:S(2)}, u32[]{:S(2)}) collective-permute-start(bf16[512,512]{1,0:T(8,128)(2,1)} %collective-permute-done.14.refs_2_.refs_3_), channel_id=1, source_target_pairs={{2,4},{3,5},{4,2},{5,3},{0,1},{1,0},{6,7},{7,6},{10,12},{11,13},{1... | collective-permute-start | bytes 1572872 | tf_op jit(solution)/shard_map/far_b/ppermute | solution.py:103
  66.7 10.7 %collective-permute-start.12 = (bf16[128,768]{1,0:T(8,128)(2,1)}, bf16[128,768]{1,0:T(8,128)(2,1)S(1)}, u32[]{:S(2)}, u32[]{:S(2)}) collective-permute-start(bf16[128,768]{1,0:T(8,128)(2,1)} %get-tuple-element.30), channel_id=1, source_target_pairs={{0,8},{1,9},{2,10},{3,11},{4,12},{5,13},{6,14},{7,15},{8,16},{9,17... | collective-permute-start | bytes 589832 | tf_op jit(solution)/shard_map/ppermute | solution.py:200
  68.4 9.0 %collective-permute-start.13 = (bf16[128,768]{1,0:T(8,128)(2,1)}, bf16[128,768]{1,0:T(8,128)(2,1)S(1)}, u32[]{:S(2)}, u32[]{:S(2)}) collective-permute-start(bf16[128,768]{1,0:T(8,128)(2,1)} %get-tuple-element.31), channel_id=1, source_target_pairs={{0,10},{1,11},{2,8},{3,9},{4,14},{5,15},{6,12},{7,13},{8,18},{9,19... | collective-permute-start | bytes 589832 | tf_op jit(solution)/shard_map/ppermute | solution.py:200
  70.9 19.5 %copy-start.3 = (bf16[512,256]{1,0:T(8,128)(2,1)}, bf16[512,256]{1,0:T(8,128)(2,1)S(1)}, u32[]{:S(2)}) copy-start(bf16[512,256]{1,0:T(8,128)(2,1)S(1)} %fusion.2.refs_0_.refs_1_) | copy-start | bytes 786436
  71.0 22.9 %copy-start.4 = (bf16[512,256]{1,0:T(8,128)(2,1)}, bf16[512,256]{1,0:T(8,128)(2,1)S(1)}, u32[]{:S(2)}) copy-start(bf16[512,256]{1,0:T(8,128)(2,1)S(1)} %pad_maximum_fusion.10.refs_8_.refs_9_) | copy-start | bytes 786436
  77.4 24.6 %collective-permute-start.21 = (bf16[512,256]{1,0:T(8,128)(2,1)S(1)}, bf16[512,256]{1,0:T(8,128)(2,1)S(1)}, u32[]{:S(2)}, u32[]{:S(2)}) collective-permute-start(bf16[512,256]{1,0:T(8,128)(2,1)S(1)} %fusion.2.refs_0_.refs_1_), channel_id=1, source_target_pairs={{2,4},{3,5},{4,2},{5,3},{0,1},{1,0},{6,7},{7,6},{10,12},{11,13},{1... | collective-permute-start | bytes 786440 | tf_op jit(solution)/shard_map/near_c/ppermute | solution.py:103
  77.4 16.9 %collective-permute-start.20 = (bf16[512,256]{1,0:T(8,128)(2,1)S(1)}, bf16[512,256]{1,0:T(8,128)(2,1)}, u32[]{:S(2)}, u32[]{:S(2)}) collective-permute-start(bf16[512,256]{1,0:T(8,128)(2,1)S(1)} %fusion.2.refs_0_.refs_1_), channel_id=1, source_target_pairs={{0,2},{1,3},{2,0},{3,1},{4,6},{5,7},{6,4},{7,5},{8,10},{9,11},{10,... | collective-permute-start | bytes 786440 | tf_op jit(solution)/shard_map/end_c/ppermute | solution.py:103
  80.6 2.2 %copy-start.7 = (bf16[512,512]{1,0:T(8,128)(2,1)}, bf16[512,512]{1,0:T(8,128)(2,1)S(1)}, u32[]{:S(2)}) copy-start(bf16[512,512]{1,0:T(8,128)(2,1)S(1)} %collective-permute-done.15.refs_4_.refs_5_) | copy-start | bytes 1572868
  80.6 11.8 %collective-permute-start.26 = (bf16[128,768]{1,0:T(8,128)(2,1)}, bf16[128,768]{1,0:T(8,128)(2,1)S(1)}, u32[]{:S(2)}, u32[]{:S(2)}) collective-permute-start(bf16[128,768]{1,0:T(8,128)(2,1)} %get-tuple-element.43), channel_id=1, source_target_pairs={{0,9},{1,8},{2,11},{3,10},{4,13},{5,12},{6,15},{7,14},{8,17},{9,16... | collective-permute-start | bytes 589832 | tf_op jit(solution)/shard_map/ppermute | solution.py:200
  80.7 2.1 %copy-start.8 = (bf16[512,512]{1,0:T(8,128)(2,1)}, bf16[512,512]{1,0:T(8,128)(2,1)S(1)}, u32[]{:S(2)}) copy-start(bf16[512,512]{1,0:T(8,128)(2,1)S(1)} %collective-permute-done.17.refs_10_.refs_11_) | copy-start | bytes 1572868
  80.7 13.2 %collective-permute-start.27 = (bf16[128,768]{1,0:T(8,128)(2,1)}, bf16[128,768]{1,0:T(8,128)(2,1)S(1)}, u32[]{:S(2)}, u32[]{:S(2)}) collective-permute-start(bf16[128,768]{1,0:T(8,128)(2,1)} %get-tuple-element.44), channel_id=1, source_target_pairs={{0,11},{1,10},{2,9},{3,8},{4,15},{5,14},{6,13},{7,12},{8,19},{9,18... | collective-permute-start | bytes 589832 | tf_op jit(solution)/shard_map/ppermute | solution.py:200
  82.8 0.8 copy-start.9
  90.4 6.9 %collective-permute-start.18 = (bf16[128,512]{1,0:T(8,128)(2,1)}, bf16[128,512]{1,0:T(8,128)(2,1)S(1)}, u32[]{:S(2)}, u32[]{:S(2)}) collective-permute-start(bf16[128,512]{1,0:T(8,128)(2,1)} %get-tuple-element.35), channel_id=1, source_target_pairs={{0,8},{1,9},{2,10},{3,11},{4,12},{5,13},{6,14},{7,15},{8,16},{9,17... | collective-permute-start | bytes 393224 | tf_op jit(solution)/shard_map/ppermute | solution.py:200
  92.4 8.4 %collective-permute-start.19 = (bf16[128,512]{1,0:T(8,128)(2,1)}, bf16[128,512]{1,0:T(8,128)(2,1)S(1)}, u32[]{:S(2)}, u32[]{:S(2)}) collective-permute-start(bf16[128,512]{1,0:T(8,128)(2,1)} %get-tuple-element.36), channel_id=1, source_target_pairs={{0,10},{1,11},{2,8},{3,9},{4,14},{5,15},{6,12},{7,13},{8,18},{9,19... | collective-permute-start | bytes 393224 | tf_op jit(solution)/shard_map/ppermute | solution.py:200
  93.9 10.4 %collective-permute-start.23 = (bf16[512,256]{1,0:T(8,128)(2,1)S(1)}, bf16[512,256]{1,0:T(8,128)(2,1)S(1)}, u32[]{:S(2)}, u32[]{:S(2)}) collective-permute-start(bf16[512,256]{1,0:T(8,128)(2,1)S(1)} %pad_maximum_fusion.10.refs_8_.refs_9_), channel_id=1, source_target_pairs={{0,2},{1,3},{2,0},{3,1},{4,6},{5,7},{6,4},{7,5},{8,10},{9,11},{10,... | collective-permute-start | bytes 786440 | tf_op jit(solution)/shard_map/qr_c/ppermute | solution.py:103
  94.4 10.0 %collective-permute-start.22 = (bf16[512,256]{1,0:T(8,128)(2,1)}, bf16[512,256]{1,0:T(8,128)(2,1)S(1)}, u32[]{:S(2)}, u32[]{:S(2)}) collective-permute-start(bf16[512,256]{1,0:T(8,128)(2,1)} %collective-permute-done.20.refs_2_.refs_3_), channel_id=1, source_target_pairs={{2,4},{3,5},{4,2},{5,3},{0,1},{1,0},{6,7},{7,6},{10,12},{11,13},{1... | collective-permute-start | bytes 786440 | tf_op jit(solution)/shard_map/far_c/ppermute | solution.py:103
  97.3 15.3 %collective-permute-start.28 = (bf16[128,512]{1,0:T(8,128)(2,1)}, bf16[128,512]{1,0:T(8,128)(2,1)S(1)}, u32[]{:S(2)}, u32[]{:S(2)}) collective-permute-start(bf16[128,512]{1,0:T(8,128)(2,1)} %get-tuple-element.45), channel_id=1, source_target_pairs={{0,9},{1,8},{2,11},{3,10},{4,13},{5,12},{6,15},{7,14},{8,17},{9,16... | collective-permute-start | bytes 393224 | tf_op jit(solution)/shard_map/ppermute | solution.py:200
  100.8 11.7 %collective-permute-start.29 = (bf16[128,512]{1,0:T(8,128)(2,1)}, bf16[128,512]{1,0:T(8,128)(2,1)S(1)}, u32[]{:S(2)}, u32[]{:S(2)}) collective-permute-start(bf16[128,512]{1,0:T(8,128)(2,1)} %get-tuple-element.46), channel_id=1, source_target_pairs={{0,11},{1,10},{2,9},{3,8},{4,15},{5,14},{6,13},{7,12},{8,19},{9,18... | collective-permute-start | bytes 393224 | tf_op jit(solution)/shard_map/ppermute | solution.py:200
  102.0 2.3 %copy-start.10 = (bf16[512,256]{1,0:T(8,128)(2,1)}, bf16[512,256]{1,0:T(8,128)(2,1)S(1)}, u32[]{:S(2)}) copy-start(bf16[512,256]{1,0:T(8,128)(2,1)S(1)} %collective-permute-done.21.refs_4_.refs_5_) | copy-start | bytes 786436
  104.3 0.7 copy-start.11
  105.0 0.7 copy-start.12
  110.7 5.7 %collective-permute-start.24 = (bf16[128,256]{1,0:T(8,128)(2,1)}, bf16[128,256]{1,0:T(8,128)(2,1)S(1)}, u32[]{:S(2)}, u32[]{:S(2)}) collective-permute-start(bf16[128,256]{1,0:T(8,128)(2,1)} %get-tuple-element.41), channel_id=1, source_target_pairs={{0,8},{1,9},{2,10},{3,11},{4,12},{5,13},{6,14},{7,15},{8,16},{9,17... | collective-permute-start | bytes 196616 | tf_op jit(solution)/shard_map/ppermute | solution.py:200
  111.0 6.4 %collective-permute-start.25 = (bf16[128,256]{1,0:T(8,128)(2,1)}, bf16[128,256]{1,0:T(8,128)(2,1)S(1)}, u32[]{:S(2)}, u32[]{:S(2)}) collective-permute-start(bf16[128,256]{1,0:T(8,128)(2,1)} %get-tuple-element.42), channel_id=1, source_target_pairs={{0,10},{1,11},{2,8},{3,9},{4,14},{5,15},{6,12},{7,13},{8,18},{9,19... | collective-permute-start | bytes 196616 | tf_op jit(solution)/shard_map/ppermute | solution.py:200
  112.6 5.7 %collective-permute-start.30 = (bf16[128,256]{1,0:T(8,128)(2,1)}, bf16[128,256]{1,0:T(8,128)(2,1)S(1)}, u32[]{:S(2)}, u32[]{:S(2)}) collective-permute-start(bf16[128,256]{1,0:T(8,128)(2,1)} %get-tuple-element.47), channel_id=1, source_target_pairs={{0,9},{1,8},{2,11},{3,10},{4,13},{5,12},{6,15},{7,14},{8,17},{9,16... | collective-permute-start | bytes 196616 | tf_op jit(solution)/shard_map/ppermute | solution.py:200
  112.7 6.7 %collective-permute-start.31 = (bf16[128,256]{1,0:T(8,128)(2,1)}, bf16[128,256]{1,0:T(8,128)(2,1)S(1)}, u32[]{:S(2)}, u32[]{:S(2)}) collective-permute-start(bf16[128,256]{1,0:T(8,128)(2,1)} %get-tuple-element.48), channel_id=1, source_target_pairs={{0,11},{1,10},{2,9},{3,8},{4,15},{5,14},{6,13},{7,12},{8,19},{9,18... | collective-permute-start | bytes 196616 | tf_op jit(solution)/shard_map/ppermute | solution.py:200

commit v4 on v3

--- a/solution.py
+++ b/solution.py
@@ -11,8 +11,8 @@
 HEADS = 24
 HEAD_DIM = 128
 K_LIST = 5
-GROUPS = (6, 4, 2)
-BLOCKS = (3, 4, 2)
+GROUPS = (7, 5)
+PARTS = ((0, 0, 7, 7), (1, 0, 5, 5))
 COST = 96
 SCALE = math.log2(math.e) / math.sqrt(HEAD_DIM)
 MASKED = -1e30
@@ -102,6 +102,10 @@
         with jax.named_scope(name):
             return lax.ppermute(block, "ctx", route)
 
+    def onto(part, block, route):
+        with jax.named_scope(f"onto_{part}"):
+            return lax.ppermute(block, ("pipe", "ctx"), route)
+
     def after(block, *others):
         return lax.optimization_barrier((block, *others))[0]
 
@@ -143,16 +147,13 @@
     qr_got = got[:, width - start :]
     own_qr = [jnp.concatenate([qr_mine[:, c], qr_got[:, c]], axis=0) for c in cut]
 
+    end_b = ctx(after(own[0], end0), inward, "end_b")
     near_b = ctx(own[0], across, "near_b")
-    end_b = ctx(after(own[0], end0), inward, "end_b")
-    far0, far1 = ctx(end0, across, "far_a0"), ctx(end1, across, "far_a1")
+    far0 = ctx(end0, across, "far_a0")
+    far1 = ctx(end1, across, "far_a1")
     qr_a = ctx(after(own_qr[0], end1), inward, "qr_a")
     qr_b = ctx(after(own_qr[1], end_b), inward, "qr_b")
     far_b = ctx(end_b, across, "far_b")
-    near_c = ctx(after(own[1], end_b), across, "near_c")
-    end_c = ctx(after(own[1], qr_a), inward, "end_c")
-    far_c = ctx(end_c, across, "far_c")
-    qr_c = ctx(after(own_qr[2], qr_b), inward, "qr_c")
 
     chips = jnp.stack([chip, chip ^ 1, 3 - chip, 3 - (chip ^ 1)])
     order = (2 * chips[:, None] + jnp.stack([core, 1 - core])[None, :]).reshape(1, 1, 8, 1)
@@ -168,24 +169,29 @@
     pairs = [
         whole(mine, sibling, end0, end1, near0, near1, far0, far1),
         twice(own[0]) + twice(end_b) + twice(near_b) + twice(far_b),
-        twice(own[1]) + twice(end_c) + twice(near_c) + twice(far_c),
     ]
-    rests = [twice(own_qr[g]) + twice(block) for g, block in enumerate((qr_a, qr_b, qr_c))]
+    rests = [twice(own_qr[g]) + twice(block) for g, block in enumerate((qr_a, qr_b))]
     same, other = [], []
     inner = (chip == 1) | (chip == 2)
-    for g, (size, block) in enumerate(zip(GROUPS, BLOCKS)):
+    for part, (g, start, size, block) in enumerate(PARTS):
         cols = block * HEAD_DIM
-        inputs = pairs[g] + rests[g] + [(gate_mine[:, cut[g]], 0)]
+        first = edges[g] + start
+        skip = start // block
+        inputs = pairs[g] + rests[g]
+        inputs = [(array, place, skip) for array, place in inputs]
+        inputs += [(gate_mine[:, first * HEAD_DIM : (first + size) * HEAD_DIM], 0, 0)]
         heights = [2 * rows] * 12 + [1]
+        if part == 0:
+            table = table
         results = pl.pallas_call(
-            functools.partial(relay_kernel, edges[g], half, block),
+            functools.partial(relay_kernel, first, half, block),
             out_shape=[jax.ShapeDtypeStruct((rows, size * HEAD_DIM), jnp.bfloat16)] * 4,
             grid_spec=pltpu.PrefetchScalarGridSpec(
                 num_scalar_prefetch=1,
                 grid=(size // block,),
                 in_specs=[
-                    pl.BlockSpec((height, cols), lambda h, m, place=place: (place, h))
-                    for height, (_, place) in zip(heights, inputs)
+                    pl.BlockSpec((height, cols), lambda h, m, place=place, skip=skip: (place, skip + h))
+                    for height, (_, place, skip) in zip(heights, inputs)
                 ],
                 out_specs=[pl.BlockSpec((rows, cols), lambda h, m: (0, h))] * 4,
             ),
@@ -194,10 +200,10 @@
                 bytes_accessed=size * 28 * rows * HEAD_DIM * 2,
                 transcendentals=size * 4 * rows * 8 * rows,
             ),
-        )(table, *(array for array, _ in inputs))
+        )(table, *(array for array, *_ in inputs))
         table = after(table, results[0])
         sent = [
-            lax.ppermute(piece, ("pipe", "ctx"), onward(change))
+            onto(part, piece, onward(change))
             for piece, change in zip(results, (0, 1, 2, 3))
         ]
         same.append(jnp.where(inner, sent[0], sent[2]))

time: 121 us -> 117 us (0.967)
  waiting for transfers between devices: 48.1 us -> 57.1 us
  starting transfers between devices: 38.2 us -> 30.7 us
  Pallas kernels: 20.6 us -> 17.6 us
  local copies, waits for them, and re-layouts: 5.07 us -> 2.23 us
    ppermute x20 -> x16, waiting for transfers between devices: 33.7 us -> 40.5 us  [ctx(): return lax.ppermute(block, 'ctx', route)]
    ppermute x12 -> x8, starting transfers between devices: 18.1 us -> 13.4 us  [onto(): return lax.ppermute(block, ('pipe', 'ctx'), route)]
    pallas_call x3 -> x2, Pallas kernels: 20.6 us -> 17.6 us  [relay_section(): pl.pallas_call(functools.partial(relay_kernel, first, half, block), out_s...]
    ppermute x20 -> x16, starting transfers between devices: 20.2 us -> 17.3 us  [ctx(): return lax.ppermute(block, 'ctx', route)]
    unnamed x29 -> x15, local copies, waits for them, and re-layouts: 2.29 us -> 0.04 us
    ppermute x12 -> x8, waiting for transfers between devices: 14.5 us -> 16.7 us  [onto(): return lax.ppermute(block, ('pipe', 'ctx'), route)]
    select_n x0 -> x1, other arithmetic: none -> 1.37 us  [picked(): jnp.where(core == 0, right, left)]
  transfers between devices with their start and end apart: 32 -> 24, of which waited for: 14 -> 8; matrix products, arithmetic and copies ran while one was open for 6% -> 6% of each run, Pallas kernels for 17% -> 15%
where the time goes in v4:
time: 117 us; the launch traced here: 116 us
  waiting for transfers between devices  57.1 us (49%)
  starting transfers between devices  30.7 us (26%)
  Pallas kernels  17.6 us (15%)
  other arithmetic  8.4 us (7%)
  local copies, waits for them, and re-layouts  2.23 us (2%)
    ppermute x16, waiting for transfers between devices, ctx(): return lax.ppermute(block, 'ctx', route)  40.5 us
    pallas_call x2, Pallas kernels, relay_section(): pl.pallas_call(functools.partial(relay_kernel, first, half, block), out_s...  17.6 us
    ppermute x16, starting transfers between devices, ctx(): return lax.ppermute(block, 'ctx', route)  17.3 us
    ppermute x8, waiting for transfers between devices, onto(): return lax.ppermute(block, ('pipe', 'ctx'), route)  16.7 us
    ppermute x8, starting transfers between devices, onto(): return lax.ppermute(block, ('pipe', 'ctx'), route)  13.4 us
  transfers between devices with their start and end apart: 24, of which 8 were waited for; matrix products, arithmetic and copies ran while one was open for 6% of the time, Pallas kernels for 15%

profile of v4, /device:TPU:0, one launch (start us, length us, event | category | flops | bytes accessed | tf_op | source)
XLA Modules:
  0.0 116.3 jit_solution(5824729777239608339)
XLA Ops:
  0.0 1.4 %broadcast_select_fusion.4 = (bf16[128,896]{1,0:T(8,128)(2,1)S(1)}, bf16[128,896]{1,0:T(8,128)(2,1)S(1)}, bf16[128,896]{1,0:T(8,128)(2,1)S(1)}, bf16[128,896]{1,0:T(8,128)(2,1)S(1)}) fusion(pred[]{:T(512)S(6)} %eq.27, bf16[128,3072]{1,0:T(8,128)(2,1)} %bitcast.20, bf16[128,3072]{1,0:T(8,128)(2,1)} %bitcast.22), kind=kLoop, calls=%fused_computation.17 | loop fusion | flops 458752 | bytes 1835009 | tf_op jit(solution)/shard_map/jit(_where)/select_n | solution.py:125
  1.4 0.8 pad_maximum_fusion.6
  2.2 0.5 collective-permute-start.3
  2.7 1.2 %broadcast_select_fusion.12 = (bf16[128,640]{1,0:T(8,128)(2,1)S(1)}, bf16[128,640]{1,0:T(8,128)(2,1)S(1)}, bf16[128,640]{1,0:T(8,128)(2,1)S(1)}, bf16[128,640]{1,0:T(8,128)(2,1)S(1)}) fusion(pred[]{:T(512)S(6)} %eq.27, bf16[128,3072]{1,0:T(8,128)(2,1)} %bitcast.21, bf16[128,3072]{1,0:T(8,128)(2,1)} %bitcast.23), kind=kLoop, calls=%fused_computation.25 | loop fusion | flops 327680 | bytes 1310721 | tf_op jit(solution)/shard_map/jit(_where)/select_n | solution.py:125
  3.9 0.3 broadcast_select_fusion.1
  4.2 1.1 pad_maximum_fusion
  5.4 0.1 add_convert_fusion
  5.5 0.1 slice_select_fusion.1
  5.6 0.5 collective-permute-start
  6.0 2.7 %collective-permute-start.2 = (f32[12,8]{0,1:T(8,128)S(1)}, f32[12,8]{0,1:T(8,128)S(1)}, u32[]{:S(2)}, u32[]{:S(2)}) collective-permute-start(f32[12,8]{0,1:T(8,128)S(1)} %get-tuple-element.48), channel_id=1, source_target_pairs={{0,3},{1,2},{2,1},{3,0},{4,7},{5,6},{6,5},{7,4},{8,11},{9,10},{10,... | collective-permute-start | bytes 1160 | tf_op jit(solution)/shard_map/table_end1/ppermute | solution.py:103
  8.7 0.8 pad_maximum_fusion.5.refs_0_
  9.6 2.0 %collective-permute-start.4 = (bf16[256,896]{1,0:T(8,128)(2,1)}, bf16[256,896]{1,0:T(8,128)(2,1)}, u32[]{:S(2)}, u32[]{:S(2)}) collective-permute-start(bf16[256,896]{1,0:T(8,128)(2,1)} %pad_maximum_fusion.5.refs_0_), channel_id=1, source_target_pairs={{0,2},{1,3},{2,0},{3,1},{4,6},{5,7},{6,4},{7,5},{8,10},{9,11},{10,... | collective-permute-start | bytes 1376264 | tf_op jit(solution)/shard_map/end_a0/ppermute | solution.py:103
  11.6 0.1 pad_add_fusion
  11.7 0.1 add_multiply_fusion
  11.7 0.6 collective-permute-done.1
  12.3 0.5 collective-permute-start.6
  12.9 2.4 %collective-permute-start.5 = (bf16[256,896]{1,0:T(8,128)(2,1)}, bf16[256,896]{1,0:T(8,128)(2,1)}, u32[]{:S(2)}, u32[]{:S(2)}) collective-permute-start(bf16[256,896]{1,0:T(8,128)(2,1)} %pad_maximum_fusion.6), channel_id=1, source_target_pairs={{0,3},{1,2},{2,1},{3,0},{4,7},{5,6},{6,5},{7,4},{8,11},{9,10},{10,... | collective-permute-start | bytes 1376264 | tf_op jit(solution)/shard_map/end_a1/ppermute | solution.py:103
  15.3 0.9 pad_maximum_fusion.3.refs_0_.refs_1_
  16.2 7.0 %collective-permute-done.4.refs_2_ = bf16[256,896]{1,0:T(8,128)(2,1)} collective-permute-done((bf16[256,896]{1,0:T(8,128)(2,1)}, bf16[256,896]{1,0:T(8,128)(2,1)}, u32[]{:S(2)}, u32[]{:S(2)}) %collective-permute-start.4) | collective-permute-done | bytes 458784 | tf_op jit(solution)/shard_map/end_a0/ppermute | solution.py:103
  23.2 2.1 %collective-permute-start.14 = (bf16[512,640]{1,0:T(8,128)(2,1)}, bf16[512,640]{1,0:T(8,128)(2,1)}, u32[]{:S(2)}, u32[]{:S(2)}) collective-permute-start(bf16[512,640]{1,0:T(8,128)(2,1)} %pad_maximum_fusion.3.refs_0_.refs_1_), channel_id=1, source_target_pairs={{0,2},{1,3},{2,0},{3,1},{4,6},{5,7},{6,4},{7,5},{8,10},{9,11},{10,... | collective-permute-start | bytes 1966088 | tf_op jit(solution)/shard_map/end_b/ppermute | solution.py:103
  25.3 0.1 broadcast_add_fusion
  25.4 0.1 add.37
  25.6 0.1 pad_maximum_fusion.1.refs_8_.refs_9_
  25.7 7.0 %collective-permute-done.5.refs_3_ = bf16[256,896]{1,0:T(8,128)(2,1)} collective-permute-done((bf16[256,896]{1,0:T(8,128)(2,1)}, bf16[256,896]{1,0:T(8,128)(2,1)}, u32[]{:S(2)}, u32[]{:S(2)}) %collective-permute-start.5) | collective-permute-done | bytes 458784 | tf_op jit(solution)/shard_map/end_a1/ppermute | solution.py:103
  32.7 2.4 %collective-permute-start.8 = (bf16[256,896]{1,0:T(8,128)(2,1)}, bf16[256,896]{1,0:T(8,128)(2,1)}, u32[]{:S(2)}, u32[]{:S(2)}) collective-permute-start(bf16[256,896]{1,0:T(8,128)(2,1)} %collective-permute-done.4.refs_2_), channel_id=1, source_target_pairs={{2,4},{3,5},{4,2},{5,3},{0,1},{1,0},{6,7},{7,6},{10,12},{11,13},{1... | collective-permute-start | bytes 1376264 | tf_op jit(solution)/shard_map/far_a0/ppermute | solution.py:103
  35.1 12.0 %collective-permute-done.14.refs_2_.refs_3_ = bf16[512,640]{1,0:T(8,128)(2,1)} collective-permute-done((bf16[512,640]{1,0:T(8,128)(2,1)}, bf16[512,640]{1,0:T(8,128)(2,1)}, u32[]{:S(2)}, u32[]{:S(2)}) %collective-permute-start.14) | collective-permute-done | bytes 655392 | tf_op jit(solution)/shard_map/end_b/ppermute | solution.py:103
  47.1 0.1 iota_compare_fusion.2
  47.2 0.6 slice.85.refs_12_
  47.8 0.1 select_reduce_fusion
  47.9 0.1 copy.12
  48.0 0.7 reshape.114.mult_ref
  48.8 0.6 collective-permute-start.15
  49.4 3.6 %collective-permute-start.17 = (bf16[512,640]{1,0:T(8,128)(2,1)S(1)}, bf16[512,640]{1,0:T(8,128)(2,1)}, u32[]{:S(2)}, u32[]{:S(2)}) collective-permute-start(bf16[512,640]{1,0:T(8,128)(2,1)S(1)} %pad_maximum_fusion.4.refs_8_.refs_9_), channel_id=1, source_target_pairs={{0,2},{1,3},{2,0},{3,1},{4,6},{5,7},{6,4},{7,5},{8,10},{9,11},{10,... | collective-permute-start | bytes 1966088 | tf_op jit(solution)/shard_map/qr_b/ppermute | solution.py:103
  53.0 13.8 %collective-permute-done.11.refs_10_.refs_11_ = bf16[512,896]{1,0:T(8,128)(2,1)} collective-permute-done((bf16[512,896]{1,0:T(8,128)(2,1)S(1)}, bf16[512,896]{1,0:T(8,128)(2,1)}, u32[]{:S(2)}, u32[]{:S(2)}) %collective-permute-start.11) | collective-permute-done | bytes 917536 | tf_op jit(solution)/shard_map/qr_a/ppermute | solution.py:103
  66.8 9.8 %shard_map.73 = (bf16[128,896]{1,0:T(8,128)(2,1)}, bf16[128,896]{1,0:T(8,128)(2,1)}, bf16[128,896]{1,0:T(8,128)(2,1)}, bf16[128,896]{1,0:T(8,128)(2,1)}) custom-call(f32[384]{0:T(512)} %reshape.114.mult_ref, bf16[256,896]{1,0:T(8,128)(2,1)} %pad_maximum_fusion.5.refs_0_, bf16[256,896]{1,0:T(8,128)(2,1)} %collective-permute-done.3.refs_1_, ...), custom_call_target="tpu_custom_call" | custom-call | flops 11274289152 | bytes 6422528 | tf_op jit(solution)/shard_map/pallas_call | solution.py:186
  76.5 2.0 %collective-permute-start.12 = (bf16[128,896]{1,0:T(8,128)(2,1)}, bf16[128,896]{1,0:T(8,128)(2,1)S(1)}, u32[]{:S(2)}, u32[]{:S(2)}) collective-permute-start(bf16[128,896]{1,0:T(8,128)(2,1)} %get-tuple-element.22), channel_id=1, source_target_pairs={{0,8},{1,9},{2,10},{3,11},{4,12},{5,13},{6,14},{7,15},{8,16},{9,17... | collective-permute-start | bytes 688136 | tf_op jit(solution)/shard_map/onto_0/ppermute | solution.py:107
  78.5 2.5 %collective-permute-start.13 = (bf16[128,896]{1,0:T(8,128)(2,1)}, bf16[128,896]{1,0:T(8,128)(2,1)S(1)}, u32[]{:S(2)}, u32[]{:S(2)}) collective-permute-start(bf16[128,896]{1,0:T(8,128)(2,1)} %get-tuple-element.23), channel_id=1, source_target_pairs={{0,10},{1,11},{2,8},{3,9},{4,14},{5,15},{6,12},{7,13},{8,18},{9,19... | collective-permute-start | bytes 688136 | tf_op jit(solution)/shard_map/onto_0/ppermute | solution.py:107
  81.0 0.6 slice.89.refs_12_
  81.6 7.0 %collective-permute-done.12 = bf16[128,896]{1,0:T(8,128)(2,1)S(1)} collective-permute-done((bf16[128,896]{1,0:T(8,128)(2,1)}, bf16[128,896]{1,0:T(8,128)(2,1)S(1)}, u32[]{:S(2)}, u32[]{:S(2)}) %collective-permute-start.12) | collective-permute-done | bytes 229408 | tf_op jit(solution)/shard_map/onto_0/ppermute | solution.py:107
  88.6 3.3 %collective-permute-start.21 = (bf16[128,896]{1,0:T(8,128)(2,1)}, bf16[128,896]{1,0:T(8,128)(2,1)S(1)}, u32[]{:S(2)}, u32[]{:S(2)}) collective-permute-start(bf16[128,896]{1,0:T(8,128)(2,1)} %get-tuple-element.30), channel_id=1, source_target_pairs={{0,11},{1,10},{2,9},{3,8},{4,15},{5,14},{6,13},{7,12},{8,19},{9,18... | collective-permute-start | bytes 688136 | tf_op jit(solution)/shard_map/onto_0/ppermute | solution.py:107
  92.0 7.8 %shard_map.74 = (bf16[128,640]{1,0:T(8,128)(2,1)}, bf16[128,640]{1,0:T(8,128)(2,1)}, bf16[128,640]{1,0:T(8,128)(2,1)}, bf16[128,640]{1,0:T(8,128)(2,1)}) custom-call(f32[384]{0:T(512)} %reshape.114.mult_ref, bf16[512,640]{1,0:T(8,128)(2,1)} %pad_maximum_fusion.3.refs_0_.refs_1_, bf16[512,640]{1,0:T(8,128)(2,1)} %pad_maximum_fusion.3.refs_0_.refs_1_, ...), custom_call_target="tpu_custom_call" | custom-call | flops 8053063680 | bytes 4587520 | tf_op jit(solution)/shard_map/pallas_call | solution.py:186
  99.8 0.6 collective-permute-start.18
  100.4 1.7 %collective-permute-start.19 = (bf16[128,640]{1,0:T(8,128)(2,1)}, bf16[128,640]{1,0:T(8,128)(2,1)S(1)}, u32[]{:S(2)}, u32[]{:S(2)}) collective-permute-start(bf16[128,640]{1,0:T(8,128)(2,1)} %get-tuple-element.28), channel_id=1, source_target_pairs={{0,10},{1,11},{2,8},{3,9},{4,14},{5,15},{6,12},{7,13},{8,18},{9,19... | collective-permute-start | bytes 491528 | tf_op jit(solution)/shard_map/onto_1/ppermute | solution.py:107
  102.1 3.3 %collective-permute-start.23 = (bf16[128,640]{1,0:T(8,128)(2,1)}, bf16[128,640]{1,0:T(8,128)(2,1)S(1)}, u32[]{:S(2)}, u32[]{:S(2)}) collective-permute-start(bf16[128,640]{1,0:T(8,128)(2,1)} %get-tuple-element.32), channel_id=1, source_target_pairs={{0,11},{1,10},{2,9},{3,8},{4,15},{5,14},{6,13},{7,12},{8,19},{9,18... | collective-permute-start | bytes 491528 | tf_op jit(solution)/shard_map/onto_1/ppermute | solution.py:107
  105.4 9.4 %collective-permute-done.18 = bf16[128,640]{1,0:T(8,128)(2,1)S(1)} collective-permute-done((bf16[128,640]{1,0:T(8,128)(2,1)}, bf16[128,640]{1,0:T(8,128)(2,1)S(1)}, u32[]{:S(2)}, u32[]{:S(2)}) %collective-permute-start.18) | collective-permute-done | bytes 163872 | tf_op jit(solution)/shard_map/onto_1/ppermute | solution.py:107
  114.9 0.3 collective-permute-done.22
  115.1 0.1 broadcast_select_fusion.3
  115.3 1.0 maximum_bitcast_fusion
  (53 shorter events, 0.6 us)
Async XLA Ops:
  1.4 2.5 %copy-start.5 = (s32[1,1,24,5]{2,1,3,0:T(1,128)S(1)}, s32[1,1,24,5]{2,1,3,0:T(1,128)}, u32[]{:S(2)}) copy-start(s32[1,1,24,5]{2,1,3,0:T(1,128)} %param.12) | copy-start | bytes 1444
  1.4 2.5 %copy-start.1 = (bf16[1,128,3072]{2,1,0:T(8,128)(2,1)S(1)}, bf16[1,128,3072]{2,1,0:T(8,128)(2,1)}, u32[]{:S(2)}) copy-start(bf16[1,128,3072]{2,1,0:T(8,128)(2,1)} %param.10) | copy-start | bytes 2359300
  1.4 2.5 %copy-start.2 = (bf16[1,128,3072]{2,1,0:T(8,128)(2,1)S(1)}, bf16[1,128,3072]{2,1,0:T(8,128)(2,1)}, u32[]{:S(2)}) copy-start(bf16[1,128,3072]{2,1,0:T(8,128)(2,1)} %param.7) | copy-start | bytes 2359300
  2.2 3.1 %collective-permute-start.3 = (bf16[256,896]{1,0:T(8,128)(2,1)}, bf16[256,896]{1,0:T(8,128)(2,1)}, u32[]{:S(2)}, u32[]{:S(2)}) collective-permute-start(bf16[256,896]{1,0:T(8,128)(2,1)} %pad_maximum_fusion.6), channel_id=1, source_target_pairs={{0,1},{1,0},{2,3},{3,2},{4,5},{5,4},{6,7},{7,6},{8,9},{9,8},{10,11... | collective-permute-start | bytes 1376264 | tf_op jit(solution)/shard_map/swap_a/ppermute | solution.py:103
  4.2 1.2 copy-start.6
  5.3 9.9 %collective-permute-start.10 = (bf16[256,2176]{1,0:T(8,128)(2,1)}, bf16[256,2176]{1,0:T(8,128)(2,1)S(1)}, u32[]{:S(2)}, u32[]{:S(2)}) collective-permute-start(bf16[256,2176]{1,0:T(8,128)(2,1)} %pad_maximum_fusion), channel_id=1, source_target_pairs={{0,1},{1,0},{2,3},{3,2},{4,5},{5,4},{6,7},{7,6},{8,9},{9,8},{10,11... | collective-permute-start | bytes 3342344 | tf_op jit(solution)/shard_map/swap_rest/ppermute | solution.py:103
  5.6 6.8 %collective-permute-start = (f32[12,8]{0,1:T(8,128)S(1)}, f32[12,8]{0,1:T(8,128)S(1)}, u32[]{:S(2)}, u32[]{:S(2)}) collective-permute-start(f32[12,8]{0,1:T(8,128)S(1)} %get-tuple-element.48), channel_id=1, source_target_pairs={{0,1},{1,0},{2,3},{3,2},{4,5},{5,4},{6,7},{7,6},{8,9},{9,8},{10,11... | collective-permute-start | bytes 1160 | tf_op jit(solution)/shard_map/table_swap/ppermute | solution.py:103
  6.0 6.8 %collective-permute-start.2 = (f32[12,8]{0,1:T(8,128)S(1)}, f32[12,8]{0,1:T(8,128)S(1)}, u32[]{:S(2)}, u32[]{:S(2)}) collective-permute-start(f32[12,8]{0,1:T(8,128)S(1)} %get-tuple-element.48), channel_id=1, source_target_pairs={{0,3},{1,2},{2,1},{3,0},{4,7},{5,6},{6,5},{7,4},{8,11},{9,10},{10,... | collective-permute-start | bytes 1160 | tf_op jit(solution)/shard_map/table_end1/ppermute | solution.py:103
  8.7 3.6 %collective-permute-start.1 = (f32[12,8]{0,1:T(8,128)S(1)}, f32[12,8]{0,1:T(8,128)S(1)}, u32[]{:S(2)}, u32[]{:S(2)}) collective-permute-start(f32[12,8]{0,1:T(8,128)S(1)} %get-tuple-element.47), channel_id=1, source_target_pairs={{0,2},{1,3},{2,0},{3,1},{4,6},{5,7},{6,4},{7,5},{8,10},{9,11},{10,... | collective-permute-start | bytes 1160 | tf_op jit(solution)/shard_map/table_end0/ppermute | solution.py:103
  9.6 13.7 %collective-permute-start.4 = (bf16[256,896]{1,0:T(8,128)(2,1)}, bf16[256,896]{1,0:T(8,128)(2,1)}, u32[]{:S(2)}, u32[]{:S(2)}) collective-permute-start(bf16[256,896]{1,0:T(8,128)(2,1)} %pad_maximum_fusion.5.refs_0_), channel_id=1, source_target_pairs={{0,2},{1,3},{2,0},{3,1},{4,6},{5,7},{6,4},{7,5},{8,10},{9,11},{10,... | collective-permute-start | bytes 1376264 | tf_op jit(solution)/shard_map/end_a0/ppermute | solution.py:103
  12.3 36.5 %collective-permute-start.7 = (bf16[256,896]{1,0:T(8,128)(2,1)}, bf16[256,896]{1,0:T(8,128)(2,1)}, u32[]{:S(2)}, u32[]{:S(2)}) collective-permute-start(bf16[256,896]{1,0:T(8,128)(2,1)} %pad_maximum_fusion.6), channel_id=1, source_target_pairs={{2,5},{3,4},{4,3},{5,2},{0,1},{1,0},{6,7},{7,6},{10,13},{11,12},{1... | collective-permute-start | bytes 1376264 | tf_op jit(solution)/shard_map/near_a1/ppermute | solution.py:103
  12.3 37.0 %collective-permute-start.6 = (bf16[256,896]{1,0:T(8,128)(2,1)}, bf16[256,896]{1,0:T(8,128)(2,1)}, u32[]{:S(2)}, u32[]{:S(2)}) collective-permute-start(bf16[256,896]{1,0:T(8,128)(2,1)} %pad_maximum_fusion.5.refs_0_), channel_id=1, source_target_pairs={{2,4},{3,5},{4,2},{5,3},{0,1},{1,0},{6,7},{7,6},{10,12},{11,13},{1... | collective-permute-start | bytes 1376264 | tf_op jit(solution)/shard_map/near_a0/ppermute | solution.py:103
  12.9 19.8 %collective-permute-start.5 = (bf16[256,896]{1,0:T(8,128)(2,1)}, bf16[256,896]{1,0:T(8,128)(2,1)}, u32[]{:S(2)}, u32[]{:S(2)}) collective-permute-start(bf16[256,896]{1,0:T(8,128)(2,1)} %pad_maximum_fusion.6), channel_id=1, source_target_pairs={{0,3},{1,2},{2,1},{3,0},{4,7},{5,6},{6,5},{7,4},{8,11},{9,10},{10,... | collective-permute-start | bytes 1376264 | tf_op jit(solution)/shard_map/end_a1/ppermute | solution.py:103
  23.2 23.9 %collective-permute-start.14 = (bf16[512,640]{1,0:T(8,128)(2,1)}, bf16[512,640]{1,0:T(8,128)(2,1)}, u32[]{:S(2)}, u32[]{:S(2)}) collective-permute-start(bf16[512,640]{1,0:T(8,128)(2,1)} %pad_maximum_fusion.3.refs_0_.refs_1_), channel_id=1, source_target_pairs={{0,2},{1,3},{2,0},{3,1},{4,6},{5,7},{6,4},{7,5},{8,10},{9,11},{10,... | collective-permute-start | bytes 1966088 | tf_op jit(solution)/shard_map/end_b/ppermute | solution.py:103
  25.6 7.1 %copy-start.4 = (f32[1,3072]{1,0:T(1,128)S(1)}, f32[1,3072]{1,0:T(1,128)}, u32[]{:S(2)}) copy-start(f32[1,3072]{1,0:T(1,128)} %param.11) | copy-start | bytes 36868
  25.6 41.1 %copy-start = (bf16[512,896]{1,0:T(8,128)(2,1)}, bf16[512,896]{1,0:T(8,128)(2,1)S(1)}, u32[]{:S(2)}) copy-start(bf16[512,896]{1,0:T(8,128)(2,1)S(1)} %pad_maximum_fusion.1.refs_8_.refs_9_) | copy-start | bytes 2752516
  32.7 34.1 %collective-permute-start.11 = (bf16[512,896]{1,0:T(8,128)(2,1)S(1)}, bf16[512,896]{1,0:T(8,128)(2,1)}, u32[]{:S(2)}, u32[]{:S(2)}) collective-permute-start(bf16[512,896]{1,0:T(8,128)(2,1)S(1)} %pad_maximum_fusion.1.refs_8_.refs_9_), channel_id=1, source_target_pairs={{0,2},{1,3},{2,0},{3,1},{4,6},{5,7},{6,4},{7,5},{8,10},{9,11},{10,... | collective-permute-start | bytes 2752520 | tf_op jit(solution)/shard_map/qr_a/ppermute | solution.py:103
  32.7 20.3 %collective-permute-start.8 = (bf16[256,896]{1,0:T(8,128)(2,1)}, bf16[256,896]{1,0:T(8,128)(2,1)}, u32[]{:S(2)}, u32[]{:S(2)}) collective-permute-start(bf16[256,896]{1,0:T(8,128)(2,1)} %collective-permute-done.4.refs_2_), channel_id=1, source_target_pairs={{2,4},{3,5},{4,2},{5,3},{0,1},{1,0},{6,7},{7,6},{10,12},{11,13},{1... | collective-permute-start | bytes 1376264 | tf_op jit(solution)/shard_map/far_a0/ppermute | solution.py:103
  47.1 5.9 %collective-permute-start.9 = (bf16[256,896]{1,0:T(8,128)(2,1)}, bf16[256,896]{1,0:T(8,128)(2,1)}, u32[]{:S(2)}, u32[]{:S(2)}) collective-permute-start(bf16[256,896]{1,0:T(8,128)(2,1)} %collective-permute-done.5.refs_3_), channel_id=1, source_target_pairs={{2,4},{3,5},{4,2},{5,3},{0,1},{1,0},{6,7},{7,6},{10,12},{11,13},{1... | collective-permute-start | bytes 1376264 | tf_op jit(solution)/shard_map/far_a1/ppermute | solution.py:103
  48.8 27.8 %copy-start.3 = (bf16[512,640]{1,0:T(8,128)(2,1)}, bf16[512,640]{1,0:T(8,128)(2,1)S(1)}, u32[]{:S(2)}) copy-start(bf16[512,640]{1,0:T(8,128)(2,1)S(1)} %pad_maximum_fusion.4.refs_8_.refs_9_) | copy-start | bytes 1966084
  48.8 43.1 %collective-permute-start.15 = (bf16[512,640]{1,0:T(8,128)(2,1)}, bf16[512,640]{1,0:T(8,128)(2,1)}, u32[]{:S(2)}, u32[]{:S(2)}) collective-permute-start(bf16[512,640]{1,0:T(8,128)(2,1)} %pad_maximum_fusion.3.refs_0_.refs_1_), channel_id=1, source_target_pairs={{2,4},{3,5},{4,2},{5,3},{0,1},{1,0},{6,7},{7,6},{10,12},{11,13},{1... | collective-permute-start | bytes 1966088 | tf_op jit(solution)/shard_map/near_b/ppermute | solution.py:103
  49.4 42.6 %collective-permute-start.17 = (bf16[512,640]{1,0:T(8,128)(2,1)S(1)}, bf16[512,640]{1,0:T(8,128)(2,1)}, u32[]{:S(2)}, u32[]{:S(2)}) collective-permute-start(bf16[512,640]{1,0:T(8,128)(2,1)S(1)} %pad_maximum_fusion.4.refs_8_.refs_9_), channel_id=1, source_target_pairs={{0,2},{1,3},{2,0},{3,1},{4,6},{5,7},{6,4},{7,5},{8,10},{9,11},{10,... | collective-permute-start | bytes 1966088 | tf_op jit(solution)/shard_map/qr_b/ppermute | solution.py:103
  53.0 39.0 %collective-permute-start.16 = (bf16[512,640]{1,0:T(8,128)(2,1)}, bf16[512,640]{1,0:T(8,128)(2,1)}, u32[]{:S(2)}, u32[]{:S(2)}) collective-permute-start(bf16[512,640]{1,0:T(8,128)(2,1)} %collective-permute-done.14.refs_2_.refs_3_), channel_id=1, source_target_pairs={{2,4},{3,5},{4,2},{5,3},{0,1},{1,0},{6,7},{7,6},{10,12},{11,13},{1... | collective-permute-start | bytes 1966088 | tf_op jit(solution)/shard_map/far_b/ppermute | solution.py:103
  76.5 12.1 %collective-permute-start.12 = (bf16[128,896]{1,0:T(8,128)(2,1)}, bf16[128,896]{1,0:T(8,128)(2,1)S(1)}, u32[]{:S(2)}, u32[]{:S(2)}) collective-permute-start(bf16[128,896]{1,0:T(8,128)(2,1)} %get-tuple-element.22), channel_id=1, source_target_pairs={{0,8},{1,9},{2,10},{3,11},{4,12},{5,13},{6,14},{7,15},{8,16},{9,17... | collective-permute-start | bytes 688136 | tf_op jit(solution)/shard_map/onto_0/ppermute | solution.py:107
  78.5 10.1 %collective-permute-start.13 = (bf16[128,896]{1,0:T(8,128)(2,1)}, bf16[128,896]{1,0:T(8,128)(2,1)S(1)}, u32[]{:S(2)}, u32[]{:S(2)}) collective-permute-start(bf16[128,896]{1,0:T(8,128)(2,1)} %get-tuple-element.23), channel_id=1, source_target_pairs={{0,10},{1,11},{2,8},{3,9},{4,14},{5,15},{6,12},{7,13},{8,18},{9,19... | collective-permute-start | bytes 688136 | tf_op jit(solution)/shard_map/onto_0/ppermute | solution.py:107
  88.6 13.4 %collective-permute-start.20 = (bf16[128,896]{1,0:T(8,128)(2,1)}, bf16[128,896]{1,0:T(8,128)(2,1)S(1)}, u32[]{:S(2)}, u32[]{:S(2)}) collective-permute-start(bf16[128,896]{1,0:T(8,128)(2,1)} %get-tuple-element.29), channel_id=1, source_target_pairs={{0,9},{1,8},{2,11},{3,10},{4,13},{5,12},{6,15},{7,14},{8,17},{9,16... | collective-permute-start | bytes 688136 | tf_op jit(solution)/shard_map/onto_0/ppermute | solution.py:107
  88.6 13.4 %collective-permute-start.21 = (bf16[128,896]{1,0:T(8,128)(2,1)}, bf16[128,896]{1,0:T(8,128)(2,1)S(1)}, u32[]{:S(2)}, u32[]{:S(2)}) collective-permute-start(bf16[128,896]{1,0:T(8,128)(2,1)} %get-tuple-element.30), channel_id=1, source_target_pairs={{0,11},{1,10},{2,9},{3,8},{4,15},{5,14},{6,13},{7,12},{8,19},{9,18... | collective-permute-start | bytes 688136 | tf_op jit(solution)/shard_map/onto_0/ppermute | solution.py:107
  99.8 15.1 %collective-permute-start.18 = (bf16[128,640]{1,0:T(8,128)(2,1)}, bf16[128,640]{1,0:T(8,128)(2,1)S(1)}, u32[]{:S(2)}, u32[]{:S(2)}) collective-permute-start(bf16[128,640]{1,0:T(8,128)(2,1)} %get-tuple-element.27), channel_id=1, source_target_pairs={{0,8},{1,9},{2,10},{3,11},{4,12},{5,13},{6,14},{7,15},{8,16},{9,17... | collective-permute-start | bytes 491528 | tf_op jit(solution)/shard_map/onto_1/ppermute | solution.py:107
  100.4 14.5 %collective-permute-start.19 = (bf16[128,640]{1,0:T(8,128)(2,1)}, bf16[128,640]{1,0:T(8,128)(2,1)S(1)}, u32[]{:S(2)}, u32[]{:S(2)}) collective-permute-start(bf16[128,640]{1,0:T(8,128)(2,1)} %get-tuple-element.28), channel_id=1, source_target_pairs={{0,10},{1,11},{2,8},{3,9},{4,14},{5,15},{6,12},{7,13},{8,18},{9,19... | collective-permute-start | bytes 491528 | tf_op jit(solution)/shard_map/onto_1/ppermute | solution.py:107
  102.1 13.1 %collective-permute-start.22 = (bf16[128,640]{1,0:T(8,128)(2,1)}, bf16[128,640]{1,0:T(8,128)(2,1)S(1)}, u32[]{:S(2)}, u32[]{:S(2)}) collective-permute-start(bf16[128,640]{1,0:T(8,128)(2,1)} %get-tuple-element.31), channel_id=1, source_target_pairs={{0,9},{1,8},{2,11},{3,10},{4,13},{5,12},{6,15},{7,14},{8,17},{9,16... | collective-permute-start | bytes 491528 | tf_op jit(solution)/shard_map/onto_1/ppermute | solution.py:107
  102.1 13.0 %collective-permute-start.23 = (bf16[128,640]{1,0:T(8,128)(2,1)}, bf16[128,640]{1,0:T(8,128)(2,1)S(1)}, u32[]{:S(2)}, u32[]{:S(2)}) collective-permute-start(bf16[128,640]{1,0:T(8,128)(2,1)} %get-tuple-element.32), channel_id=1, source_target_pairs={{0,11},{1,10},{2,9},{3,8},{4,15},{5,14},{6,13},{7,12},{8,19},{9,18... | collective-permute-start | bytes 491528 | tf_op jit(solution)/shard_map/onto_1/ppermute | solution.py:107

commit v5 on v4

--- a/solution.py
+++ b/solution.py
@@ -58,9 +58,10 @@
             jnp.concatenate([ref[rows:, cols] for ref in pairs], axis=0),
             mults,
         )
-        for t, (rest, o_ref) in enumerate(zip(rests, outs)):
+        for t, rest in enumerate(rests):
             part = mixed[t * rows : (t + 1) * rows]
-            o_ref[:, cols] = finish(rest[rows:, cols], g_ref[:, cols], part)
+            place = slice(t % 2 * rows, (t % 2 + 1) * rows)
+            outs[t // 2][place, cols] = finish(rest[rows:, cols], g_ref[:, cols], part)
 
 
 def multiplicity(lists, valid, me, tiles):
@@ -185,7 +186,7 @@
             table = table
         results = pl.pallas_call(
             functools.partial(relay_kernel, first, half, block),
-            out_shape=[jax.ShapeDtypeStruct((rows, size * HEAD_DIM), jnp.bfloat16)] * 4,
+            out_shape=[jax.ShapeDtypeStruct((2 * rows, size * HEAD_DIM), jnp.bfloat16)] * 2,
             grid_spec=pltpu.PrefetchScalarGridSpec(
                 num_scalar_prefetch=1,
                 grid=(size // block,),
@@ -193,7 +194,7 @@
                     pl.BlockSpec((height, cols), lambda h, m, place=place, skip=skip: (place, skip + h))
                     for height, (_, place, skip) in zip(heights, inputs)
                 ],
-                out_specs=[pl.BlockSpec((rows, cols), lambda h, m: (0, h))] * 4,
+                out_specs=[pl.BlockSpec((2 * rows, cols), lambda h, m: (0, h))] * 2,
             ),
             cost_estimate=pl.CostEstimate(
                 flops=size * COST * rows * 8 * rows * HEAD_DIM,
@@ -202,12 +203,10 @@
             ),
         )(table, *(array for array, *_ in inputs))
         table = after(table, results[0])
-        sent = [
-            onto(part, piece, onward(change))
-            for piece, change in zip(results, (0, 1, 2, 3))
-        ]
-        same.append(jnp.where(inner, sent[0], sent[2]))
-        other.append(jnp.where(inner, sent[1], sent[3]))
+        sent = [onto(part, piece, onward(change)) for piece, change in zip(results, (0, 2))]
+        here = jnp.where(inner, *sent)
+        same.append(here[:rows])
+        other.append(ctx(here[rows:], swap, f"settle_{part}"))
     same, other = jnp.concatenate(same, axis=1), jnp.concatenate(other, axis=1)
     left, right = jnp.where(core == 0, same, other), jnp.where(core == 0, other, same)
     return jnp.concatenate([left, right], axis=1)[None]

time: 117 us -> 114 us (0.974)
  other arithmetic: 8.4 us -> 5.82 us
    ppermute x8 -> x4, waiting for transfers between devices: 16.7 us -> 14.5 us  [onto(): return lax.ppermute(block, ('pipe', 'ctx'), route)]
    ppermute x16 -> x18, waiting for transfers between devices: 40.5 us -> 42.4 us  [ctx(): return lax.ppermute(block, 'ctx', route)]
    ppermute x8 -> x4, starting transfers between devices: 13.4 us -> 12.6 us  [onto(): return lax.ppermute(block, ('pipe', 'ctx'), route)]
    ppermute x16 -> x18, starting transfers between devices: 17.3 us -> 17.5 us  [ctx(): return lax.ppermute(block, 'ctx', route)]
  transfers between devices with their start and end apart: 24 -> 22, of which waited for: 8 -> 8; matrix products, arithmetic and copies ran while one was open for 6% -> 5% of each run, Pallas kernels for 15% -> 16%
where the time goes in v5:
time: 114 us
  waiting for transfers between devices  56.9 us (50%)
  starting transfers between devices  30 us (26%)
  Pallas kernels  17.8 us (16%)
  other arithmetic  5.82 us (5%)
  local copies, waits for them, and re-layouts  3.25 us (3%)
    ppermute x18, waiting for transfers between devices, ctx(): return lax.ppermute(block, 'ctx', route)  42.4 us
    pallas_call x2, Pallas kernels, relay_section(): pl.pallas_call(functools.partial(relay_kernel, first, half, block), out_s...  17.8 us
    ppermute x18, starting transfers between devices, ctx(): return lax.ppermute(block, 'ctx', route)  17.5 us
    ppermute x4, waiting for transfers between devices, onto(): return lax.ppermute(block, ('pipe', 'ctx'), route)  14.5 us
    ppermute x4, starting transfers between devices, onto(): return lax.ppermute(block, ('pipe', 'ctx'), route)  12.6 us
  transfers between devices with their start and end apart: 22, of which 8 were waited for; matrix products, arithmetic and copies ran while one was open for 5% of the time, Pallas kernels for 16%

profile of v5, /device:TPU:0, one launch (start us, length us, event | category | flops | bytes accessed | tf_op | source)
XLA Modules:
  0.0 114.1 jit_solution(6638820554426590932)
XLA Ops:
  0.0 1.4 %broadcast_select_fusion.6 = (bf16[128,896]{1,0:T(8,128)(2,1)S(1)}, bf16[128,896]{1,0:T(8,128)(2,1)S(1)}, bf16[128,896]{1,0:T(8,128)(2,1)S(1)}, bf16[128,896]{1,0:T(8,128)(2,1)S(1)}) fusion(pred[]{:T(512)S(6)} %eq.27, bf16[128,3072]{1,0:T(8,128)(2,1)} %bitcast.20, bf16[128,3072]{1,0:T(8,128)(2,1)} %bitcast.22), kind=kLoop, calls=%fused_computation.18 | loop fusion | flops 458752 | bytes 1835009 | tf_op jit(solution)/shard_map/jit(_where)/select_n | solution.py:126
  1.5 0.5 collective-permute-start.3
  2.0 1.3 %broadcast_select_fusion.10 = (bf16[128,640]{1,0:T(8,128)(2,1)S(1)}, bf16[128,640]{1,0:T(8,128)(2,1)S(1)}, bf16[128,640]{1,0:T(8,128)(2,1)S(1)}, bf16[128,640]{1,0:T(8,128)(2,1)S(1)}) fusion(pred[]{:T(512)S(6)} %eq.27, bf16[128,3072]{1,0:T(8,128)(2,1)} %bitcast.21, bf16[128,3072]{1,0:T(8,128)(2,1)} %bitcast.23), kind=kLoop, calls=%fused_computation.22 | loop fusion | flops 327680 | bytes 1310721 | tf_op jit(solution)/shard_map/jit(_where)/select_n | solution.py:126
  3.3 0.3 broadcast_select_fusion.1
  3.6 0.1 pad_maximum_fusion
  3.7 0.5 collective-permute-start.10
  4.3 0.1 add_convert_fusion
  4.3 0.1 slice_select_fusion.1
  4.4 2.6 %collective-permute-start.2 = (f32[12,8]{0,1:T(8,128)S(1)}, f32[12,8]{0,1:T(8,128)S(1)}, u32[]{:S(2)}, u32[]{:S(2)}) collective-permute-start(f32[12,8]{0,1:T(8,128)S(1)} %get-tuple-element.44), channel_id=1, source_target_pairs={{0,3},{1,2},{2,1},{3,0},{4,7},{5,6},{6,5},{7,4},{8,11},{9,10},{10,... | collective-permute-start | bytes 1160 | tf_op jit(solution)/shard_map/table_end1/ppermute | solution.py:104
  7.1 0.4 collective-permute-start
  7.5 0.8 pad_maximum_fusion.5.refs_0_
  8.3 2.0 %collective-permute-start.4 = (bf16[256,896]{1,0:T(8,128)(2,1)}, bf16[256,896]{1,0:T(8,128)(2,1)}, u32[]{:S(2)}, u32[]{:S(2)}) collective-permute-start(bf16[256,896]{1,0:T(8,128)(2,1)} %pad_maximum_fusion.5.refs_0_), channel_id=1, source_target_pairs={{0,2},{1,3},{2,0},{3,1},{4,6},{5,7},{6,4},{7,5},{8,10},{9,11},{10,... | collective-permute-start | bytes 1376264 | tf_op jit(solution)/shard_map/end_a0/ppermute | solution.py:104
  10.4 0.1 pad_add_fusion
  10.4 0.1 add_multiply_fusion
  10.5 0.6 collective-permute-done.1
  11.1 2.9 %collective-permute-start.5 = (bf16[256,896]{1,0:T(8,128)(2,1)}, bf16[256,896]{1,0:T(8,128)(2,1)}, u32[]{:S(2)}, u32[]{:S(2)}) collective-permute-start(bf16[256,896]{1,0:T(8,128)(2,1)} %copy-done.5), channel_id=1, source_target_pairs={{0,3},{1,2},{2,1},{3,0},{4,7},{5,6},{6,5},{7,4},{8,11},{9,10},{10,... | collective-permute-start | bytes 1376264 | tf_op jit(solution)/shard_map/end_a1/ppermute | solution.py:104
  14.1 7.9 %collective-permute-done.4.refs_2_ = bf16[256,896]{1,0:T(8,128)(2,1)} collective-permute-done((bf16[256,896]{1,0:T(8,128)(2,1)}, bf16[256,896]{1,0:T(8,128)(2,1)}, u32[]{:S(2)}, u32[]{:S(2)}) %collective-permute-start.4) | collective-permute-done | bytes 458784 | tf_op jit(solution)/shard_map/end_a0/ppermute | solution.py:104
  22.0 2.1 %collective-permute-start.14 = (bf16[512,640]{1,0:T(8,128)(2,1)S(1)}, bf16[512,640]{1,0:T(8,128)(2,1)}, u32[]{:S(2)}, u32[]{:S(2)}) collective-permute-start(bf16[512,640]{1,0:T(8,128)(2,1)S(1)} %pad_maximum_fusion.3.refs_0_.refs_1_), channel_id=1, source_target_pairs={{0,2},{1,3},{2,0},{3,1},{4,6},{5,7},{6,4},{7,5},{8,10},{9,11},{10,... | collective-permute-start | bytes 1966088 | tf_op jit(solution)/shard_map/end_b/ppermute | solution.py:104
  24.1 0.1 broadcast_add_fusion
  24.2 0.1 add.37
  24.3 0.1 pad_maximum_fusion.1.refs_8_.refs_9_
  24.4 7.0 %collective-permute-done.5.refs_3_ = bf16[256,896]{1,0:T(8,128)(2,1)} collective-permute-done((bf16[256,896]{1,0:T(8,128)(2,1)}, bf16[256,896]{1,0:T(8,128)(2,1)}, u32[]{:S(2)}, u32[]{:S(2)}) %collective-permute-start.5) | collective-permute-done | bytes 458784 | tf_op jit(solution)/shard_map/end_a1/ppermute | solution.py:104
  31.4 0.1 collective-permute-start.11
  31.5 2.0 %collective-permute-start.8 = (bf16[256,896]{1,0:T(8,128)(2,1)}, bf16[256,896]{1,0:T(8,128)(2,1)}, u32[]{:S(2)}, u32[]{:S(2)}) collective-permute-start(bf16[256,896]{1,0:T(8,128)(2,1)} %collective-permute-done.4.refs_2_), channel_id=1, source_target_pairs={{2,4},{3,5},{4,2},{5,3},{0,1},{1,0},{6,7},{7,6},{10,12},{11,13},{1... | collective-permute-start | bytes 1376264 | tf_op jit(solution)/shard_map/far_a0/ppermute | solution.py:104
  33.5 12.4 %collective-permute-done.14.refs_2_.refs_3_ = bf16[512,640]{1,0:T(8,128)(2,1)} collective-permute-done((bf16[512,640]{1,0:T(8,128)(2,1)S(1)}, bf16[512,640]{1,0:T(8,128)(2,1)}, u32[]{:S(2)}, u32[]{:S(2)}) %collective-permute-start.14) | collective-permute-done | bytes 655392 | tf_op jit(solution)/shard_map/end_b/ppermute | solution.py:104
  45.9 0.1 iota_compare_fusion.2
  46.0 0.6 slice.101.refs_12_
  46.6 0.6 slice.106.refs_12_
  47.2 0.1 select_reduce_fusion
  47.3 0.1 copy.12
  47.4 0.7 reshape.114.mult_ref
  48.2 0.6 collective-permute-start.15
  48.7 3.6 %collective-permute-start.17 = (bf16[512,640]{1,0:T(8,128)(2,1)S(1)}, bf16[512,640]{1,0:T(8,128)(2,1)}, u32[]{:S(2)}, u32[]{:S(2)}) collective-permute-start(bf16[512,640]{1,0:T(8,128)(2,1)S(1)} %pad_maximum_fusion.4.refs_8_.refs_9_), channel_id=1, source_target_pairs={{0,2},{1,3},{2,0},{3,1},{4,6},{5,7},{6,4},{7,5},{8,10},{9,11},{10,... | collective-permute-start | bytes 1966088 | tf_op jit(solution)/shard_map/qr_b/ppermute | solution.py:104
  52.3 13.2 %collective-permute-done.11.refs_10_.refs_11_ = bf16[512,896]{1,0:T(8,128)(2,1)} collective-permute-done((bf16[512,896]{1,0:T(8,128)(2,1)S(1)}, bf16[512,896]{1,0:T(8,128)(2,1)}, u32[]{:S(2)}, u32[]{:S(2)}) %collective-permute-start.11) | collective-permute-done | bytes 917536 | tf_op jit(solution)/shard_map/qr_a/ppermute | solution.py:104
  65.6 9.9 %shard_map.73 = (bf16[256,896]{1,0:T(8,128)(2,1)}, bf16[256,896]{1,0:T(8,128)(2,1)}) custom-call(f32[384]{0:T(512)} %reshape.114.mult_ref, bf16[256,896]{1,0:T(8,128)(2,1)} %pad_maximum_fusion.5.refs_0_, bf16[256,896]{1,0:T(8,128)(2,1)} %copy-done.9, bf16[256,896]{1,0:T(8,128)(2,1)} %collective-permute-done.4.refs_2_, ...), custom_call_target="tpu_custom_call" | custom-call | flops 11274289152 | bytes 6422528 | tf_op jit(solution)/shard_map/pallas_call | solution.py:187
  75.5 2.0 %collective-permute-start.12 = (bf16[256,896]{1,0:T(8,128)(2,1)}, bf16[256,896]{1,0:T(8,128)(2,1)S(1)}, u32[]{:S(2)}, u32[]{:S(2)}) collective-permute-start(bf16[256,896]{1,0:T(8,128)(2,1)} %get-tuple-element.18), channel_id=1, source_target_pairs={{0,8},{1,9},{2,10},{3,11},{4,12},{5,13},{6,14},{7,15},{8,16},{9,17... | collective-permute-start | bytes 1376264 | tf_op jit(solution)/shard_map/onto_0/ppermute | solution.py:108
  77.5 2.5 %collective-permute-start.13 = (bf16[256,896]{1,0:T(8,128)(2,1)}, bf16[256,896]{1,0:T(8,128)(2,1)S(1)}, u32[]{:S(2)}, u32[]{:S(2)}) collective-permute-start(bf16[256,896]{1,0:T(8,128)(2,1)} %get-tuple-element.19), channel_id=1, source_target_pairs={{0,10},{1,11},{2,8},{3,9},{4,14},{5,15},{6,12},{7,13},{8,18},{9,19... | collective-permute-start | bytes 1376264 | tf_op jit(solution)/shard_map/onto_0/ppermute | solution.py:108
  80.0 0.8 copy-done.8
  80.8 7.9 %shard_map.74 = (bf16[256,640]{1,0:T(8,128)(2,1)}, bf16[256,640]{1,0:T(8,128)(2,1)}) custom-call(f32[384]{0:T(512)} %reshape.114.mult_ref, bf16[512,640]{1,0:T(8,128)(2,1)} %copy-done.3, bf16[512,640]{1,0:T(8,128)(2,1)} %copy-done.3, bf16[512,640]{1,0:T(8,128)(2,1)} %collective-permute-done.14.refs_2_.refs_3_, ...), custom_call_target="tpu_custom_call" | custom-call | flops 8053063680 | bytes 4587520 | tf_op jit(solution)/shard_map/pallas_call | solution.py:187
  88.7 1.5 %collective-permute-start.18 = (bf16[256,640]{1,0:T(8,128)(2,1)}, bf16[256,640]{1,0:T(8,128)(2,1)S(1)}, u32[]{:S(2)}, u32[]{:S(2)}) collective-permute-start(bf16[256,640]{1,0:T(8,128)(2,1)} %get-tuple-element.23), channel_id=1, source_target_pairs={{0,8},{1,9},{2,10},{3,11},{4,12},{5,13},{6,14},{7,15},{8,16},{9,17... | collective-permute-start | bytes 983048 | tf_op jit(solution)/shard_map/onto_1/ppermute | solution.py:108
  90.2 6.6 %collective-permute-start.19 = (bf16[256,640]{1,0:T(8,128)(2,1)}, bf16[256,640]{1,0:T(8,128)(2,1)S(1)}, u32[]{:S(2)}, u32[]{:S(2)}) collective-permute-start(bf16[256,640]{1,0:T(8,128)(2,1)} %get-tuple-element.24), channel_id=1, source_target_pairs={{0,10},{1,11},{2,8},{3,9},{4,14},{5,15},{6,12},{7,13},{8,18},{9,19... | collective-permute-start | bytes 983048 | tf_op jit(solution)/shard_map/onto_1/ppermute | solution.py:108
  96.8 9.8 %collective-permute-done.12 = bf16[256,896]{1,0:T(8,128)(2,1)S(1)} collective-permute-done((bf16[256,896]{1,0:T(8,128)(2,1)}, bf16[256,896]{1,0:T(8,128)(2,1)S(1)}, u32[]{:S(2)}, u32[]{:S(2)}) %collective-permute-start.12) | collective-permute-done | bytes 458784 | tf_op jit(solution)/shard_map/onto_0/ppermute | solution.py:108
  106.7 0.1 collective-permute-start.20
  106.8 4.6 %collective-permute-done.18 = bf16[256,640]{1,0:T(8,128)(2,1)S(1)} collective-permute-done((bf16[256,640]{1,0:T(8,128)(2,1)}, bf16[256,640]{1,0:T(8,128)(2,1)S(1)}, u32[]{:S(2)}, u32[]{:S(2)}) %collective-permute-start.18) | collective-permute-done | bytes 327712 | tf_op jit(solution)/shard_map/onto_1/ppermute | solution.py:108
  111.5 0.1 collective-permute-start.21
  111.6 1.3 %collective-permute-done.21 = bf16[128,640]{1,0:T(8,128)(2,1)S(1)} collective-permute-done((bf16[128,640]{1,0:T(8,128)(2,1)S(1)}, bf16[128,640]{1,0:T(8,128)(2,1)S(1)}, u32[]{:S(2)}, u32[]{:S(2)}) %collective-permute-start.21) | collective-permute-done | bytes 163872 | tf_op jit(solution)/shard_map/settle_1/ppermute | solution.py:104
  113.0 0.1 broadcast_select_fusion.4
  113.1 1.0 maximum_bitcast_fusion
  (59 shorter events, 0.7 us)
Async XLA Ops:
  1.4 1.9 %copy-start.7 = (s32[1,1,24,5]{2,1,3,0:T(1,128)S(1)}, s32[1,1,24,5]{2,1,3,0:T(1,128)}, u32[]{:S(2)}) copy-start(s32[1,1,24,5]{2,1,3,0:T(1,128)} %param.12) | copy-start | bytes 1444
  1.4 1.9 %copy-start.1 = (bf16[1,128,3072]{2,1,0:T(8,128)(2,1)S(1)}, bf16[1,128,3072]{2,1,0:T(8,128)(2,1)}, u32[]{:S(2)}) copy-start(bf16[1,128,3072]{2,1,0:T(8,128)(2,1)} %param.10) | copy-start | bytes 2359300
  1.4 1.9 %copy-start.2 = (bf16[1,128,3072]{2,1,0:T(8,128)(2,1)S(1)}, bf16[1,128,3072]{2,1,0:T(8,128)(2,1)}, u32[]{:S(2)}) copy-start(bf16[1,128,3072]{2,1,0:T(8,128)(2,1)} %param.7) | copy-start | bytes 2359300
  1.5 2.1 %copy-start.5 = (bf16[256,896]{1,0:T(8,128)(2,1)}, bf16[256,896]{1,0:T(8,128)(2,1)S(1)}, u32[]{:S(2)}) copy-start(bf16[256,896]{1,0:T(8,128)(2,1)S(1)} %pad_maximum_fusion.6) | copy-start | bytes 1376260
  1.5 2.2 %collective-permute-start.3 = (bf16[256,896]{1,0:T(8,128)(2,1)S(1)}, bf16[256,896]{1,0:T(8,128)(2,1)S(1)}, u32[]{:S(2)}, u32[]{:S(2)}) collective-permute-start(bf16[256,896]{1,0:T(8,128)(2,1)S(1)} %pad_maximum_fusion.6), channel_id=1, source_target_pairs={{0,1},{1,0},{2,3},{3,2},{4,5},{5,4},{6,7},{7,6},{8,9},{9,8},{10,11... | collective-permute-start | bytes 1376264 | tf_op jit(solution)/shard_map/swap_a/ppermute | solution.py:104
  3.6 0.7 copy-start.10
  3.7 4.6 %copy-start.9 = (bf16[256,896]{1,0:T(8,128)(2,1)}, bf16[256,896]{1,0:T(8,128)(2,1)S(1)}, u32[]{:S(2)}) copy-start(bf16[256,896]{1,0:T(8,128)(2,1)S(1)} %collective-permute-done.3.refs_1_) | copy-start | bytes 1376260
  3.7 10.3 %collective-permute-start.10 = (bf16[256,2176]{1,0:T(8,128)(2,1)S(1)}, bf16[256,2176]{1,0:T(8,128)(2,1)S(1)}, u32[]{:S(2)}, u32[]{:S(2)}) collective-permute-start(bf16[256,2176]{1,0:T(8,128)(2,1)S(1)} %pad_maximum_fusion), channel_id=1, source_target_pairs={{0,1},{1,0},{2,3},{3,2},{4,5},{5,4},{6,7},{7,6},{8,9},{9,8},{10,11... | collective-permute-start | bytes 3342344 | tf_op jit(solution)/shard_map/swap_rest/ppermute | solution.py:104
  4.4 6.1 %collective-permute-start.2 = (f32[12,8]{0,1:T(8,128)S(1)}, f32[12,8]{0,1:T(8,128)S(1)}, u32[]{:S(2)}, u32[]{:S(2)}) collective-permute-start(f32[12,8]{0,1:T(8,128)S(1)} %get-tuple-element.44), channel_id=1, source_target_pairs={{0,3},{1,2},{2,1},{3,0},{4,7},{5,6},{6,5},{7,4},{8,11},{9,10},{10,... | collective-permute-start | bytes 1160 | tf_op jit(solution)/shard_map/table_end1/ppermute | solution.py:104
  7.1 4.1 %collective-permute-start = (f32[12,8]{0,1:T(8,128)S(1)}, f32[12,8]{0,1:T(8,128)S(1)}, u32[]{:S(2)}, u32[]{:S(2)}) collective-permute-start(f32[12,8]{0,1:T(8,128)S(1)} %get-tuple-element.44), channel_id=1, source_target_pairs={{0,1},{1,0},{2,3},{3,2},{4,5},{5,4},{6,7},{7,6},{8,9},{9,8},{10,11... | collective-permute-start | bytes 1160 | tf_op jit(solution)/shard_map/table_swap/ppermute | solution.py:104
  7.5 3.6 %collective-permute-start.1 = (f32[12,8]{0,1:T(8,128)S(1)}, f32[12,8]{0,1:T(8,128)S(1)}, u32[]{:S(2)}, u32[]{:S(2)}) collective-permute-start(f32[12,8]{0,1:T(8,128)S(1)} %get-tuple-element.43), channel_id=1, source_target_pairs={{0,2},{1,3},{2,0},{3,1},{4,6},{5,7},{6,4},{7,5},{8,10},{9,11},{10,... | collective-permute-start | bytes 1160 | tf_op jit(solution)/shard_map/table_end0/ppermute | solution.py:104
  8.3 13.7 %collective-permute-start.4 = (bf16[256,896]{1,0:T(8,128)(2,1)}, bf16[256,896]{1,0:T(8,128)(2,1)}, u32[]{:S(2)}, u32[]{:S(2)}) collective-permute-start(bf16[256,896]{1,0:T(8,128)(2,1)} %pad_maximum_fusion.5.refs_0_), channel_id=1, source_target_pairs={{0,2},{1,3},{2,0},{3,1},{4,6},{5,7},{6,4},{7,5},{8,10},{9,11},{10,... | collective-permute-start | bytes 1376264 | tf_op jit(solution)/shard_map/end_a0/ppermute | solution.py:104
  10.5 37.6 %collective-permute-start.6 = (bf16[256,896]{1,0:T(8,128)(2,1)}, bf16[256,896]{1,0:T(8,128)(2,1)}, u32[]{:S(2)}, u32[]{:S(2)}) collective-permute-start(bf16[256,896]{1,0:T(8,128)(2,1)} %pad_maximum_fusion.5.refs_0_), channel_id=1, source_target_pairs={{2,4},{3,5},{4,2},{5,3},{0,1},{1,0},{6,7},{7,6},{10,12},{11,13},{1... | collective-permute-start | bytes 1376264 | tf_op jit(solution)/shard_map/near_a0/ppermute | solution.py:104
  11.1 37.6 %collective-permute-start.7 = (bf16[256,896]{1,0:T(8,128)(2,1)}, bf16[256,896]{1,0:T(8,128)(2,1)}, u32[]{:S(2)}, u32[]{:S(2)}) collective-permute-start(bf16[256,896]{1,0:T(8,128)(2,1)} %copy-done.5), channel_id=1, source_target_pairs={{2,5},{3,4},{4,3},{5,2},{0,1},{1,0},{6,7},{7,6},{10,13},{11,12},{1... | collective-permute-start | bytes 1376264 | tf_op jit(solution)/shard_map/near_a1/ppermute | solution.py:104
  11.1 20.3 %collective-permute-start.5 = (bf16[256,896]{1,0:T(8,128)(2,1)}, bf16[256,896]{1,0:T(8,128)(2,1)}, u32[]{:S(2)}, u32[]{:S(2)}) collective-permute-start(bf16[256,896]{1,0:T(8,128)(2,1)} %copy-done.5), channel_id=1, source_target_pairs={{0,3},{1,2},{2,1},{3,0},{4,7},{5,6},{6,5},{7,4},{8,11},{9,10},{10,... | collective-permute-start | bytes 1376264 | tf_op jit(solution)/shard_map/end_a1/ppermute | solution.py:104
  14.1 34.0 %copy-start.3 = (bf16[512,640]{1,0:T(8,128)(2,1)}, bf16[512,640]{1,0:T(8,128)(2,1)S(1)}, u32[]{:S(2)}) copy-start(bf16[512,640]{1,0:T(8,128)(2,1)S(1)} %pad_maximum_fusion.3.refs_0_.refs_1_) | copy-start | bytes 1966084
  22.0 23.9 %collective-permute-start.14 = (bf16[512,640]{1,0:T(8,128)(2,1)S(1)}, bf16[512,640]{1,0:T(8,128)(2,1)}, u32[]{:S(2)}, u32[]{:S(2)}) collective-permute-start(bf16[512,640]{1,0:T(8,128)(2,1)S(1)} %pad_maximum_fusion.3.refs_0_.refs_1_), channel_id=1, source_target_pairs={{0,2},{1,3},{2,0},{3,1},{4,6},{5,7},{6,4},{7,5},{8,10},{9,11},{10,... | collective-permute-start | bytes 1966088 | tf_op jit(solution)/shard_map/end_b/ppermute | solution.py:104
  24.3 7.2 %copy-start.6 = (f32[1,3072]{1,0:T(1,128)S(1)}, f32[1,3072]{1,0:T(1,128)}, u32[]{:S(2)}) copy-start(f32[1,3072]{1,0:T(1,128)} %param.11) | copy-start | bytes 36868
  24.4 41.1 %copy-start = (bf16[512,896]{1,0:T(8,128)(2,1)}, bf16[512,896]{1,0:T(8,128)(2,1)S(1)}, u32[]{:S(2)}) copy-start(bf16[512,896]{1,0:T(8,128)(2,1)S(1)} %pad_maximum_fusion.1.refs_8_.refs_9_) | copy-start | bytes 2752516
  31.4 34.1 %collective-permute-start.11 = (bf16[512,896]{1,0:T(8,128)(2,1)S(1)}, bf16[512,896]{1,0:T(8,128)(2,1)}, u32[]{:S(2)}, u32[]{:S(2)}) collective-permute-start(bf16[512,896]{1,0:T(8,128)(2,1)S(1)} %pad_maximum_fusion.1.refs_8_.refs_9_), channel_id=1, source_target_pairs={{0,2},{1,3},{2,0},{3,1},{4,6},{5,7},{6,4},{7,5},{8,10},{9,11},{10,... | collective-permute-start | bytes 2752520 | tf_op jit(solution)/shard_map/qr_a/ppermute | solution.py:104
  31.5 20.8 %collective-permute-start.8 = (bf16[256,896]{1,0:T(8,128)(2,1)}, bf16[256,896]{1,0:T(8,128)(2,1)}, u32[]{:S(2)}, u32[]{:S(2)}) collective-permute-start(bf16[256,896]{1,0:T(8,128)(2,1)} %collective-permute-done.4.refs_2_), channel_id=1, source_target_pairs={{2,4},{3,5},{4,2},{5,3},{0,1},{1,0},{6,7},{7,6},{10,12},{11,13},{1... | collective-permute-start | bytes 1376264 | tf_op jit(solution)/shard_map/far_a0/ppermute | solution.py:104
  45.9 6.4 %collective-permute-start.9 = (bf16[256,896]{1,0:T(8,128)(2,1)}, bf16[256,896]{1,0:T(8,128)(2,1)}, u32[]{:S(2)}, u32[]{:S(2)}) collective-permute-start(bf16[256,896]{1,0:T(8,128)(2,1)} %collective-permute-done.5.refs_3_), channel_id=1, source_target_pairs={{2,4},{3,5},{4,2},{5,3},{0,1},{1,0},{6,7},{7,6},{10,12},{11,13},{1... | collective-permute-start | bytes 1376264 | tf_op jit(solution)/shard_map/far_a1/ppermute | solution.py:104
  48.1 27.3 %copy-start.4 = (bf16[512,640]{1,0:T(8,128)(2,1)}, bf16[512,640]{1,0:T(8,128)(2,1)S(1)}, u32[]{:S(2)}) copy-start(bf16[512,640]{1,0:T(8,128)(2,1)S(1)} %pad_maximum_fusion.4.refs_8_.refs_9_) | copy-start | bytes 1966084
  48.2 31.8 %collective-permute-start.15 = (bf16[512,640]{1,0:T(8,128)(2,1)S(1)}, bf16[512,640]{1,0:T(8,128)(2,1)S(1)}, u32[]{:S(2)}, u32[]{:S(2)}) collective-permute-start(bf16[512,640]{1,0:T(8,128)(2,1)S(1)} %pad_maximum_fusion.3.refs_0_.refs_1_), channel_id=1, source_target_pairs={{2,4},{3,5},{4,2},{5,3},{0,1},{1,0},{6,7},{7,6},{10,12},{11,13},{1... | collective-permute-start | bytes 1966088 | tf_op jit(solution)/shard_map/near_b/ppermute | solution.py:104
  48.7 31.2 %collective-permute-start.17 = (bf16[512,640]{1,0:T(8,128)(2,1)S(1)}, bf16[512,640]{1,0:T(8,128)(2,1)}, u32[]{:S(2)}, u32[]{:S(2)}) collective-permute-start(bf16[512,640]{1,0:T(8,128)(2,1)S(1)} %pad_maximum_fusion.4.refs_8_.refs_9_), channel_id=1, source_target_pairs={{0,2},{1,3},{2,0},{3,1},{4,6},{5,7},{6,4},{7,5},{8,10},{9,11},{10,... | collective-permute-start | bytes 1966088 | tf_op jit(solution)/shard_map/qr_b/ppermute | solution.py:104
  52.3 27.6 %collective-permute-start.16 = (bf16[512,640]{1,0:T(8,128)(2,1)}, bf16[512,640]{1,0:T(8,128)(2,1)}, u32[]{:S(2)}, u32[]{:S(2)}) collective-permute-start(bf16[512,640]{1,0:T(8,128)(2,1)} %collective-permute-done.14.refs_2_.refs_3_), channel_id=1, source_target_pairs={{2,4},{3,5},{4,2},{5,3},{0,1},{1,0},{6,7},{7,6},{10,12},{11,13},{1... | collective-permute-start | bytes 1966088 | tf_op jit(solution)/shard_map/far_b/ppermute | solution.py:104
  75.5 31.1 %collective-permute-start.12 = (bf16[256,896]{1,0:T(8,128)(2,1)}, bf16[256,896]{1,0:T(8,128)(2,1)S(1)}, u32[]{:S(2)}, u32[]{:S(2)}) collective-permute-start(bf16[256,896]{1,0:T(8,128)(2,1)} %get-tuple-element.18), channel_id=1, source_target_pairs={{0,8},{1,9},{2,10},{3,11},{4,12},{5,13},{6,14},{7,15},{8,16},{9,17... | collective-permute-start | bytes 1376264 | tf_op jit(solution)/shard_map/onto_0/ppermute | solution.py:108
  77.5 29.1 %collective-permute-start.13 = (bf16[256,896]{1,0:T(8,128)(2,1)}, bf16[256,896]{1,0:T(8,128)(2,1)S(1)}, u32[]{:S(2)}, u32[]{:S(2)}) collective-permute-start(bf16[256,896]{1,0:T(8,128)(2,1)} %get-tuple-element.19), channel_id=1, source_target_pairs={{0,10},{1,11},{2,8},{3,9},{4,14},{5,15},{6,12},{7,13},{8,18},{9,19... | collective-permute-start | bytes 1376264 | tf_op jit(solution)/shard_map/onto_0/ppermute | solution.py:108
  80.0 0.8 copy-start.8
  88.7 22.7 %collective-permute-start.18 = (bf16[256,640]{1,0:T(8,128)(2,1)}, bf16[256,640]{1,0:T(8,128)(2,1)S(1)}, u32[]{:S(2)}, u32[]{:S(2)}) collective-permute-start(bf16[256,640]{1,0:T(8,128)(2,1)} %get-tuple-element.23), channel_id=1, source_target_pairs={{0,8},{1,9},{2,10},{3,11},{4,12},{5,13},{6,14},{7,15},{8,16},{9,17... | collective-permute-start | bytes 983048 | tf_op jit(solution)/shard_map/onto_1/ppermute | solution.py:108
  90.2 21.3 %collective-permute-start.19 = (bf16[256,640]{1,0:T(8,128)(2,1)}, bf16[256,640]{1,0:T(8,128)(2,1)S(1)}, u32[]{:S(2)}, u32[]{:S(2)}) collective-permute-start(bf16[256,640]{1,0:T(8,128)(2,1)} %get-tuple-element.24), channel_id=1, source_target_pairs={{0,10},{1,11},{2,8},{3,9},{4,14},{5,15},{6,12},{7,13},{8,18},{9,19... | collective-permute-start | bytes 983048 | tf_op jit(solution)/shard_map/onto_1/ppermute | solution.py:108
  106.7 4.9 %collective-permute-start.20 = (bf16[128,896]{1,0:T(8,128)(2,1)S(1)}, bf16[128,896]{1,0:T(8,128)(2,1)S(1)}, u32[]{:S(2)}, u32[]{:S(2)}) collective-permute-start(bf16[128,896]{1,0:T(8,128)(2,1)S(1)} %get-tuple-element.40), channel_id=1, source_target_pairs={{0,1},{1,0},{2,3},{3,2},{4,5},{5,4},{6,7},{7,6},{8,9},{9,8},{10,11... | collective-permute-start | bytes 688136 | tf_op jit(solution)/shard_map/settle_0/ppermute | solution.py:104
  111.5 1.5 %collective-permute-start.21 = (bf16[128,640]{1,0:T(8,128)(2,1)S(1)}, bf16[128,640]{1,0:T(8,128)(2,1)S(1)}, u32[]{:S(2)}, u32[]{:S(2)}) collective-permute-start(bf16[128,640]{1,0:T(8,128)(2,1)S(1)} %get-tuple-element.42), channel_id=1, source_target_pairs={{0,1},{1,0},{2,3},{3,2},{4,5},{5,4},{6,7},{7,6},{8,9},{9,8},{10,11... | collective-permute-start | bytes 491528 | tf_op jit(solution)/shard_map/settle_1/ppermute | solution.py:104

commit v6 on v5

--- a/solution.py
+++ b/solution.py
@@ -92,11 +92,14 @@
     inward, inward_x = ([(i, i ^ change) for i in range(8)] for change in (2, 3))
     across, across_x = ([(i, (i ^ 6) ^ change) for i in (2, 3, 4, 5)] + idle for change in (0, 1))
 
-    def onward(change):
+    outward = [(i, i ^ 2) for i in (2, 3, 4, 5)]
+
+    def onward(change, chips=(0, 1, 2, 3)):
         return [
             (p * tiles + i, (p + 1) % sections * tiles + (i ^ change))
             for p in range(sections)
             for i in range(tiles)
+            if i // 2 in chips
         ]
 
     def ctx(block, route, name):
@@ -203,7 +206,11 @@
             ),
         )(table, *(array for array, *_ in inputs))
         table = after(table, results[0])
-        sent = [onto(part, piece, onward(change)) for piece, change in zip(results, (0, 2))]
+        if part == 0:
+            sent = [onto(part, piece, onward(change)) for piece, change in zip(results, (0, 2))]
+        else:
+            back = ctx(results[1], outward, "back")
+            sent = [onto(part, results[0], onward(0, (1, 2))), onto(part, back, onward(0, (0, 3)))]
         here = jnp.where(inner, *sent)
         same.append(here[:rows])
         other.append(ctx(here[rows:], swap, f"settle_{part}"))

time: 114 us -> 114 us (level)
  starting transfers between devices: 30 us -> 27.3 us
  waiting for transfers between devices: 56.9 us -> 58.8 us
    ppermute x18 -> x19, waiting for transfers between devices: 42.4 us -> 52.6 us  [ctx(): return lax.ppermute(block, 'ctx', route)]
    ppermute x4, waiting for transfers between devices: 14.5 us -> 6.25 us  [onto(): return lax.ppermute(block, ('pipe', 'ctx'), route)]
    ppermute x4, starting transfers between devices: 12.6 us -> 8.56 us  [onto(): return lax.ppermute(block, ('pipe', 'ctx'), route)]
    ppermute x18 -> x19, starting transfers between devices: 17.5 us -> 18.7 us  [ctx(): return lax.ppermute(block, 'ctx', route)]
  transfers between devices with their start and end apart: 22 -> 23, of which waited for: 8 -> 8; matrix products, arithmetic and copies ran while one was open for 5% -> 5% of each run, Pallas kernels for 16% -> 16%
where the time goes in v6:
time: 114 us; the launch traced here: 113 us
  waiting for transfers between devices  58.8 us (52%)
  starting transfers between devices  27.3 us (24%)
  Pallas kernels  17.8 us (16%)
  other arithmetic  5.83 us (5%)
  local copies, waits for them, and re-layouts  3.28 us (3%)
    ppermute x19, waiting for transfers between devices, ctx(): return lax.ppermute(block, 'ctx', route)  52.6 us
    ppermute x19, starting transfers between devices, ctx(): return lax.ppermute(block, 'ctx', route)  18.7 us
    pallas_call x2, Pallas kernels, relay_section(): pl.pallas_call(functools.partial(relay_kernel, first, half, block), out_s...  17.8 us
    ppermute x4, starting transfers between devices, onto(): return lax.ppermute(block, ('pipe', 'ctx'), route)  8.56 us
    ppermute x4, waiting for transfers between devices, onto(): return lax.ppermute(block, ('pipe', 'ctx'), route)  6.25 us
  transfers between devices with their start and end apart: 23, of which 8 were waited for; matrix products, arithmetic and copies ran while one was open for 5% of the time, Pallas kernels for 16%

profile of v6, /device:TPU:0, one launch (start us, length us, event | category | flops | bytes accessed | tf_op | source)
XLA Modules:
  0.0 113.4 jit_solution(6237524889716446439)
XLA Ops:
  0.0 1.4 %broadcast_select_fusion.6 = (bf16[128,896]{1,0:T(8,128)(2,1)S(1)}, bf16[128,896]{1,0:T(8,128)(2,1)S(1)}, bf16[128,896]{1,0:T(8,128)(2,1)S(1)}, bf16[128,896]{1,0:T(8,128)(2,1)S(1)}) fusion(pred[]{:T(512)S(6)} %eq.27, bf16[128,3072]{1,0:T(8,128)(2,1)} %bitcast.20, bf16[128,3072]{1,0:T(8,128)(2,1)} %bitcast.22), kind=kLoop, calls=%fused_computation.18 | loop fusion | flops 458752 | bytes 1835009 | tf_op jit(solution)/shard_map/jit(_where)/select_n | solution.py:129
  1.5 0.5 collective-permute-start.3
  2.0 1.3 %broadcast_select_fusion.10 = (bf16[128,640]{1,0:T(8,128)(2,1)S(1)}, bf16[128,640]{1,0:T(8,128)(2,1)S(1)}, bf16[128,640]{1,0:T(8,128)(2,1)S(1)}, bf16[128,640]{1,0:T(8,128)(2,1)S(1)}) fusion(pred[]{:T(512)S(6)} %eq.27, bf16[128,3072]{1,0:T(8,128)(2,1)} %bitcast.21, bf16[128,3072]{1,0:T(8,128)(2,1)} %bitcast.23), kind=kLoop, calls=%fused_computation.22 | loop fusion | flops 327680 | bytes 1310721 | tf_op jit(solution)/shard_map/jit(_where)/select_n | solution.py:129
  3.3 0.3 broadcast_select_fusion.1
  3.6 0.1 pad_maximum_fusion
  3.7 0.5 collective-permute-start.10
  4.3 0.1 add_convert_fusion
  4.3 0.1 slice_select_fusion.1
  4.4 2.6 %collective-permute-start.2 = (f32[12,8]{0,1:T(8,128)S(1)}, f32[12,8]{0,1:T(8,128)S(1)}, u32[]{:S(2)}, u32[]{:S(2)}) collective-permute-start(f32[12,8]{0,1:T(8,128)S(1)} %get-tuple-element.44), channel_id=1, source_target_pairs={{0,3},{1,2},{2,1},{3,0},{4,7},{5,6},{6,5},{7,4},{8,11},{9,10},{10,... | collective-permute-start | bytes 1160 | tf_op jit(solution)/shard_map/table_end1/ppermute | solution.py:107
  7.1 0.4 collective-permute-start
  7.5 0.8 pad_maximum_fusion.5.refs_0_
  8.3 2.0 %collective-permute-start.4 = (bf16[256,896]{1,0:T(8,128)(2,1)}, bf16[256,896]{1,0:T(8,128)(2,1)}, u32[]{:S(2)}, u32[]{:S(2)}) collective-permute-start(bf16[256,896]{1,0:T(8,128)(2,1)} %pad_maximum_fusion.5.refs_0_), channel_id=1, source_target_pairs={{0,2},{1,3},{2,0},{3,1},{4,6},{5,7},{6,4},{7,5},{8,10},{9,11},{10,... | collective-permute-start | bytes 1376264 | tf_op jit(solution)/shard_map/end_a0/ppermute | solution.py:107
  10.4 0.1 pad_add_fusion
  10.4 0.1 add_multiply_fusion
  10.5 0.6 collective-permute-done.1
  11.1 2.9 %collective-permute-start.5 = (bf16[256,896]{1,0:T(8,128)(2,1)}, bf16[256,896]{1,0:T(8,128)(2,1)}, u32[]{:S(2)}, u32[]{:S(2)}) collective-permute-start(bf16[256,896]{1,0:T(8,128)(2,1)} %copy-done.5), channel_id=1, source_target_pairs={{0,3},{1,2},{2,1},{3,0},{4,7},{5,6},{6,5},{7,4},{8,11},{9,10},{10,... | collective-permute-start | bytes 1376264 | tf_op jit(solution)/shard_map/end_a1/ppermute | solution.py:107
  14.1 7.9 %collective-permute-done.4.refs_2_ = bf16[256,896]{1,0:T(8,128)(2,1)} collective-permute-done((bf16[256,896]{1,0:T(8,128)(2,1)}, bf16[256,896]{1,0:T(8,128)(2,1)}, u32[]{:S(2)}, u32[]{:S(2)}) %collective-permute-start.4) | collective-permute-done | bytes 458784 | tf_op jit(solution)/shard_map/end_a0/ppermute | solution.py:107
  22.0 2.1 %collective-permute-start.14 = (bf16[512,640]{1,0:T(8,128)(2,1)S(1)}, bf16[512,640]{1,0:T(8,128)(2,1)}, u32[]{:S(2)}, u32[]{:S(2)}) collective-permute-start(bf16[512,640]{1,0:T(8,128)(2,1)S(1)} %pad_maximum_fusion.3.refs_0_.refs_1_), channel_id=1, source_target_pairs={{0,2},{1,3},{2,0},{3,1},{4,6},{5,7},{6,4},{7,5},{8,10},{9,11},{10,... | collective-permute-start | bytes 1966088 | tf_op jit(solution)/shard_map/end_b/ppermute | solution.py:107
  24.1 0.1 broadcast_add_fusion
  24.2 0.1 add.37
  24.4 0.1 pad_maximum_fusion.1.refs_8_.refs_9_
  24.4 7.0 %collective-permute-done.5.refs_3_ = bf16[256,896]{1,0:T(8,128)(2,1)} collective-permute-done((bf16[256,896]{1,0:T(8,128)(2,1)}, bf16[256,896]{1,0:T(8,128)(2,1)}, u32[]{:S(2)}, u32[]{:S(2)}) %collective-permute-start.5) | collective-permute-done | bytes 458784 | tf_op jit(solution)/shard_map/end_a1/ppermute | solution.py:107
  31.5 2.0 %collective-permute-start.8 = (bf16[256,896]{1,0:T(8,128)(2,1)}, bf16[256,896]{1,0:T(8,128)(2,1)}, u32[]{:S(2)}, u32[]{:S(2)}) collective-permute-start(bf16[256,896]{1,0:T(8,128)(2,1)} %collective-permute-done.4.refs_2_), channel_id=1, source_target_pairs={{2,4},{3,5},{4,2},{5,3},{0,1},{1,0},{6,7},{7,6},{10,12},{11,13},{1... | collective-permute-start | bytes 1376264 | tf_op jit(solution)/shard_map/far_a0/ppermute | solution.py:107
  33.5 12.4 %collective-permute-done.14.refs_2_.refs_3_ = bf16[512,640]{1,0:T(8,128)(2,1)} collective-permute-done((bf16[512,640]{1,0:T(8,128)(2,1)S(1)}, bf16[512,640]{1,0:T(8,128)(2,1)}, u32[]{:S(2)}, u32[]{:S(2)}) %collective-permute-start.14) | collective-permute-done | bytes 655392 | tf_op jit(solution)/shard_map/end_b/ppermute | solution.py:107
  45.9 0.1 iota_compare_fusion.2
  46.0 0.6 slice.101.refs_12_
  46.6 0.6 slice.106.refs_12_
  47.2 0.1 select_reduce_fusion
  47.3 0.1 copy.12
  47.4 0.7 reshape.114.mult_ref
  48.2 0.6 collective-permute-start.15
  48.8 3.6 %collective-permute-start.17 = (bf16[512,640]{1,0:T(8,128)(2,1)S(1)}, bf16[512,640]{1,0:T(8,128)(2,1)}, u32[]{:S(2)}, u32[]{:S(2)}) collective-permute-start(bf16[512,640]{1,0:T(8,128)(2,1)S(1)} %pad_maximum_fusion.4.refs_8_.refs_9_), channel_id=1, source_target_pairs={{0,2},{1,3},{2,0},{3,1},{4,6},{5,7},{6,4},{7,5},{8,10},{9,11},{10,... | collective-permute-start | bytes 1966088 | tf_op jit(solution)/shard_map/qr_b/ppermute | solution.py:107
  52.4 13.2 %collective-permute-done.11.refs_10_.refs_11_ = bf16[512,896]{1,0:T(8,128)(2,1)} collective-permute-done((bf16[512,896]{1,0:T(8,128)(2,1)S(1)}, bf16[512,896]{1,0:T(8,128)(2,1)}, u32[]{:S(2)}, u32[]{:S(2)}) %collective-permute-start.11) | collective-permute-done | bytes 917536 | tf_op jit(solution)/shard_map/qr_a/ppermute | solution.py:107
  65.6 9.9 %shard_map.73 = (bf16[256,896]{1,0:T(8,128)(2,1)}, bf16[256,896]{1,0:T(8,128)(2,1)}) custom-call(f32[384]{0:T(512)} %reshape.114.mult_ref, bf16[256,896]{1,0:T(8,128)(2,1)} %pad_maximum_fusion.5.refs_0_, bf16[256,896]{1,0:T(8,128)(2,1)} %copy-done.9, bf16[256,896]{1,0:T(8,128)(2,1)} %collective-permute-done.4.refs_2_, ...), custom_call_target="tpu_custom_call" | custom-call | flops 11274289152 | bytes 6422528 | tf_op jit(solution)/shard_map/pallas_call | solution.py:190
  75.5 2.0 %collective-permute-start.12 = (bf16[256,896]{1,0:T(8,128)(2,1)}, bf16[256,896]{1,0:T(8,128)(2,1)S(1)}, u32[]{:S(2)}, u32[]{:S(2)}) collective-permute-start(bf16[256,896]{1,0:T(8,128)(2,1)} %get-tuple-element.18), channel_id=1, source_target_pairs={{0,8},{1,9},{2,10},{3,11},{4,12},{5,13},{6,14},{7,15},{8,16},{9,17... | collective-permute-start | bytes 1376264 | tf_op jit(solution)/shard_map/onto_0/ppermute | solution.py:111
  77.5 2.5 %collective-permute-start.13 = (bf16[256,896]{1,0:T(8,128)(2,1)}, bf16[256,896]{1,0:T(8,128)(2,1)S(1)}, u32[]{:S(2)}, u32[]{:S(2)}) collective-permute-start(bf16[256,896]{1,0:T(8,128)(2,1)} %get-tuple-element.19), channel_id=1, source_target_pairs={{0,10},{1,11},{2,8},{3,9},{4,14},{5,15},{6,12},{7,13},{8,18},{9,19... | collective-permute-start | bytes 1376264 | tf_op jit(solution)/shard_map/onto_0/ppermute | solution.py:111
  80.0 0.8 copy-done.8
  80.9 7.9 %shard_map.74 = (bf16[256,640]{1,0:T(8,128)(2,1)}, bf16[256,640]{1,0:T(8,128)(2,1)}) custom-call(f32[384]{0:T(512)} %reshape.114.mult_ref, bf16[512,640]{1,0:T(8,128)(2,1)} %copy-done.3, bf16[512,640]{1,0:T(8,128)(2,1)} %copy-done.3, bf16[512,640]{1,0:T(8,128)(2,1)} %collective-permute-done.14.refs_2_.refs_3_, ...), custom_call_target="tpu_custom_call" | custom-call | flops 8053063680 | bytes 4587520 | tf_op jit(solution)/shard_map/pallas_call | solution.py:190
  88.7 1.3 %collective-permute-start.19 = (bf16[256,640]{1,0:T(8,128)(2,1)}, bf16[256,640]{1,0:T(8,128)(2,1)S(1)}, u32[]{:S(2)}, u32[]{:S(2)}) collective-permute-start(bf16[256,640]{1,0:T(8,128)(2,1)} %get-tuple-element.24), channel_id=1, source_target_pairs={{2,0},{3,1},{4,6},{5,7},{10,8},{11,9},{12,14},{13,15},{18,16},{19,... | collective-permute-start | bytes 983048 | tf_op jit(solution)/shard_map/back/ppermute | solution.py:107
  90.0 0.7 collective-permute-start.18
  90.7 10.2 %collective-permute-done.19 = bf16[256,640]{1,0:T(8,128)(2,1)S(1)} collective-permute-done((bf16[256,640]{1,0:T(8,128)(2,1)}, bf16[256,640]{1,0:T(8,128)(2,1)S(1)}, u32[]{:S(2)}, u32[]{:S(2)}) %collective-permute-start.19) | collective-permute-done | bytes 327712 | tf_op jit(solution)/shard_map/back/ppermute | solution.py:107
  100.9 3.4 %collective-permute-start.20 = (bf16[256,640]{1,0:T(8,128)(2,1)S(1)}, bf16[256,640]{1,0:T(8,128)(2,1)S(1)}, u32[]{:S(2)}, u32[]{:S(2)}) collective-permute-start(bf16[256,640]{1,0:T(8,128)(2,1)S(1)} %collective-permute-done.19), channel_id=1, source_target_pairs={{0,8},{1,9},{6,14},{7,15},{8,16},{9,17},{14,22},{15,23},{16,24},{1... | collective-permute-start | bytes 983048 | tf_op jit(solution)/shard_map/onto_1/ppermute | solution.py:111
  104.4 0.1 collective-permute-start.21
  104.5 6.2 %collective-permute-done.20 = bf16[256,640]{1,0:T(8,128)(2,1)S(1)} collective-permute-done((bf16[256,640]{1,0:T(8,128)(2,1)S(1)}, bf16[256,640]{1,0:T(8,128)(2,1)S(1)}, u32[]{:S(2)}, u32[]{:S(2)}) %collective-permute-start.20) | collective-permute-done | bytes 327712 | tf_op jit(solution)/shard_map/onto_1/ppermute | solution.py:111
  110.8 0.1 collective-permute-start.22
  110.9 1.3 %collective-permute-done.22 = bf16[128,640]{1,0:T(8,128)(2,1)S(1)} collective-permute-done((bf16[128,640]{1,0:T(8,128)(2,1)S(1)}, bf16[128,640]{1,0:T(8,128)(2,1)S(1)}, u32[]{:S(2)}, u32[]{:S(2)}) %collective-permute-start.22) | collective-permute-done | bytes 163872 | tf_op jit(solution)/shard_map/settle_1/ppermute | solution.py:107
  112.3 0.1 broadcast_select_fusion.4
  112.4 1.0 maximum_bitcast_fusion
  (61 shorter events, 0.8 us)
Async XLA Ops:
  1.4 1.9 %copy-start.7 = (s32[1,1,24,5]{2,1,3,0:T(1,128)S(1)}, s32[1,1,24,5]{2,1,3,0:T(1,128)}, u32[]{:S(2)}) copy-start(s32[1,1,24,5]{2,1,3,0:T(1,128)} %param.12) | copy-start | bytes 1444
  1.4 1.9 %copy-start.1 = (bf16[1,128,3072]{2,1,0:T(8,128)(2,1)S(1)}, bf16[1,128,3072]{2,1,0:T(8,128)(2,1)}, u32[]{:S(2)}) copy-start(bf16[1,128,3072]{2,1,0:T(8,128)(2,1)} %param.10) | copy-start | bytes 2359300
  1.4 1.9 %copy-start.2 = (bf16[1,128,3072]{2,1,0:T(8,128)(2,1)S(1)}, bf16[1,128,3072]{2,1,0:T(8,128)(2,1)}, u32[]{:S(2)}) copy-start(bf16[1,128,3072]{2,1,0:T(8,128)(2,1)} %param.7) | copy-start | bytes 2359300
  1.5 2.1 %copy-start.5 = (bf16[256,896]{1,0:T(8,128)(2,1)}, bf16[256,896]{1,0:T(8,128)(2,1)S(1)}, u32[]{:S(2)}) copy-start(bf16[256,896]{1,0:T(8,128)(2,1)S(1)} %pad_maximum_fusion.6) | copy-start | bytes 1376260
  1.5 2.2 %collective-permute-start.3 = (bf16[256,896]{1,0:T(8,128)(2,1)S(1)}, bf16[256,896]{1,0:T(8,128)(2,1)S(1)}, u32[]{:S(2)}, u32[]{:S(2)}) collective-permute-start(bf16[256,896]{1,0:T(8,128)(2,1)S(1)} %pad_maximum_fusion.6), channel_id=1, source_target_pairs={{0,1},{1,0},{2,3},{3,2},{4,5},{5,4},{6,7},{7,6},{8,9},{9,8},{10,11... | collective-permute-start | bytes 1376264 | tf_op jit(solution)/shard_map/swap_a/ppermute | solution.py:107
  3.6 0.7 copy-start.10
  3.7 4.6 %copy-start.9 = (bf16[256,896]{1,0:T(8,128)(2,1)}, bf16[256,896]{1,0:T(8,128)(2,1)S(1)}, u32[]{:S(2)}) copy-start(bf16[256,896]{1,0:T(8,128)(2,1)S(1)} %collective-permute-done.3.refs_1_) | copy-start | bytes 1376260
  3.7 10.3 %collective-permute-start.10 = (bf16[256,2176]{1,0:T(8,128)(2,1)S(1)}, bf16[256,2176]{1,0:T(8,128)(2,1)S(1)}, u32[]{:S(2)}, u32[]{:S(2)}) collective-permute-start(bf16[256,2176]{1,0:T(8,128)(2,1)S(1)} %pad_maximum_fusion), channel_id=1, source_target_pairs={{0,1},{1,0},{2,3},{3,2},{4,5},{5,4},{6,7},{7,6},{8,9},{9,8},{10,11... | collective-permute-start | bytes 3342344 | tf_op jit(solution)/shard_map/swap_rest/ppermute | solution.py:107
  4.4 6.1 %collective-permute-start.2 = (f32[12,8]{0,1:T(8,128)S(1)}, f32[12,8]{0,1:T(8,128)S(1)}, u32[]{:S(2)}, u32[]{:S(2)}) collective-permute-start(f32[12,8]{0,1:T(8,128)S(1)} %get-tuple-element.44), channel_id=1, source_target_pairs={{0,3},{1,2},{2,1},{3,0},{4,7},{5,6},{6,5},{7,4},{8,11},{9,10},{10,... | collective-permute-start | bytes 1160 | tf_op jit(solution)/shard_map/table_end1/ppermute | solution.py:107
  7.1 4.1 %collective-permute-start = (f32[12,8]{0,1:T(8,128)S(1)}, f32[12,8]{0,1:T(8,128)S(1)}, u32[]{:S(2)}, u32[]{:S(2)}) collective-permute-start(f32[12,8]{0,1:T(8,128)S(1)} %get-tuple-element.44), channel_id=1, source_target_pairs={{0,1},{1,0},{2,3},{3,2},{4,5},{5,4},{6,7},{7,6},{8,9},{9,8},{10,11... | collective-permute-start | bytes 1160 | tf_op jit(solution)/shard_map/table_swap/ppermute | solution.py:107
  7.5 3.6 %collective-permute-start.1 = (f32[12,8]{0,1:T(8,128)S(1)}, f32[12,8]{0,1:T(8,128)S(1)}, u32[]{:S(2)}, u32[]{:S(2)}) collective-permute-start(f32[12,8]{0,1:T(8,128)S(1)} %get-tuple-element.43), channel_id=1, source_target_pairs={{0,2},{1,3},{2,0},{3,1},{4,6},{5,7},{6,4},{7,5},{8,10},{9,11},{10,... | collective-permute-start | bytes 1160 | tf_op jit(solution)/shard_map/table_end0/ppermute | solution.py:107
  8.3 13.7 %collective-permute-start.4 = (bf16[256,896]{1,0:T(8,128)(2,1)}, bf16[256,896]{1,0:T(8,128)(2,1)}, u32[]{:S(2)}, u32[]{:S(2)}) collective-permute-start(bf16[256,896]{1,0:T(8,128)(2,1)} %pad_maximum_fusion.5.refs_0_), channel_id=1, source_target_pairs={{0,2},{1,3},{2,0},{3,1},{4,6},{5,7},{6,4},{7,5},{8,10},{9,11},{10,... | collective-permute-start | bytes 1376264 | tf_op jit(solution)/shard_map/end_a0/ppermute | solution.py:107
  10.5 37.6 %collective-permute-start.6 = (bf16[256,896]{1,0:T(8,128)(2,1)}, bf16[256,896]{1,0:T(8,128)(2,1)}, u32[]{:S(2)}, u32[]{:S(2)}) collective-permute-start(bf16[256,896]{1,0:T(8,128)(2,1)} %pad_maximum_fusion.5.refs_0_), channel_id=1, source_target_pairs={{2,4},{3,5},{4,2},{5,3},{0,1},{1,0},{6,7},{7,6},{10,12},{11,13},{1... | collective-permute-start | bytes 1376264 | tf_op jit(solution)/shard_map/near_a0/ppermute | solution.py:107
  11.1 37.6 %collective-permute-start.7 = (bf16[256,896]{1,0:T(8,128)(2,1)}, bf16[256,896]{1,0:T(8,128)(2,1)}, u32[]{:S(2)}, u32[]{:S(2)}) collective-permute-start(bf16[256,896]{1,0:T(8,128)(2,1)} %copy-done.5), channel_id=1, source_target_pairs={{2,5},{3,4},{4,3},{5,2},{0,1},{1,0},{6,7},{7,6},{10,13},{11,12},{1... | collective-permute-start | bytes 1376264 | tf_op jit(solution)/shard_map/near_a1/ppermute | solution.py:107
  11.1 20.3 %collective-permute-start.5 = (bf16[256,896]{1,0:T(8,128)(2,1)}, bf16[256,896]{1,0:T(8,128)(2,1)}, u32[]{:S(2)}, u32[]{:S(2)}) collective-permute-start(bf16[256,896]{1,0:T(8,128)(2,1)} %copy-done.5), channel_id=1, source_target_pairs={{0,3},{1,2},{2,1},{3,0},{4,7},{5,6},{6,5},{7,4},{8,11},{9,10},{10,... | collective-permute-start | bytes 1376264 | tf_op jit(solution)/shard_map/end_a1/ppermute | solution.py:107
  14.1 34.1 %copy-start.3 = (bf16[512,640]{1,0:T(8,128)(2,1)}, bf16[512,640]{1,0:T(8,128)(2,1)S(1)}, u32[]{:S(2)}) copy-start(bf16[512,640]{1,0:T(8,128)(2,1)S(1)} %pad_maximum_fusion.3.refs_0_.refs_1_) | copy-start | bytes 1966084
  22.0 23.9 %collective-permute-start.14 = (bf16[512,640]{1,0:T(8,128)(2,1)S(1)}, bf16[512,640]{1,0:T(8,128)(2,1)}, u32[]{:S(2)}, u32[]{:S(2)}) collective-permute-start(bf16[512,640]{1,0:T(8,128)(2,1)S(1)} %pad_maximum_fusion.3.refs_0_.refs_1_), channel_id=1, source_target_pairs={{0,2},{1,3},{2,0},{3,1},{4,6},{5,7},{6,4},{7,5},{8,10},{9,11},{10,... | collective-permute-start | bytes 1966088 | tf_op jit(solution)/shard_map/end_b/ppermute | solution.py:107
  24.3 7.2 %copy-start.6 = (f32[1,3072]{1,0:T(1,128)S(1)}, f32[1,3072]{1,0:T(1,128)}, u32[]{:S(2)}) copy-start(f32[1,3072]{1,0:T(1,128)} %param.11) | copy-start | bytes 36868
  24.4 41.1 %copy-start = (bf16[512,896]{1,0:T(8,128)(2,1)}, bf16[512,896]{1,0:T(8,128)(2,1)S(1)}, u32[]{:S(2)}) copy-start(bf16[512,896]{1,0:T(8,128)(2,1)S(1)} %pad_maximum_fusion.1.refs_8_.refs_9_) | copy-start | bytes 2752516
  31.4 34.1 %collective-permute-start.11 = (bf16[512,896]{1,0:T(8,128)(2,1)S(1)}, bf16[512,896]{1,0:T(8,128)(2,1)}, u32[]{:S(2)}, u32[]{:S(2)}) collective-permute-start(bf16[512,896]{1,0:T(8,128)(2,1)S(1)} %pad_maximum_fusion.1.refs_8_.refs_9_), channel_id=1, source_target_pairs={{0,2},{1,3},{2,0},{3,1},{4,6},{5,7},{6,4},{7,5},{8,10},{9,11},{10,... | collective-permute-start | bytes 2752520 | tf_op jit(solution)/shard_map/qr_a/ppermute | solution.py:107
  31.5 20.8 %collective-permute-start.8 = (bf16[256,896]{1,0:T(8,128)(2,1)}, bf16[256,896]{1,0:T(8,128)(2,1)}, u32[]{:S(2)}, u32[]{:S(2)}) collective-permute-start(bf16[256,896]{1,0:T(8,128)(2,1)} %collective-permute-done.4.refs_2_), channel_id=1, source_target_pairs={{2,4},{3,5},{4,2},{5,3},{0,1},{1,0},{6,7},{7,6},{10,12},{11,13},{1... | collective-permute-start | bytes 1376264 | tf_op jit(solution)/shard_map/far_a0/ppermute | solution.py:107
  45.9 6.5 %collective-permute-start.9 = (bf16[256,896]{1,0:T(8,128)(2,1)}, bf16[256,896]{1,0:T(8,128)(2,1)}, u32[]{:S(2)}, u32[]{:S(2)}) collective-permute-start(bf16[256,896]{1,0:T(8,128)(2,1)} %collective-permute-done.5.refs_3_), channel_id=1, source_target_pairs={{2,4},{3,5},{4,2},{5,3},{0,1},{1,0},{6,7},{7,6},{10,12},{11,13},{1... | collective-permute-start | bytes 1376264 | tf_op jit(solution)/shard_map/far_a1/ppermute | solution.py:107
  48.2 27.3 %copy-start.4 = (bf16[512,640]{1,0:T(8,128)(2,1)}, bf16[512,640]{1,0:T(8,128)(2,1)S(1)}, u32[]{:S(2)}) copy-start(bf16[512,640]{1,0:T(8,128)(2,1)S(1)} %pad_maximum_fusion.4.refs_8_.refs_9_) | copy-start | bytes 1966084
  48.2 31.8 %collective-permute-start.15 = (bf16[512,640]{1,0:T(8,128)(2,1)S(1)}, bf16[512,640]{1,0:T(8,128)(2,1)S(1)}, u32[]{:S(2)}, u32[]{:S(2)}) collective-permute-start(bf16[512,640]{1,0:T(8,128)(2,1)S(1)} %pad_maximum_fusion.3.refs_0_.refs_1_), channel_id=1, source_target_pairs={{2,4},{3,5},{4,2},{5,3},{0,1},{1,0},{6,7},{7,6},{10,12},{11,13},{1... | collective-permute-start | bytes 1966088 | tf_op jit(solution)/shard_map/near_b/ppermute | solution.py:107
  48.8 31.2 %collective-permute-start.17 = (bf16[512,640]{1,0:T(8,128)(2,1)S(1)}, bf16[512,640]{1,0:T(8,128)(2,1)}, u32[]{:S(2)}, u32[]{:S(2)}) collective-permute-start(bf16[512,640]{1,0:T(8,128)(2,1)S(1)} %pad_maximum_fusion.4.refs_8_.refs_9_), channel_id=1, source_target_pairs={{0,2},{1,3},{2,0},{3,1},{4,6},{5,7},{6,4},{7,5},{8,10},{9,11},{10,... | collective-permute-start | bytes 1966088 | tf_op jit(solution)/shard_map/qr_b/ppermute | solution.py:107
  52.4 27.6 %collective-permute-start.16 = (bf16[512,640]{1,0:T(8,128)(2,1)}, bf16[512,640]{1,0:T(8,128)(2,1)}, u32[]{:S(2)}, u32[]{:S(2)}) collective-permute-start(bf16[512,640]{1,0:T(8,128)(2,1)} %collective-permute-done.14.refs_2_.refs_3_), channel_id=1, source_target_pairs={{2,4},{3,5},{4,2},{5,3},{0,1},{1,0},{6,7},{7,6},{10,12},{11,13},{1... | collective-permute-start | bytes 1966088 | tf_op jit(solution)/shard_map/far_b/ppermute | solution.py:107
  75.5 28.8 %collective-permute-start.12 = (bf16[256,896]{1,0:T(8,128)(2,1)}, bf16[256,896]{1,0:T(8,128)(2,1)S(1)}, u32[]{:S(2)}, u32[]{:S(2)}) collective-permute-start(bf16[256,896]{1,0:T(8,128)(2,1)} %get-tuple-element.18), channel_id=1, source_target_pairs={{0,8},{1,9},{2,10},{3,11},{4,12},{5,13},{6,14},{7,15},{8,16},{9,17... | collective-permute-start | bytes 1376264 | tf_op jit(solution)/shard_map/onto_0/ppermute | solution.py:111
  77.5 26.8 %collective-permute-start.13 = (bf16[256,896]{1,0:T(8,128)(2,1)}, bf16[256,896]{1,0:T(8,128)(2,1)S(1)}, u32[]{:S(2)}, u32[]{:S(2)}) collective-permute-start(bf16[256,896]{1,0:T(8,128)(2,1)} %get-tuple-element.19), channel_id=1, source_target_pairs={{0,10},{1,11},{2,8},{3,9},{4,14},{5,15},{6,12},{7,13},{8,18},{9,19... | collective-permute-start | bytes 1376264 | tf_op jit(solution)/shard_map/onto_0/ppermute | solution.py:111
  80.0 0.9 copy-start.8
  88.7 12.2 %collective-permute-start.19 = (bf16[256,640]{1,0:T(8,128)(2,1)}, bf16[256,640]{1,0:T(8,128)(2,1)S(1)}, u32[]{:S(2)}, u32[]{:S(2)}) collective-permute-start(bf16[256,640]{1,0:T(8,128)(2,1)} %get-tuple-element.24), channel_id=1, source_target_pairs={{2,0},{3,1},{4,6},{5,7},{10,8},{11,9},{12,14},{13,15},{18,16},{19,... | collective-permute-start | bytes 983048 | tf_op jit(solution)/shard_map/back/ppermute | solution.py:107
  90.0 14.5 %collective-permute-start.18 = (bf16[256,640]{1,0:T(8,128)(2,1)}, bf16[256,640]{1,0:T(8,128)(2,1)S(1)}, u32[]{:S(2)}, u32[]{:S(2)}) collective-permute-start(bf16[256,640]{1,0:T(8,128)(2,1)} %get-tuple-element.23), channel_id=1, source_target_pairs={{2,10},{3,11},{4,12},{5,13},{10,18},{11,19},{12,20},{13,21},{18,26... | collective-permute-start | bytes 983048 | tf_op jit(solution)/shard_map/onto_1/ppermute | solution.py:111
  100.9 9.9 %collective-permute-start.20 = (bf16[256,640]{1,0:T(8,128)(2,1)S(1)}, bf16[256,640]{1,0:T(8,128)(2,1)S(1)}, u32[]{:S(2)}, u32[]{:S(2)}) collective-permute-start(bf16[256,640]{1,0:T(8,128)(2,1)S(1)} %collective-permute-done.19), channel_id=1, source_target_pairs={{0,8},{1,9},{6,14},{7,15},{8,16},{9,17},{14,22},{15,23},{16,24},{1... | collective-permute-start | bytes 983048 | tf_op jit(solution)/shard_map/onto_1/ppermute | solution.py:111
  104.4 6.5 %collective-permute-start.21 = (bf16[128,896]{1,0:T(8,128)(2,1)S(1)}, bf16[128,896]{1,0:T(8,128)(2,1)S(1)}, u32[]{:S(2)}, u32[]{:S(2)}) collective-permute-start(bf16[128,896]{1,0:T(8,128)(2,1)S(1)} %get-tuple-element.40), channel_id=1, source_target_pairs={{0,1},{1,0},{2,3},{3,2},{4,5},{5,4},{6,7},{7,6},{8,9},{9,8},{10,11... | collective-permute-start | bytes 688136 | tf_op jit(solution)/shard_map/settle_0/ppermute | solution.py:107
  110.8 1.5 %collective-permute-start.22 = (bf16[128,640]{1,0:T(8,128)(2,1)S(1)}, bf16[128,640]{1,0:T(8,128)(2,1)S(1)}, u32[]{:S(2)}, u32[]{:S(2)}) collective-permute-start(bf16[128,640]{1,0:T(8,128)(2,1)S(1)} %get-tuple-element.42), channel_id=1, source_target_pairs={{0,1},{1,0},{2,3},{3,2},{4,5},{5,4},{6,7},{7,6},{8,9},{9,8},{10,11... | collective-permute-start | bytes 491528 | tf_op jit(solution)/shard_map/settle_1/ppermute | solution.py:107
